TPU v7x, 128 devices: a whole 4x4x4 slice. The times are simulated.
128 devices in a mesh: ep: 8 (over x_lo, y), blk: 16 (over x_hi, z, core).
Axes of the slice: x: 4 (x_hi: 2, x_lo: 2; x = x_hi * 2 + x_lo), y: 4, z: 4, core: 2. Of those that a mesh axis runs over, the one named last changes fastest.
Arguments:
- tokens: bfloat16 [16384, 7168], P(('ep', 'blk')), may hold values from -6 to 6
- route: int32 [16384, 8], P(('ep', 'blk')), may hold values from 0 to 255, as said below
- gates: float32 [16384, 8], P(('ep', 'blk')), may hold values from 0.1 to 1
- cotangent: bfloat16 [16384, 7168], P(('ep', 'blk')), may hold values from -6 to 6
- w_gate: bfloat16 [8, 7168, 2048], P('ep', None, 'blk'), may hold values from -0.0625 to 0.0625
- w_up: bfloat16 [8, 7168, 2048], P('ep', None, 'blk'), may hold values from -0.0625 to 0.0625
- w_down: bfloat16 [8, 2048, 7168], P('ep', 'blk'), may hold values from -0.125 to 0.125
Outputs:
- mixed: bfloat16 [16384, 7168], P(('ep', 'blk'))
- grad_tokens: bfloat16 [16384, 7168], P(('ep', 'blk'))
- grad_gate: bfloat16 [8, 7168, 2048], P('ep', None, 'blk')
- grad_up: bfloat16 [8, 7168, 2048], P('ep', None, 'blk')
- grad_down: bfloat16 [8, 2048, 7168], P('ep', 'blk')
Inputs may be any that keep to these rules, and one draw needn't show every extreme that they name: `route`: each row names 8 different experts; numbers below 8 are the window's experts. Among the 128 rows of one device each window expert is named by 1 to 4 rows, and in every draw one window expert is named by exactly 4 rows on every device.
All inputs are finite; a program needn't handle non-finite values.
Results may differ from a plain program's by a relative error of at most 0.025.
Values may be sent and summed in bfloat16 or wider, within the bound.
No kernel may reach another device: no remote copies, remote signals or barrier semaphores. Data moves between devices by JAX's collectives and lax.ppermute only.
A program may use at most 192 MiB of HBM per device.

v0:
```python
import jax
import jax.numpy as jnp
from jax import lax
from jax.sharding import PartitionSpec as P

CAP = 4


def local(tokens, route, gates, cotangent, w_gate, w_up, w_down):
    groups = lax.axis_size("ep")
    model_width = tokens.shape[1]
    matches = route[:, :, None] == jnp.arange(groups, dtype=jnp.int32)
    member = jnp.any(matches, axis=1)
    weight = jnp.sum(jnp.where(matches, gates[:, :, None], 0.0), axis=1)
    places = jnp.cumsum(member.astype(jnp.int32), axis=0) - 1
    picked = member[:, :, None] & (places[:, :, None] == jnp.arange(CAP, dtype=jnp.int32))
    picked_b = picked.astype(jnp.bfloat16)
    picked_w = jnp.where(picked, weight[:, :, None], 0.0)
    slot_gate = jnp.sum(picked_w, axis=0)
    x_slots = jnp.einsum(
        "tec,td->ecd", picked_b, tokens, preferred_element_type=jnp.float32
    ).astype(jnp.bfloat16)
    d_rows = jnp.einsum("tec,td->ecd", picked_b, cotangent, preferred_element_type=jnp.float32)
    d_slots = (d_rows * slot_gate[:, :, None]).astype(jnp.bfloat16)
    moved_x, moved_d = (
        lax.all_to_all(x_slots, "ep", split_axis=0, concat_axis=0, tiled=True),
        lax.all_to_all(d_slots, "ep", split_axis=0, concat_axis=0, tiled=True),
    )
    rows_x, rows_d = (
        lax.all_gather(moved_x.reshape(-1, model_width), "blk", axis=0, tiled=True),
        lax.all_gather(moved_d.reshape(-1, model_width), "blk", axis=0, tiled=True),
    )
    gate_pre = jnp.dot(rows_x, w_gate[0], preferred_element_type=jnp.float32)
    up_pre = jnp.dot(rows_x, w_up[0], preferred_element_type=jnp.float32)
    logistic = jax.nn.sigmoid(gate_pre)
    hidden = (gate_pre * logistic * up_pre).astype(jnp.bfloat16)
    expert_rows = lax.psum_scatter(
        jnp.dot(hidden, w_down[0], preferred_element_type=jnp.float32).astype(jnp.bfloat16),
        "blk",
        scatter_dimension=0,
        tiled=True,
    ).astype(jnp.float32)
    expert_rows = expert_rows.astype(jnp.bfloat16).reshape(groups, CAP, model_width)
    hidden_grad = jnp.einsum("rd,fd->rf", rows_d, w_down[0], preferred_element_type=jnp.float32)
    grad_down = jnp.einsum("rf,rd->fd", hidden, rows_d, preferred_element_type=jnp.float32).astype(
        jnp.bfloat16
    )
    slope = logistic * (1.0 + gate_pre * (1.0 - logistic))
    gate_grad = (hidden_grad * up_pre * slope).astype(jnp.bfloat16)
    up_grad = (hidden_grad * gate_pre * logistic).astype(jnp.bfloat16)
    grad_gate = jnp.einsum(
        "rd,rf->df", rows_x, gate_grad, preferred_element_type=jnp.float32
    ).astype(jnp.bfloat16)
    grad_up = jnp.einsum("rd,rf->df", rows_x, up_grad, preferred_element_type=jnp.float32).astype(
        jnp.bfloat16
    )
    first = jnp.einsum("rf,df->rd", gate_grad, w_gate[0], preferred_element_type=jnp.float32)
    second = jnp.einsum("rf,df->rd", up_grad, w_up[0], preferred_element_type=jnp.float32)
    input_rows = lax.psum_scatter(
        (first + second).astype(jnp.bfloat16), "blk", scatter_dimension=0, tiled=True
    ).astype(jnp.float32)
    input_rows = input_rows.astype(jnp.bfloat16).reshape(groups, CAP, model_width)
    back_out, back_in = (
        lax.all_to_all(expert_rows, "ep", split_axis=0, concat_axis=0, tiled=True),
        lax.all_to_all(input_rows, "ep", split_axis=0, concat_axis=0, tiled=True),
    )
    mixed = jnp.einsum(
        "tec,ecd->td", picked_w, back_out.astype(jnp.float32), precision=lax.Precision.HIGHEST
    ).astype(jnp.bfloat16)
    grad_tokens = jnp.einsum(
        "tec,ecd->td", picked_b, back_in, preferred_element_type=jnp.float32
    ).astype(jnp.bfloat16)
    return (mixed, grad_tokens, grad_gate[None], grad_up[None], grad_down[None])


def solution(mesh):
    return jax.shard_map(
        local,
        mesh=mesh,
        in_specs=(
            P(("ep", "blk"), None),
            P(("ep", "blk"), None),
            P(("ep", "blk"), None),
            P(("ep", "blk"), None),
            P("ep", None, "blk"),
            P("ep", None, "blk"),
            P("ep", "blk", None),
        ),
        out_specs=(
            P(("ep", "blk"), None),
            P(("ep", "blk"), None),
            P("ep", None, "blk"),
            P("ep", None, "blk"),
            P("ep", "blk", None),
        ),
        check_vma=False,
    )
```

profile of v0, /device:TPU:0, one launch (start us, length us, event | category | flops | bytes accessed | tf_op | source)
XLA Modules:
  0.0 387.4 jit_solution(17030118052168971951)
XLA Ops:
  7.2 0.8 fusion.20
  8.1 0.1 copy.34
  8.2 0.2 reduce_window_sum.11
  8.4 1.9 convolution_convert_fusion.4
  10.3 0.4 copy.36
  10.7 14.7 %all_to_all.20 = bf16[8,4,7168]{2,1,0:T(4,128)(2,1)S(1)} all-to-all(bf16[8,4,7168]{2,1,0:T(4,128)(2,1)S(1)} %copy.36), channel_id=1, replica_groups=mesh['ep'=8,'blk'=16] {'ep'}, dimensions={0} | all-to-all | bytes 917504 | tf_op jit(solution)/shard_map/all_to_all | solution.py:26
  25.4 0.9 reshape.36
  26.4 1.9 fusion.5
  28.3 0.4 copy.38
  28.7 10.9 %all_to_all.21 = bf16[8,4,7168]{2,1,0:T(4,128)(2,1)S(1)} all-to-all(bf16[8,4,7168]{2,1,0:T(4,128)(2,1)S(1)} %copy.38), channel_id=1, replica_groups=mesh['ep'=8,'blk'=16] {'ep'}, dimensions={0} | all-to-all | bytes 917504 | tf_op jit(solution)/shard_map/all_to_all | solution.py:27
  39.5 0.9 reshape.38
  40.5 54.4 %all-gather.3.cloned.1.call-done = bf16[512,7168]{1,0:T(8,128)(2,1)} async-done(((bf16[32,7168]{1,0:T(8,128)(2,1)}), bf16[512,7168]{1,0:T(8,128)(2,1)}) %all-gather.3.cloned.1.call-update) | async-done | bytes 7340048 | tf_op jit(solution)/shard_map/all_gather | solution.py:30
  94.9 5.8 %fusion.11 = f32[512,128]{1,0:T(8,128)S(1)} fusion(bf16[512,7168]{1,0:T(8,128)(2,1)} %all-gather.3.cloned.1.call-done, bf16[1,7168,128]{2,1,0:T(8,128)(2,1)} %param.12), kind=kOutput, calls=%fused_computation.20 | convolution fusion | flops 939524096 | bytes 9437184 | tf_op jit(solution)/shard_map/dot_general | solution.py:34
  100.8 0.4 copy-done.4
  101.1 2.1 fusion.15
  103.2 61.2 %all-gather.5.cloned.1.call-done = bf16[512,7168]{1,0:T(8,128)(2,1)} async-done(((bf16[32,7168]{1,0:T(8,128)(2,1)}), bf16[512,7168]{1,0:T(8,128)(2,1)}) %all-gather.5.cloned.1.call-update) | async-done | bytes 7340048 | tf_op jit(solution)/shard_map/all_gather | solution.py:31
  164.4 5.2 %multiply_convert_fusion = (bf16[512,128]{1,0:T(8,128)(2,1)S(1)}, bf16[512,128]{1,0:T(8,128)(2,1)S(1)}, bf16[512,128]{1,0:T(8,128)(2,1)S(1)}) fusion(f32[512,128]{1,0:T(8,128)S(1)} %fusion.15, f32[512,128]{1,0:T(8,128)S(1)} %fusion.11, bf16[512,7168]{1,0:T(8,128)(2,1)} %all-gather.5.cloned.1.call-done, bf16[1,128,7168]{2,1,0:T(8,128)(2,1)S(1)} %copy-done), kind=kOutput, calls=%fused_computation.29 | convolution fusion | flops 940572672 | bytes 10092544 | tf_op jit(solution)/shard_map/rd,fd->rf/dot_general | solution.py:44
  169.6 5.0 %convolution_convert_fusion = bf16[512,7168]{1,0:T(8,128)(2,1)} fusion(bf16[512,128]{1,0:T(8,128)(2,1)S(1)} %get-tuple-element.7, bf16[1,128,7168]{2,1,0:T(8,128)(2,1)S(1)} %copy-done), kind=kOutput, calls=%fused_computation.1 | convolution fusion | flops 943194112 | bytes 9306112 | tf_op jit(solution)/shard_map/dot_general | solution.py:38
  174.6 0.2 reduce-scatter.5.cloned.1.call-start
  174.9 9.6 %fusion.13 = f32[512,7168]{1,0:T(8,128)} fusion(bf16[512,128]{1,0:T(8,128)(2,1)S(1)} %get-tuple-element.6, bf16[1,7168,128]{2,1,0:T(8,128)(2,1)} %param.11), kind=kOutput, calls=%fused_computation.22 | convolution fusion | flops 939524096 | bytes 16646144 | tf_op jit(solution)/shard_map/rf,df->rd/dot_general | solution.py:57
  184.5 11.6 %add_convert_fusion = bf16[512,7168]{1,0:T(8,128)(2,1)} fusion(f32[512,7168]{1,0:T(8,128)} %fusion.13, bf16[512,128]{1,0:T(8,128)(2,1)S(1)} %get-tuple-element.5, bf16[1,7168,128]{2,1,0:T(8,128)(2,1)S(1)} %copy-done.3), kind=kOutput, calls=%fused_computation | convolution fusion | flops 946864128 | bytes 23986176 | tf_op jit(solution)/shard_map/rf,df->rd/dot_general | solution.py:58
  196.2 6.6 %fusion.3 = bf16[1,7168,128]{2,1,0:T(8,128)(2,1)} fusion(bf16[512,7168]{1,0:T(8,128)(2,1)} %all-gather.3.cloned.1.call-done, bf16[512,128]{1,0:T(8,128)(2,1)S(1)} %get-tuple-element.5), kind=kOutput, calls=%fused_computation.10 | convolution fusion | flops 940441600 | bytes 9306112 | tf_op jit(solution)/shard_map/rd,rf->df/dot_general | solution.py:54
  202.7 64.2 %reduce-scatter.3.cloned.1.call-done = bf16[32,7168]{1,0:T(8,128)(2,1)} async-done(((bf16[512,7168]{1,0:T(8,128)(2,1)}), bf16[32,7168]{1,0:T(8,128)(2,1)}) %reduce-scatter.3.cloned.1.call-update) | async-done | bytes 458768 | tf_op jit(solution)/shard_map/reduce_scatter | solution.py:37
  266.9 2.0 reshape.37
  268.8 4.3 %all-to-all-start.1 = ((bf16[8,4,7168]{2,1,0:T(4,128)(2,1)}), bf16[8,4,7168]{2,1,0:T(4,128)(2,1)S(1)}, u32[]{:S(2)}, u32[]{:S(2)}) async-start(bf16[8,4,7168]{2,1,0:T(4,128)(2,1)} %reshape.37), calls=%async_computation.2 | async-start | bytes 917504 | tf_op jit(solution)/shard_map/all_to_all | solution.py:64
  273.1 6.4 %fusion.2 = bf16[1,7168,128]{2,1,0:T(8,128)(2,1)} fusion(bf16[512,7168]{1,0:T(8,128)(2,1)} %all-gather.3.cloned.1.call-done, bf16[512,128]{1,0:T(8,128)(2,1)S(1)} %get-tuple-element.6), kind=kOutput, calls=%fused_computation.9 | convolution fusion | flops 940441600 | bytes 9306112 | tf_op jit(solution)/shard_map/rd,rf->df/dot_general | solution.py:51
  279.6 84.6 %reduce-scatter.5.cloned.1.call-done = bf16[32,7168]{1,0:T(8,128)(2,1)} async-done(((bf16[512,7168]{1,0:T(8,128)(2,1)}), bf16[32,7168]{1,0:T(8,128)(2,1)}) %reduce-scatter.5.cloned.1.call-update) | async-done | bytes 458768 | tf_op jit(solution)/shard_map/reduce_scatter | solution.py:59
  364.2 2.0 reshape.39
  366.1 4.3 %all-to-all-start.3 = ((bf16[8,4,7168]{2,1,0:T(4,128)(2,1)}), bf16[8,4,7168]{2,1,0:T(4,128)(2,1)S(1)}, u32[]{:S(2)}, u32[]{:S(2)}) async-start(bf16[8,4,7168]{2,1,0:T(4,128)(2,1)} %reshape.39), calls=%async_computation.5 | async-start | bytes 917504 | tf_op jit(solution)/shard_map/all_to_all | solution.py:65
  370.5 5.6 %fusion.4 = bf16[1,128,7168]{2,1,0:T(8,128)(2,1)} fusion(bf16[512,128]{1,0:T(8,128)(2,1)S(1)} %get-tuple-element.7, bf16[512,7168]{1,0:T(8,128)(2,1)} %all-gather.5.cloned.1.call-done), kind=kOutput, calls=%fused_computation.11 | convolution fusion | flops 940441600 | bytes 9306112 | tf_op jit(solution)/shard_map/rf,rd->fd/dot_general | solution.py:45
  376.1 2.9 fusion
  378.9 1.9 fusion.1
  (27 shorter events, 0.4 us)
Async XLA Ops:
  7.2 157.3 %copy-start = (bf16[1,128,7168]{2,1,0:T(8,128)(2,1)S(1)}, bf16[1,128,7168]{2,1,0:T(8,128)(2,1)}, u32[]{:S(2)}) copy-start(bf16[1,128,7168]{2,1,0:T(8,128)(2,1)} %param.13) | copy-start | bytes 5505028
  7.2 87.8 %all-gather.3.cloned.1.call-start = ((), (), s32[]{:S(2)}) async-start(), calls=%async_computation.6 | async-start | bytes 7798784 | tf_op jit(solution)/shard_map/all_gather | solution.py:30
  10.3 16.0 %copy-start.5 = (s32[128,8]{0,1:T(8,128)S(1)}, s32[128,8]{0,1:T(8,128)}, u32[]{:S(2)}) copy-start(s32[128,8]{0,1:T(8,128)} %param.8) | copy-start | bytes 12292
  10.3 16.0 %copy-start.6 = (f32[128,8]{0,1:T(8,128)S(1)}, f32[128,8]{0,1:T(8,128)}, u32[]{:S(2)}) copy-start(f32[128,8]{0,1:T(8,128)} %param.9) | copy-start | bytes 12292
  26.3 138.2 %all-gather.5.cloned.1.call-start = ((), (), s32[]{:S(2)}) async-start(), calls=%async_computation.8 | async-start | bytes 7798784 | tf_op jit(solution)/shard_map/all_gather | solution.py:31
  40.4 226.4 %reduce-scatter.3.cloned.1.call-start = ((), (), s32[]{:S(2)}) async-start(), calls=%async_computation.7 | async-start | bytes 7798784 | tf_op jit(solution)/shard_map/reduce_scatter | solution.py:37
  94.9 5.8 %copy-start.2 = (bf16[512,7168]{1,0:T(8,128)(2,1)S(1)}, bf16[512,7168]{1,0:T(8,128)(2,1)}, u32[]{:S(2)}) copy-start(bf16[512,7168]{1,0:T(8,128)(2,1)} %all-gather.3.cloned.1.call-done) | copy-start | bytes 22020100
  94.9 6.2 %copy-start.4 = (bf16[1,7168,128]{2,1,0:T(8,128)(2,1)S(1)}, bf16[1,7168,128]{2,1,0:T(8,128)(2,1)}, u32[]{:S(2)}) copy-start(bf16[1,7168,128]{2,1,0:T(8,128)(2,1)} %param.11) | copy-start | bytes 5505028
  174.6 189.5 %reduce-scatter.5.cloned.1.call-start = ((), (), s32[]{:S(2)}) async-start(), calls=%async_computation.9 | async-start | bytes 7798784 | tf_op jit(solution)/shard_map/reduce_scatter | solution.py:59
  174.9 9.6 %copy-start.3 = (bf16[1,7168,128]{2,1,0:T(8,128)(2,1)S(1)}, bf16[1,7168,128]{2,1,0:T(8,128)(2,1)}, u32[]{:S(2)}) copy-start(bf16[1,7168,128]{2,1,0:T(8,128)(2,1)} %param.12) | copy-start | bytes 5505028
  268.8 97.3 %all-to-all-start.1 = ((bf16[8,4,7168]{2,1,0:T(4,128)(2,1)}), bf16[8,4,7168]{2,1,0:T(4,128)(2,1)S(1)}, u32[]{:S(2)}, u32[]{:S(2)}) async-start(bf16[8,4,7168]{2,1,0:T(4,128)(2,1)} %reshape.37), calls=%async_computation.2 | async-start | bytes 917504 | tf_op jit(solution)/shard_map/all_to_all | solution.py:64
  366.1 12.8 %all-to-all-start.3 = ((bf16[8,4,7168]{2,1,0:T(4,128)(2,1)}), bf16[8,4,7168]{2,1,0:T(4,128)(2,1)S(1)}, u32[]{:S(2)}, u32[]{:S(2)}) async-start(bf16[8,4,7168]{2,1,0:T(4,128)(2,1)} %reshape.39), calls=%async_computation.5 | async-start | bytes 917504 | tf_op jit(solution)/shard_map/all_to_all | solution.py:65
  370.5 10.4 %copy-start.1 = (bf16[1,128,7168]{2,1,0:T(8,128)(2,1)S(1)}, bf16[1,128,7168]{2,1,0:T(8,128)(2,1)}, u32[]{:S(2)}) copy-start(bf16[1,128,7168]{2,1,0:T(8,128)(2,1)} %param.13) | copy-start | bytes 5505028
Sparse Core Ops, SparseCore 0:
  26.4 68.5 all-gather.2
  98.0 66.3 all-gather.4
  174.8 92.0 reduce-scatter.2
  271.0 93.1 reduce-scatter.4
where the time goes:
time: 389 us; the launch traced here: 387 us
  waiting for transfers between devices  264 us (68%)
  matrix products  66.4 us (17%)
  blocking collectives  25.6 us (7%)
  between operations  13.9 us (4%)
  starting transfers between devices  8.96 us (2%)
  local copies, waits for them, and re-layouts  6.95 us (2%)
    reduce_scatter x1, waiting for transfers between devices, local(): lax.psum_scatter((first + second).astype(jnp.bfloat16), 'blk', scatter_di...  84.6 us
    reduce_scatter x1, waiting for transfers between devices, local(): lax.psum_scatter(jnp.dot(hidden, w_down[0], preferred_element_type=jnp.fl...  64.2 us
    all_gather x1, waiting for transfers between devices, local(): lax.all_gather(moved_d.reshape(-1, model_width), 'blk', axis=0, tiled=True)  61.2 us
    all_gather x1, waiting for transfers between devices, local(): lax.all_gather(moved_x.reshape(-1, model_width), 'blk', axis=0, tiled=True)  54.4 us
    all_to_all x1, blocking collectives, local(): lax.all_to_all(x_slots, 'ep', split_axis=0, concat_axis=0, tiled=True)  14.7 us
    dot_general x1, matrix products, local(): jnp.einsum('rf,df->rd', up_grad, w_up[0], preferred_element_type=jnp.floa...  11.6 us
    all_to_all x1, blocking collectives, local(): lax.all_to_all(d_slots, 'ep', split_axis=0, concat_axis=0, tiled=True)  10.9 us
    dot_general x1, matrix products, local(): jnp.einsum('rf,df->rd', gate_grad, w_gate[0], preferred_element_type=jnp....  9.62 us
  transfers between devices with their start and end apart: 6, of which 4 were waited for; matrix products, arithmetic and copies ran while one was open for 15% of the time, Pallas kernels for 0%

commit v1 on v0

v1 whole, which is shorter than its diff:
```python
import jax
import jax.numpy as jnp
from jax import lax
from jax.sharding import Mesh, PartitionSpec as P

CAP = 4
PAIR = ("xl", "y")
REST = ("xh", "z", "core")
PLANE = ("xl", "y", "xh")
SWAP = [(0, 1), (1, 0)]
F32 = jnp.float32
BF16 = jnp.bfloat16
def z_by(step):
    return [(i, (i + step) % 4) for i in range(4)]


def after(value, *first):
    return lax.optimization_barrier((value,) + first)[0]


def add(*terms):
    return sum(t.astype(F32) for t in terms).astype(BF16)


def near_z(rows):
    return lax.ppermute(rows, "z", z_by(1)), lax.ppermute(rows, "z", z_by(3))


def far_z(below, above):
    cut = below.shape[0] // 2
    return lax.ppermute(below[:cut], "z", z_by(1)), lax.ppermute(above[cut:], "z", z_by(3))


def scatter_z(parts, *first):
    cut = parts.shape[0] // 8
    part = [parts[i * cut : (i + 1) * cut] for i in range(8)]
    up_1 = lax.ppermute(after(parts[3 * cut : 5 * cut], *first), "z", z_by(1))
    down_1 = lax.ppermute(after(parts[5 * cut : 7 * cut], *first), "z", z_by(3))
    up_2 = lax.ppermute(add(part[2], up_1[cut:]), "z", z_by(1))
    down_2 = lax.ppermute(add(part[7], down_1[:cut]), "z", z_by(3))
    top = add(part[0], down_1[cut:], up_2)
    low = add(part[1], up_1[:cut], down_2)
    return jnp.concatenate([top, low], axis=0), (up_1, down_1)


def to_plane(slots):
    width = slots.shape[-1]
    twice = jnp.broadcast_to(slots.reshape(8, 1, CAP, width), (8, 2, CAP, width))
    moved = lax.all_to_all(
        twice.reshape(16, CAP, width), PLANE, split_axis=0, concat_axis=0, tiled=True
    )
    return moved.reshape(16 * CAP, width)


def to_slots(rows):
    width = rows.shape[1]
    sent = rows.reshape(16, CAP, width)
    back = lax.all_to_all(sent, PLANE, split_axis=0, concat_axis=0, tiled=True)
    return back.reshape(16 * CAP, width)


def local(tokens, route, gates, cotangent, w_gate, w_up, w_down):
    model_width = tokens.shape[1]
    half = w_down.shape[1]
    matches = route[:, :, None] == jnp.arange(8, dtype=jnp.int32)
    member = jnp.any(matches, axis=1)
    weight = jnp.sum(jnp.where(matches, gates[:, :, None], 0.0), axis=1)
    places = jnp.cumsum(member.astype(jnp.int32), axis=0) - 1
    picked = member[:, :, None] & (places[:, :, None] == jnp.arange(CAP, dtype=jnp.int32))
    picked_b = picked.astype(BF16).reshape(-1, 8 * CAP)
    picked_w = jnp.where(picked, weight[:, :, None], 0.0)
    twice_b = jnp.repeat(picked.astype(BF16), 2, axis=1).reshape(-1, 16 * CAP)
    twice_w = jnp.repeat(picked_w, 2, axis=1).reshape(-1, 16 * CAP)
    picked_w = picked_w.reshape(-1, 8 * CAP)
    slot_gate = jnp.sum(picked_w, axis=0)
    x_slots = jnp.einsum("ts,td->sd", picked_b, tokens, preferred_element_type=F32).astype(BF16)
    d_rows = jnp.einsum("ts,td->sd", picked_b, cotangent, preferred_element_type=F32)
    d_slots = (d_rows * slot_gate[:, None]).astype(BF16)

    gate_other = lax.ppermute(w_gate[0], "core", SWAP)
    up_other = lax.ppermute(w_up[0], "core", SWAP)
    down_other = lax.ppermute(w_down[0], "core", SWAP)

    plane_x = to_plane(x_slots)
    x_below, x_above = near_z(plane_x)
    plane_d = to_plane(after(d_slots, plane_x))
    parts = (w_gate[0], gate_other, w_up[0], up_other, w_down[0], down_other)
    parts = lax.optimization_barrier((plane_x,) + parts)[1:]
    w_in = jnp.concatenate(parts[:4], axis=1)
    w_out = jnp.concatenate(parts[4:], axis=0)
    w_in, w_out = lax.optimization_barrier((w_in, w_out))
    x_far = far_z(x_below, x_above)
    d_below, d_above = near_z(after(plane_d, x_below, x_above))
    rows_x = jnp.concatenate([plane_x, x_above, x_far[0], x_far[1], x_below], axis=0)

    pre = jnp.dot(rows_x, w_in, preferred_element_type=F32)
    gate_pre, up_pre = pre[:, : 2 * half], pre[:, 2 * half :]
    logistic = jax.nn.sigmoid(gate_pre)
    hidden = (gate_pre * logistic * up_pre).astype(BF16)
    hidden, gate_pre, up_pre = lax.optimization_barrier((hidden, gate_pre, up_pre))
    d_far = far_z(after(d_below, hidden), after(d_above, hidden))
    y_part = jnp.dot(hidden, w_out, preferred_element_type=F32).astype(BF16)
    y_rows, y_first = scatter_z(y_part, d_below, d_above)
    rows_d = jnp.concatenate([plane_d, d_above, d_far[0], d_far[1], d_below], axis=0)

    hidden_grad = jnp.einsum("rd,fd->rf", rows_d, w_out, preferred_element_type=F32)
    logistic = jax.nn.sigmoid(gate_pre)
    slope = logistic * (1.0 + gate_pre * (1.0 - logistic))
    gate_grad = (hidden_grad * up_pre * slope).astype(BF16)
    up_grad = (hidden_grad * gate_pre * logistic).astype(BF16)
    both = jnp.concatenate([gate_grad, up_grad], axis=1)
    q_part = jnp.einsum("rf,df->rd", both, w_in, preferred_element_type=F32).astype(BF16)
    q_rows, q_first = scatter_z(q_part, *y_first)

    both_own = jnp.concatenate([gate_grad[:, :half], up_grad[:, :half]], axis=1)
    both_other = jnp.concatenate([gate_grad[:, half:], up_grad[:, half:]], axis=1)
    in_other = jnp.einsum("rd,rf->df", rows_x, both_other, preferred_element_type=F32)
    out_other = jnp.einsum("rf,rd->fd", hidden[:, half:], rows_d, preferred_element_type=F32)
    in_got = lax.ppermute(in_other.astype(BF16), "core", SWAP)
    out_got = lax.ppermute(out_other.astype(BF16), "core", SWAP)
    in_own = jnp.einsum("rd,rf->df", rows_x, both_own, preferred_element_type=F32)
    out_own = jnp.einsum("rf,rd->fd", hidden[:, :half], rows_d, preferred_element_type=F32)
    grad_in = (in_own + in_got.astype(F32)).astype(BF16)
    grad_down = (out_own + out_got.astype(F32)).astype(BF16)

    back_out = to_slots(y_rows)
    back_in = to_slots(q_rows)
    mixed = jnp.dot(
        twice_w, back_out.astype(F32), precision=lax.Precision.HIGHEST
    ).astype(BF16)
    grad_tokens = jnp.dot(twice_b, back_in, preferred_element_type=F32).astype(BF16)
    return (mixed, grad_tokens, grad_in[None, :, :half], grad_in[None, :, half:], grad_down[None])


def solution(mesh):
    fine = Mesh(mesh.devices.reshape(2, 4, 2, 4, 2), PAIR + REST)
    rows = P(PAIR + REST, None)
    wide = P(PAIR, None, REST)
    tall = P(PAIR, REST, None)
    return jax.shard_map(
        local,
        mesh=fine,
        in_specs=(rows, rows, rows, rows, wide, wide, tall),
        out_specs=(rows, rows, wide, wide, tall),
        check_vma=False,
    )
```

time: 389 us -> 216 us (0.56)
  waiting for transfers between devices: 264 us -> 118 us
  matrix products: 66.4 us -> 27.9 us
  starting transfers between devices: 8.96 us -> 43.8 us
  blocking collectives: 25.6 us -> 0 us
  between operations: 13.9 us -> 1.24 us
  local copies, waits for them, and re-layouts: 6.95 us -> 15.8 us
  other arithmetic: 1.11 us -> 8.52 us
    reduce_scatter x2 -> x0, waiting for transfers between devices: 149 us -> none  [the longest x1 84.6 us: local(): lax.psum_scatter((first + second).astype(jnp.bfloat16), 'blk', scatter_di...]
    all_gather x2 -> x0, waiting for transfers between devices: 116 us -> none  [the longest x1 61.2 us: local(): lax.all_gather(moved_d.reshape(-1, model_width), 'blk', axis=0, tiled=True)]
    ppermute x0 -> x21, waiting for transfers between devices: none -> 84.5 us  [the longest x2 26.1 us: far_z(): lax.ppermute(below[:cut], 'z', z_by(1))]
    dot_general x13 -> x12, matrix products: 66.4 us -> 27.9 us  [the longest x1 4.52 us: local(): jnp.einsum('rf,rd->fd', hidden[:, :half], rows_d, preferred_element_type=...]
    all_to_all x2 -> x4, waiting for transfers between devices: 0.01 us -> 33.6 us  [the longest x2 21.1 us: to_plane(): lax.all_to_all(twice.reshape(16, CAP, width), PLANE, split_axis=0, concat...]
    all_to_all x2 -> x0, blocking collectives: 25.6 us -> none  [the longest x1 14.7 us: local(): lax.all_to_all(x_slots, 'ep', split_axis=0, concat_axis=0, tiled=True)]
    ppermute x0 -> x21, starting transfers between devices: none -> 20.8 us  [the longest x4 7.27 us: near_z(): return (lax.ppermute(rows, 'z', z_by(1)), lax.ppermute(rows, 'z', z_by(3)))]
    all_to_all x2 -> x4, starting transfers between devices: 8.61 us -> 22.9 us  [the longest x2 11.6 us: to_plane(): lax.all_to_all(twice.reshape(16, CAP, width), PLANE, split_axis=0, concat...]
  transfers between devices with their start and end apart: 6 -> 25, of which waited for: 4 -> 12; matrix products, arithmetic and copies ran while one was open for 15% -> 19% of each run, Pallas kernels for 0% -> 0%
where the time goes in v1:
time: 216 us; the launch traced here: 215 us
  waiting for transfers between devices  118 us (55%)
  starting transfers between devices  43.8 us (20%)
  matrix products  27.9 us (13%)
  local copies, waits for them, and re-layouts  15.8 us (7%)
  other arithmetic  8.52 us (4%)
    ppermute x2, waiting for transfers between devices, far_z(): lax.ppermute(below[:cut], 'z', z_by(1))  26.1 us
    ppermute x2, waiting for transfers between devices, scatter_z(): up_1 = lax.ppermute(after(parts[3 * cut:5 * cut], *first), 'z', z_by(1))  23.1 us
    ppermute x2, waiting for transfers between devices, scatter_z(): up_2 = lax.ppermute(add(part[2], up_1[cut:]), 'z', z_by(1))  21.2 us
    all_to_all x2, waiting for transfers between devices, to_plane(): lax.all_to_all(twice.reshape(16, CAP, width), PLANE, split_axis=0, concat...  21.1 us
    ppermute x4, waiting for transfers between devices, near_z(): return (lax.ppermute(rows, 'z', z_by(1)), lax.ppermute(rows, 'z', z_by(3)))  14.2 us
    all_to_all x2, waiting for transfers between devices, to_slots(): back = lax.all_to_all(sent, PLANE, split_axis=0, concat_axis=0, tiled=True)  12.5 us
    all_to_all x2, starting transfers between devices, to_plane(): lax.all_to_all(twice.reshape(16, CAP, width), PLANE, split_axis=0, concat...  11.6 us
    all_to_all x2, starting transfers between devices, to_slots(): back = lax.all_to_all(sent, PLANE, split_axis=0, concat_axis=0, tiled=True)  11.3 us
  transfers between devices with their start and end apart: 25, of which 12 were waited for; matrix products, arithmetic and copies ran while one was open for 19% of the time, Pallas kernels for 0%

profile of v1, /device:TPU:0, one launch (start us, length us, event | category | flops | bytes accessed | tf_op | source)
XLA Modules:
  0.0 215.3 jit_solution(5075972529124532568)
XLA Ops:
  3.9 7.1 %all-to-all-start = ((bf16[16,4,7168]{2,1,0:T(4,128)(2,1)}), bf16[16,4,7168]{2,1,0:T(4,128)(2,1)S(1)}, u32[]{:S(2)}, u32[]{:S(2)}) async-start(bf16[16,4,7168]{2,1,0:T(4,128)(2,1)} %bitcast.3), calls=%async_computation | async-start | bytes 1835008 | tf_op jit(solution)/shard_map/all_to_all | solution.py:49
  13.1 12.8 %all-to-all-done = bf16[16,4,7168]{2,1,0:T(4,128)(2,1)S(1)} async-done(((bf16[16,4,7168]{2,1,0:T(4,128)(2,1)}), bf16[16,4,7168]{2,1,0:T(4,128)(2,1)S(1)}, u32[]{:S(2)}, u32[]{:S(2)}) %all-to-all-start) | async-done | bytes 917536 | tf_op jit(solution)/shard_map/all_to_all | solution.py:49
  27.5 4.5 %all-to-all-start.1 = ((bf16[16,4,7168]{2,1,0:T(4,128)(2,1)}), bf16[16,4,7168]{2,1,0:T(4,128)(2,1)S(1)}, u32[]{:S(2)}, u32[]{:S(2)}) async-start(bf16[16,4,7168]{2,1,0:T(4,128)(2,1)} %bitcast.7), calls=%async_computation.1 | async-start | bytes 1835008 | tf_op jit(solution)/shard_map/all_to_all | solution.py:49
  32.7 4.0 %collective-permute-start = (bf16[64,7168]{1,0:T(8,128)(2,1)S(1)}, bf16[64,7168]{1,0:T(8,128)(2,1)}, u32[]{:S(2)}, u32[]{:S(2)}) collective-permute-start(bf16[64,7168]{1,0:T(8,128)(2,1)S(1)} %reshape.69), channel_id=1, source_target_pairs={{0,6},{2,0},{4,2},{6,4},{1,7},{3,1},{5,3},{7,5},{8,14},{10,8},{12,... | collective-permute-start | bytes 2752520 | tf_op jit(solution)/shard_map/ppermute | solution.py:26
  37.7 8.2 %all-to-all-done.1 = bf16[16,4,7168]{2,1,0:T(4,128)(2,1)S(1)} async-done(((bf16[16,4,7168]{2,1,0:T(4,128)(2,1)}), bf16[16,4,7168]{2,1,0:T(4,128)(2,1)S(1)}, u32[]{:S(2)}, u32[]{:S(2)}) %all-to-all-start.1) | async-done | bytes 917536 | tf_op jit(solution)/shard_map/all_to_all | solution.py:49
  46.3 10.6 %collective-permute-done = bf16[64,7168]{1,0:T(8,128)(2,1)} collective-permute-done((bf16[64,7168]{1,0:T(8,128)(2,1)S(1)}, bf16[64,7168]{1,0:T(8,128)(2,1)}, u32[]{:S(2)}, u32[]{:S(2)}) %collective-permute-start) | collective-permute-done | bytes 917536 | tf_op jit(solution)/shard_map/ppermute | solution.py:26
  56.9 3.5 %collective-permute-done.1 = bf16[64,7168]{1,0:T(8,128)(2,1)} collective-permute-done((bf16[64,7168]{1,0:T(8,128)(2,1)S(1)}, bf16[64,7168]{1,0:T(8,128)(2,1)}, u32[]{:S(2)}, u32[]{:S(2)}) %collective-permute-start.1) | collective-permute-done | bytes 917536 | tf_op jit(solution)/shard_map/ppermute | solution.py:26
  60.4 3.2 %collective-permute-start.8 = (bf16[64,7168]{1,0:T(8,128)(2,1)S(1)}, bf16[64,7168]{1,0:T(8,128)(2,1)S(1)}, u32[]{:S(2)}, u32[]{:S(2)}) collective-permute-start(bf16[64,7168]{1,0:T(8,128)(2,1)S(1)} %reshape.71), channel_id=1, source_target_pairs={{0,6},{2,0},{4,2},{6,4},{1,7},{3,1},{5,3},{7,5},{8,14},{10,8},{12,... | collective-permute-start | bytes 2752520 | tf_op jit(solution)/shard_map/ppermute | solution.py:26
  65.8 2.2 %constant_dynamic-update-slice_fusion.3 = bf16[256,7168]{1,0:T(8,128)(2,1)} fusion(bf16[256,7168]{1,0:T(8,128)(2,1)} %constant_dynamic-update-slice_fusion.4, bf16[64,7168]{1,0:T(8,128)(2,1)} %collective-permute-done), kind=kLoop, calls=%fused_computation.50 | loop fusion | bytes 1835008
  67.9 3.2 %collective-permute-start.3 = (bf16[32,7168]{1,0:T(8,128)(2,1)S(1)}, bf16[32,7168]{1,0:T(8,128)(2,1)S(1)}, u32[]{:S(2)}, u32[]{:S(2)}) collective-permute-start(bf16[32,7168]{1,0:T(8,128)(2,1)S(1)} %slice.137), channel_id=1, source_target_pairs={{0,6},{2,0},{4,2},{6,4},{1,7},{3,1},{5,3},{7,5},{8,14},{10,8},{12,... | collective-permute-start | bytes 1376264 | tf_op jit(solution)/shard_map/ppermute | solution.py:31
  71.2 3.1 %pad_maximum_fusion = bf16[7168,512]{1,0:T(8,128)(2,1)S(1)} fusion(bf16[7168,128]{1,0:T(8,128)(2,1)} %collective-permute-done.5, bf16[7168,128]{1,0:T(8,128)(2,1)S(1)} %bitcast.35, bf16[7168,128]{1,0:T(8,128)(2,1)} %collective-permute-done.4, bf16[7168,128]{1,0:T(8,128)(2,1)S(1)} %bitcast.37), kind=kLoop, calls=%fused_computation.14 | loop fusion | flops 29360128 | bytes 14680064 | tf_op jit(solution)/shard_map/concatenate | solution.py:89
  76.2 16.8 %collective-permute-done.2 = bf16[32,7168]{1,0:T(8,128)(2,1)S(1)} collective-permute-done((bf16[32,7168]{1,0:T(8,128)(2,1)S(1)}, bf16[32,7168]{1,0:T(8,128)(2,1)S(1)}, u32[]{:S(2)}, u32[]{:S(2)}) %collective-permute-start.2) | collective-permute-done | bytes 458784 | tf_op jit(solution)/shard_map/ppermute | solution.py:31
  94.4 2.0 fusion.28
  98.0 3.3 %collective-permute-start.14 = (bf16[32,7168]{1,0:T(8,128)(2,1)S(1)}, bf16[32,7168]{1,0:T(8,128)(2,1)S(1)}, u32[]{:S(2)}, u32[]{:S(2)}) collective-permute-start(bf16[32,7168]{1,0:T(8,128)(2,1)S(1)} %slice.117), channel_id=1, source_target_pairs={{0,6},{2,0},{4,2},{6,4},{1,7},{3,1},{5,3},{7,5},{8,14},{10,8},{12,... | collective-permute-start | bytes 1376264 | tf_op jit(solution)/shard_map/ppermute | solution.py:31
  103.4 9.2 %collective-permute-done.13 = bf16[32,7168]{1,0:T(8,128)(2,1)S(1)} collective-permute-done((bf16[32,7168]{1,0:T(8,128)(2,1)S(1)}, bf16[32,7168]{1,0:T(8,128)(2,1)S(1)}, u32[]{:S(2)}, u32[]{:S(2)}) %collective-permute-start.13) | collective-permute-done | bytes 458784 | tf_op jit(solution)/shard_map/ppermute | solution.py:31
  112.8 2.4 %convolution_convert_fusion.3 = bf16[128,7168]{1,0:T(8,128)(2,1)} fusion(bf16[256,7168]{1,0:T(8,128)(2,1)S(1)} %constant_dynamic-update-slice_fusion.5, bf16[256,256]{1,0:T(8,128)(2,1)S(1)} %get-tuple-element.31), kind=kOutput, calls=%fused_computation.7 | convolution fusion | flops 470679552 | bytes 5570560 | tf_op jit(solution)/shard_map/rf,rd->fd/dot_general | solution.py:118
  116.4 3.1 %convolution_convert_fusion = bf16[7168,256]{1,0:T(8,128)(2,1)} fusion(bf16[256,7168]{1,0:T(8,128)(2,1)S(1)} %constant_dynamic-update-slice_fusion, bf16[256,128]{1,0:T(8,128)(2,1)S(1)} %get-tuple-element.64, bf16[256,128]{1,0:T(8,128)(2,1)S(1)} %get-tuple-element.59), kind=kOutput, calls=%fused_computation.2 | convolution fusion | flops 941621248 | bytes 7471104 | tf_op jit(solution)/shard_map/rd,rf->df/dot_general | solution.py:117
  120.0 2.1 convolution_convert_fusion.1
  122.1 7.5 %collective-permute-done.10 = bf16[64,7168]{1,0:T(8,128)(2,1)S(1)} collective-permute-done((bf16[64,7168]{1,0:T(8,128)(2,1)S(1)}, bf16[64,7168]{1,0:T(8,128)(2,1)S(1)}, u32[]{:S(2)}, u32[]{:S(2)}) %collective-permute-start.10) | collective-permute-done | bytes 917536 | tf_op jit(solution)/shard_map/ppermute | solution.py:37
  130.0 3.3 %collective-permute-start.15 = (bf16[64,7168]{1,0:T(8,128)(2,1)S(1)}, bf16[64,7168]{1,0:T(8,128)(2,1)S(1)}, u32[]{:S(2)}, u32[]{:S(2)}) collective-permute-start(bf16[64,7168]{1,0:T(8,128)(2,1)S(1)} %get-tuple-element.41), channel_id=1, source_target_pairs={{0,6},{2,0},{4,2},{6,4},{1,7},{3,1},{5,3},{7,5},{8,14},{10,8},{12,... | collective-permute-start | bytes 2752520 | tf_op jit(solution)/shard_map/ppermute | solution.py:38
  133.2 11.2 %collective-permute-done.11 = bf16[32,7168]{1,0:T(8,128)(2,1)S(1)} collective-permute-done((bf16[32,7168]{1,0:T(8,128)(2,1)S(1)}, bf16[32,7168]{1,0:T(8,128)(2,1)S(1)}, u32[]{:S(2)}, u32[]{:S(2)}) %collective-permute-start.11) | collective-permute-done | bytes 458784 | tf_op jit(solution)/shard_map/ppermute | solution.py:39
  145.0 15.6 %collective-permute-done.16 = bf16[64,7168]{1,0:T(8,128)(2,1)S(1)} collective-permute-done((bf16[64,7168]{1,0:T(8,128)(2,1)S(1)}, bf16[64,7168]{1,0:T(8,128)(2,1)S(1)}, u32[]{:S(2)}, u32[]{:S(2)}) %collective-permute-start.16) | collective-permute-done | bytes 917536 | tf_op jit(solution)/shard_map/ppermute | solution.py:37
  161.0 10.0 %collective-permute-done.17 = bf16[32,7168]{1,0:T(8,128)(2,1)S(1)} collective-permute-done((bf16[32,7168]{1,0:T(8,128)(2,1)S(1)}, bf16[32,7168]{1,0:T(8,128)(2,1)S(1)}, u32[]{:S(2)}, u32[]{:S(2)}) %collective-permute-start.17) | collective-permute-done | bytes 458784 | tf_op jit(solution)/shard_map/ppermute | solution.py:39
  172.7 7.1 %all-to-all-start.2 = ((bf16[16,4,7168]{2,1,0:T(4,128)(2,1)}), bf16[16,4,7168]{2,1,0:T(4,128)(2,1)S(1)}, u32[]{:S(2)}, u32[]{:S(2)}) async-start(bf16[16,4,7168]{2,1,0:T(4,128)(2,1)} %reshape.72), calls=%async_computation.2 | async-start | bytes 1835008 | tf_op jit(solution)/shard_map/all_to_all | solution.py:58
  182.3 8.8 %all-to-all-done.2 = bf16[16,4,7168]{2,1,0:T(4,128)(2,1)S(1)} async-done(((bf16[16,4,7168]{2,1,0:T(4,128)(2,1)}), bf16[16,4,7168]{2,1,0:T(4,128)(2,1)S(1)}, u32[]{:S(2)}, u32[]{:S(2)}) %all-to-all-start.2) | async-done | bytes 917536 | tf_op jit(solution)/shard_map/all_to_all | solution.py:58
  191.1 4.2 %all-to-all-start.3 = ((bf16[16,4,7168]{2,1,0:T(4,128)(2,1)}), bf16[16,4,7168]{2,1,0:T(4,128)(2,1)S(1)}, u32[]{:S(2)}, u32[]{:S(2)}) async-start(bf16[16,4,7168]{2,1,0:T(4,128)(2,1)} %reshape.74), calls=%async_computation.3 | async-start | bytes 1835008 | tf_op jit(solution)/shard_map/all_to_all | solution.py:58
  195.4 4.5 %fusion.2 = bf16[1,128,7168]{2,1,0:T(8,128)(2,1)} fusion(bf16[256,7168]{1,0:T(8,128)(2,1)} %copy-done.4, bf16[128,7168]{1,0:T(8,128)(2,1)} %collective-permute-done.20, bf16[256,256]{1,0:T(8,128)(2,1)S(1)} %get-tuple-element.31), kind=kOutput, calls=%fused_computation.10 | convolution fusion | flops 472514560 | bytes 7405568 | tf_op jit(solution)/shard_map/rf,rd->fd/dot_general | solution.py:122
  200.1 2.9 %convolution_convert_fusion.5 = bf16[128,7168]{1,0:T(8,128)(2,1)} fusion(f32[128,64]{0,1:T(8,128)S(1)} %bitcast.40, bf16[64,7168]{1,0:T(8,128)(2,1)S(1)} %reshape.73), kind=kOutput, calls=%fused_computation.9 | convolution fusion | flops 705560576 | bytes 2785280 | tf_op jit(solution)/shard_map/dot_general | solution.py:128
  203.0 3.7 %all-to-all-done.3 = bf16[16,4,7168]{2,1,0:T(4,128)(2,1)S(1)} async-done(((bf16[16,4,7168]{2,1,0:T(4,128)(2,1)}), bf16[16,4,7168]{2,1,0:T(4,128)(2,1)S(1)}, u32[]{:S(2)}, u32[]{:S(2)}) %all-to-all-start.3) | async-done | bytes 917536 | tf_op jit(solution)/shard_map/all_to_all | solution.py:58
  206.9 1.9 convolution_convert_fusion.4
  208.8 4.5 %fusion = bf16[7168,256]{1,0:T(8,128)(2,1)S(1)} fusion(bf16[256,7168]{1,0:T(8,128)(2,1)} %copy-done.3, bf16[7168,256]{1,0:T(8,128)(2,1)} %collective-permute-done.19, bf16[256,128]{1,0:T(8,128)(2,1)S(1)} %get-tuple-element.65, bf16[256,128]{1,0:T(8,128)(2,1)S(1)} %get-tuple-element.58), kind=kOutput, calls=%fused_computation.1 | convolution fusion | flops 945291264 | bytes 11141120 | tf_op jit(solution)/shard_map/rd,rf->df/dot_general | solution.py:121
  213.3 2.1 slice_bitcast_fusion
  (112 shorter events, 25.4 us)
Async XLA Ops:
  0.6 10.4 %copy-start.11 = (s32[128,8]{0,1:T(8,128)S(1)}, s32[128,8]{0,1:T(8,128)}, u32[]{:S(2)}) copy-start(s32[128,8]{0,1:T(8,128)} %param.8) | copy-start | bytes 12292
  3.9 22.0 %all-to-all-start = ((bf16[16,4,7168]{2,1,0:T(4,128)(2,1)}), bf16[16,4,7168]{2,1,0:T(4,128)(2,1)S(1)}, u32[]{:S(2)}, u32[]{:S(2)}) async-start(bf16[16,4,7168]{2,1,0:T(4,128)(2,1)} %bitcast.3), calls=%async_computation | async-start | bytes 1835008 | tf_op jit(solution)/shard_map/all_to_all | solution.py:49
  27.5 18.4 %all-to-all-start.1 = ((bf16[16,4,7168]{2,1,0:T(4,128)(2,1)}), bf16[16,4,7168]{2,1,0:T(4,128)(2,1)S(1)}, u32[]{:S(2)}, u32[]{:S(2)}) async-start(bf16[16,4,7168]{2,1,0:T(4,128)(2,1)} %bitcast.7), calls=%async_computation.1 | async-start | bytes 1835008 | tf_op jit(solution)/shard_map/all_to_all | solution.py:49
  32.0 36.0 %collective-permute-start.4 = (bf16[7168,128]{1,0:T(8,128)(2,1)}, bf16[7168,128]{1,0:T(8,128)(2,1)}, u32[]{:S(2)}, u32[]{:S(2)}) collective-permute-start(bf16[7168,128]{1,0:T(8,128)(2,1)} %bitcast.36), channel_id=1, source_target_pairs={{0,1},{1,0},{2,3},{3,2},{4,5},{5,4},{6,7},{7,6},{8,9},{9,8},{10,11... | collective-permute-start | bytes 5505032 | tf_op jit(solution)/shard_map/ppermute | solution.py:80
  32.1 35.9 %collective-permute-start.5 = (bf16[7168,128]{1,0:T(8,128)(2,1)}, bf16[7168,128]{1,0:T(8,128)(2,1)}, u32[]{:S(2)}, u32[]{:S(2)}) collective-permute-start(bf16[7168,128]{1,0:T(8,128)(2,1)} %bitcast.34), channel_id=1, source_target_pairs={{0,1},{1,0},{2,3},{3,2},{4,5},{5,4},{6,7},{7,6},{8,9},{9,8},{10,11... | collective-permute-start | bytes 5505032 | tf_op jit(solution)/shard_map/ppermute | solution.py:81
  32.6 38.6 %collective-permute-start.6 = (bf16[128,7168]{1,0:T(8,128)(2,1)}, bf16[128,7168]{1,0:T(8,128)(2,1)}, u32[]{:S(2)}, u32[]{:S(2)}) collective-permute-start(bf16[128,7168]{1,0:T(8,128)(2,1)} %bitcast.38), channel_id=1, source_target_pairs={{0,1},{1,0},{2,3},{3,2},{4,5},{5,4},{6,7},{7,6},{8,9},{9,8},{10,11... | collective-permute-start | bytes 5505032 | tf_op jit(solution)/shard_map/ppermute | solution.py:82
  32.7 24.2 %collective-permute-start = (bf16[64,7168]{1,0:T(8,128)(2,1)S(1)}, bf16[64,7168]{1,0:T(8,128)(2,1)}, u32[]{:S(2)}, u32[]{:S(2)}) collective-permute-start(bf16[64,7168]{1,0:T(8,128)(2,1)S(1)} %reshape.69), channel_id=1, source_target_pairs={{0,6},{2,0},{4,2},{6,4},{1,7},{3,1},{5,3},{7,5},{8,14},{10,8},{12,... | collective-permute-start | bytes 2752520 | tf_op jit(solution)/shard_map/ppermute | solution.py:26
  36.7 23.7 %collective-permute-start.1 = (bf16[64,7168]{1,0:T(8,128)(2,1)S(1)}, bf16[64,7168]{1,0:T(8,128)(2,1)}, u32[]{:S(2)}, u32[]{:S(2)}) collective-permute-start(bf16[64,7168]{1,0:T(8,128)(2,1)S(1)} %reshape.69), channel_id=1, source_target_pairs={{0,2},{2,4},{4,6},{6,0},{1,3},{3,5},{5,7},{7,1},{8,10},{10,12},{12... | collective-permute-start | bytes 2752520 | tf_op jit(solution)/shard_map/ppermute | solution.py:26
  46.2 25.0 %copy-start.6 = (bf16[1,7168,128]{2,1,0:T(8,128)(2,1)S(1)}, bf16[1,7168,128]{2,1,0:T(8,128)(2,1)}, u32[]{:S(2)}) copy-start(bf16[1,7168,128]{2,1,0:T(8,128)(2,1)} %param.12) | copy-start | bytes 5505028
  46.2 25.0 %copy-start.7 = (bf16[1,7168,128]{2,1,0:T(8,128)(2,1)S(1)}, bf16[1,7168,128]{2,1,0:T(8,128)(2,1)}, u32[]{:S(2)}) copy-start(bf16[1,7168,128]{2,1,0:T(8,128)(2,1)} %param.11) | copy-start | bytes 5505028
  60.4 37.4 %collective-permute-start.7 = (bf16[64,7168]{1,0:T(8,128)(2,1)S(1)}, bf16[64,7168]{1,0:T(8,128)(2,1)S(1)}, u32[]{:S(2)}, u32[]{:S(2)}) collective-permute-start(bf16[64,7168]{1,0:T(8,128)(2,1)S(1)} %reshape.71), channel_id=1, source_target_pairs={{0,2},{2,4},{4,6},{6,0},{1,3},{3,5},{5,7},{7,1},{8,10},{10,12},{12... | collective-permute-start | bytes 2752520 | tf_op jit(solution)/shard_map/ppermute | solution.py:26
  60.4 37.5 %collective-permute-start.8 = (bf16[64,7168]{1,0:T(8,128)(2,1)S(1)}, bf16[64,7168]{1,0:T(8,128)(2,1)S(1)}, u32[]{:S(2)}, u32[]{:S(2)}) collective-permute-start(bf16[64,7168]{1,0:T(8,128)(2,1)S(1)} %reshape.71), channel_id=1, source_target_pairs={{0,6},{2,0},{4,2},{6,4},{1,7},{3,1},{5,3},{7,5},{8,14},{10,8},{12,... | collective-permute-start | bytes 2752520 | tf_op jit(solution)/shard_map/ppermute | solution.py:26
  67.9 25.1 %collective-permute-start.2 = (bf16[32,7168]{1,0:T(8,128)(2,1)S(1)}, bf16[32,7168]{1,0:T(8,128)(2,1)S(1)}, u32[]{:S(2)}, u32[]{:S(2)}) collective-permute-start(bf16[32,7168]{1,0:T(8,128)(2,1)S(1)} %slice.136), channel_id=1, source_target_pairs={{0,2},{2,4},{4,6},{6,0},{1,3},{3,5},{5,7},{7,1},{8,10},{10,12},{12... | collective-permute-start | bytes 1376264 | tf_op jit(solution)/shard_map/ppermute | solution.py:31
  67.9 25.1 %collective-permute-start.3 = (bf16[32,7168]{1,0:T(8,128)(2,1)S(1)}, bf16[32,7168]{1,0:T(8,128)(2,1)S(1)}, u32[]{:S(2)}, u32[]{:S(2)}) collective-permute-start(bf16[32,7168]{1,0:T(8,128)(2,1)S(1)} %slice.137), channel_id=1, source_target_pairs={{0,6},{2,0},{4,2},{6,4},{1,7},{3,1},{5,3},{7,5},{8,14},{10,8},{12,... | collective-permute-start | bytes 1376264 | tf_op jit(solution)/shard_map/ppermute | solution.py:31
  74.3 18.7 %copy-start.2 = (bf16[256,7168]{1,0:T(8,128)(2,1)S(1)}, bf16[256,7168]{1,0:T(8,128)(2,1)}, u32[]{:S(2)}) copy-start(bf16[256,7168]{1,0:T(8,128)(2,1)} %constant_dynamic-update-slice_fusion.3) | copy-start | bytes 11010052
  94.4 22.0 %copy-start.3 = (bf16[256,7168]{1,0:T(8,128)(2,1)}, bf16[256,7168]{1,0:T(8,128)(2,1)S(1)}, u32[]{:S(2)}) copy-start(bf16[256,7168]{1,0:T(8,128)(2,1)S(1)} %constant_dynamic-update-slice_fusion) | copy-start | bytes 11010052
  97.9 14.7 %collective-permute-start.13 = (bf16[32,7168]{1,0:T(8,128)(2,1)S(1)}, bf16[32,7168]{1,0:T(8,128)(2,1)S(1)}, u32[]{:S(2)}, u32[]{:S(2)}) collective-permute-start(bf16[32,7168]{1,0:T(8,128)(2,1)S(1)} %slice.116), channel_id=1, source_target_pairs={{0,2},{2,4},{4,6},{6,0},{1,3},{3,5},{5,7},{7,1},{8,10},{10,12},{12... | collective-permute-start | bytes 1376264 | tf_op jit(solution)/shard_map/ppermute | solution.py:31
  98.0 14.6 %collective-permute-start.14 = (bf16[32,7168]{1,0:T(8,128)(2,1)S(1)}, bf16[32,7168]{1,0:T(8,128)(2,1)S(1)}, u32[]{:S(2)}, u32[]{:S(2)}) collective-permute-start(bf16[32,7168]{1,0:T(8,128)(2,1)S(1)} %slice.117), channel_id=1, source_target_pairs={{0,6},{2,0},{4,2},{6,4},{1,7},{3,1},{5,3},{7,5},{8,14},{10,8},{12,... | collective-permute-start | bytes 1376264 | tf_op jit(solution)/shard_map/ppermute | solution.py:31
  101.3 28.7 %collective-permute-start.9 = (bf16[64,7168]{1,0:T(8,128)(2,1)S(1)}, bf16[64,7168]{1,0:T(8,128)(2,1)S(1)}, u32[]{:S(2)}, u32[]{:S(2)}) collective-permute-start(bf16[64,7168]{1,0:T(8,128)(2,1)S(1)} %get-tuple-element.35), channel_id=1, source_target_pairs={{0,6},{2,0},{4,2},{6,4},{1,7},{3,1},{5,3},{7,5},{8,14},{10,8},{12,... | collective-permute-start | bytes 2752520 | tf_op jit(solution)/shard_map/ppermute | solution.py:38
  103.0 26.7 %collective-permute-start.10 = (bf16[64,7168]{1,0:T(8,128)(2,1)S(1)}, bf16[64,7168]{1,0:T(8,128)(2,1)S(1)}, u32[]{:S(2)}, u32[]{:S(2)}) collective-permute-start(bf16[64,7168]{1,0:T(8,128)(2,1)S(1)} %get-tuple-element.36), channel_id=1, source_target_pairs={{0,2},{2,4},{4,6},{6,0},{1,3},{3,5},{5,7},{7,1},{8,10},{10,12},{12... | collective-permute-start | bytes 2752520 | tf_op jit(solution)/shard_map/ppermute | solution.py:37
  115.1 80.2 %collective-permute-start.20 = (bf16[128,7168]{1,0:T(8,128)(2,1)}, bf16[128,7168]{1,0:T(8,128)(2,1)}, u32[]{:S(2)}, u32[]{:S(2)}) collective-permute-start(bf16[128,7168]{1,0:T(8,128)(2,1)} %convolution_convert_fusion.3), channel_id=1, source_target_pairs={{0,1},{1,0},{2,3},{3,2},{4,5},{5,4},{6,7},{7,6},{8,9},{9,8},{10,11... | collective-permute-start | bytes 5505032 | tf_op jit(solution)/shard_map/ppermute | solution.py:120
  119.5 89.3 %collective-permute-start.19 = (bf16[7168,256]{1,0:T(8,128)(2,1)}, bf16[7168,256]{1,0:T(8,128)(2,1)}, u32[]{:S(2)}, u32[]{:S(2)}) collective-permute-start(bf16[7168,256]{1,0:T(8,128)(2,1)} %convolution_convert_fusion), channel_id=1, source_target_pairs={{0,1},{1,0},{2,3},{3,2},{4,5},{5,4},{6,7},{7,6},{8,9},{9,8},{10,11... | collective-permute-start | bytes 11010056 | tf_op jit(solution)/shard_map/ppermute | solution.py:119
  122.1 48.8 %copy-start.5 = (bf16[256,7168]{1,0:T(8,128)(2,1)}, bf16[256,7168]{1,0:T(8,128)(2,1)S(1)}, u32[]{:S(2)}) copy-start(bf16[256,7168]{1,0:T(8,128)(2,1)S(1)} %convolution_convert_fusion.1) | copy-start | bytes 11010052
  129.7 14.7 %collective-permute-start.11 = (bf16[32,7168]{1,0:T(8,128)(2,1)S(1)}, bf16[32,7168]{1,0:T(8,128)(2,1)S(1)}, u32[]{:S(2)}, u32[]{:S(2)}) collective-permute-start(bf16[32,7168]{1,0:T(8,128)(2,1)S(1)} %add_convert_fusion.7), channel_id=1, source_target_pairs={{0,2},{2,4},{4,6},{6,0},{1,3},{3,5},{5,7},{7,1},{8,10},{10,12},{12... | collective-permute-start | bytes 1376264 | tf_op jit(solution)/shard_map/ppermute | solution.py:39
  130.0 31.0 %collective-permute-start.15 = (bf16[64,7168]{1,0:T(8,128)(2,1)S(1)}, bf16[64,7168]{1,0:T(8,128)(2,1)S(1)}, u32[]{:S(2)}, u32[]{:S(2)}) collective-permute-start(bf16[64,7168]{1,0:T(8,128)(2,1)S(1)} %get-tuple-element.41), channel_id=1, source_target_pairs={{0,6},{2,0},{4,2},{6,4},{1,7},{3,1},{5,3},{7,5},{8,14},{10,8},{12,... | collective-permute-start | bytes 2752520 | tf_op jit(solution)/shard_map/ppermute | solution.py:38
  133.2 27.3 %collective-permute-start.16 = (bf16[64,7168]{1,0:T(8,128)(2,1)S(1)}, bf16[64,7168]{1,0:T(8,128)(2,1)S(1)}, u32[]{:S(2)}, u32[]{:S(2)}) collective-permute-start(bf16[64,7168]{1,0:T(8,128)(2,1)S(1)} %get-tuple-element.42), channel_id=1, source_target_pairs={{0,2},{2,4},{4,6},{6,0},{1,3},{3,5},{5,7},{7,1},{8,10},{10,12},{12... | collective-permute-start | bytes 2752520 | tf_op jit(solution)/shard_map/ppermute | solution.py:37
  144.7 16.0 %collective-permute-start.12 = (bf16[32,7168]{1,0:T(8,128)(2,1)S(1)}, bf16[32,7168]{1,0:T(8,128)(2,1)S(1)}, u32[]{:S(2)}, u32[]{:S(2)}) collective-permute-start(bf16[32,7168]{1,0:T(8,128)(2,1)S(1)} %get-tuple-element.46), channel_id=1, source_target_pairs={{0,6},{2,0},{4,2},{6,4},{1,7},{3,1},{5,3},{7,5},{8,14},{10,8},{12,... | collective-permute-start | bytes 1376264 | tf_op jit(solution)/shard_map/ppermute | solution.py:40
  160.6 10.7 %copy-start.9 = (bf16[64,7168]{1,0:T(8,128)(2,1)}, bf16[64,7168]{1,0:T(8,128)(2,1)S(1)}, u32[]{:S(2)}) copy-start(bf16[64,7168]{1,0:T(8,128)(2,1)S(1)} %collective-permute-done.16) | copy-start | bytes 2752516
  160.7 10.3 %collective-permute-start.17 = (bf16[32,7168]{1,0:T(8,128)(2,1)S(1)}, bf16[32,7168]{1,0:T(8,128)(2,1)S(1)}, u32[]{:S(2)}, u32[]{:S(2)}) collective-permute-start(bf16[32,7168]{1,0:T(8,128)(2,1)S(1)} %add_convert_fusion.3), channel_id=1, source_target_pairs={{0,2},{2,4},{4,6},{6,0},{1,3},{3,5},{5,7},{7,1},{8,10},{10,12},{12... | collective-permute-start | bytes 1376264 | tf_op jit(solution)/shard_map/ppermute | solution.py:39
  171.2 8.6 %collective-permute-start.18 = (bf16[32,7168]{1,0:T(8,128)(2,1)S(1)}, bf16[32,7168]{1,0:T(8,128)(2,1)S(1)}, u32[]{:S(2)}, u32[]{:S(2)}) collective-permute-start(bf16[32,7168]{1,0:T(8,128)(2,1)S(1)} %get-tuple-element.44), channel_id=1, source_target_pairs={{0,6},{2,0},{4,2},{6,4},{1,7},{3,1},{5,3},{7,5},{8,14},{10,8},{12,... | collective-permute-start | bytes 1376264 | tf_op jit(solution)/shard_map/ppermute | solution.py:40
  172.7 18.5 %all-to-all-start.2 = ((bf16[16,4,7168]{2,1,0:T(4,128)(2,1)}), bf16[16,4,7168]{2,1,0:T(4,128)(2,1)S(1)}, u32[]{:S(2)}, u32[]{:S(2)}) async-start(bf16[16,4,7168]{2,1,0:T(4,128)(2,1)} %reshape.72), calls=%async_computation.2 | async-start | bytes 1835008 | tf_op jit(solution)/shard_map/all_to_all | solution.py:58
  191.1 15.6 %all-to-all-start.3 = ((bf16[16,4,7168]{2,1,0:T(4,128)(2,1)}), bf16[16,4,7168]{2,1,0:T(4,128)(2,1)S(1)}, u32[]{:S(2)}, u32[]{:S(2)}) async-start(bf16[16,4,7168]{2,1,0:T(4,128)(2,1)} %reshape.74), calls=%async_computation.3 | async-start | bytes 1835008 | tf_op jit(solution)/shard_map/all_to_all | solution.py:58
  (6 other events, 36.8 us)

commit v2 on v1

v2 whole, which is shorter than its diff:
```python
import jax
import jax.numpy as jnp
from jax import lax
from jax.sharding import Mesh, PartitionSpec as P

CAP = 4
LINE = 4 * CAP
PAIR = ("xl", "y")
REST = ("xh", "z", "core")
PLANE = ("xl", "xh", "y")
SWAP = [(0, 1), (1, 0)]
F32 = jnp.float32
BF16 = jnp.bfloat16
def z_by(step):
    return [(i, (i + step) % 4) for i in range(4)]


def tie(*values):
    return lax.optimization_barrier(values)


def add(*terms):
    return sum(t.astype(F32) for t in terms).astype(BF16)


def near_z(rows):
    return lax.ppermute(rows, "z", z_by(1)), lax.ppermute(rows, "z", z_by(3))


def halves(below, above):
    cut = below.shape[0] // 2
    return below[:cut], above[cut:]


def far_z(low, high):
    return lax.ppermute(low, "z", z_by(1)), lax.ppermute(high, "z", z_by(3))


def across(rows):
    return lax.ppermute(rows, "xh", SWAP)


def near_x(below, above):
    return across(jnp.concatenate([below[:LINE], above[:LINE]], axis=0))


def all_rows(plane, below, above, low, high, near, far):
    return jnp.concatenate(
        [plane, above, near[LINE:], low, high, far, below, near[:LINE]], axis=0
    )


def scatter_in(parts):
    cut = parts.shape[0] // 8
    return parts[3 * cut : 5 * cut], parts[5 * cut : 7 * cut]


def scatter_far(parts, up_1, down_1):
    cut = parts.shape[0] // 8
    return add(parts[2 * cut : 3 * cut], up_1[cut:]), add(parts[7 * cut :], down_1[:cut])


def scatter_out(parts, up_1, down_1, up_2, down_2):
    cut = parts.shape[0] // 8
    top = add(parts[:cut], down_1[cut:], up_2)
    low = add(parts[cut : 2 * cut], up_1[:cut], down_2)
    return jnp.concatenate([top, low], axis=0)


def relative(blocks):
    xl, xh = lax.axis_index("xl"), lax.axis_index("xh")
    same = jnp.where(xl == 0, blocks[:2], blocks[2:])
    other = jnp.where(xl == 0, blocks[2:], blocks[:2])
    own = jnp.where(xh == 0, same[0], same[1])
    far = jnp.where(xh == 0, same[1], same[0])
    return jnp.concatenate([own, other.reshape(2 * LINE, -1), far], axis=0)


def absolute(rows):
    xl, xh = lax.axis_index("xl"), lax.axis_index("xh")
    own, far = rows[:LINE], rows[3 * LINE :]
    other = rows[LINE : 3 * LINE]
    same = jnp.concatenate([jnp.where(xh == 0, own, far), jnp.where(xh == 0, far, own)], axis=0)
    first, second = jnp.where(xl == 0, same, other), jnp.where(xl == 0, other, same)
    return jnp.concatenate([first, second], axis=0)


def to_plane(slots):
    width = slots.shape[-1]
    twice = jnp.broadcast_to(slots.reshape(2, 1, 4, CAP, width), (2, 2, 4, CAP, width))
    return twice.reshape(16, CAP, width)


def move_plane(twice):
    moved = lax.all_to_all(twice, PLANE, split_axis=0, concat_axis=0, tiled=True)
    return relative(moved.reshape(4, LINE, -1))


def to_slots(rows):
    width = rows.shape[1]
    sent = absolute(rows).reshape(16, CAP, width)
    back = lax.all_to_all(sent, PLANE, split_axis=0, concat_axis=0, tiled=True)
    return back.reshape(16 * CAP, width)


def local(tokens, route, gates, cotangent, w_gate, w_up, w_down):
    model_width = tokens.shape[1]
    half = w_down.shape[1]
    matches = route[:, :, None] == jnp.arange(8, dtype=jnp.int32)
    member = jnp.any(matches, axis=1)
    weight = jnp.sum(jnp.where(matches, gates[:, :, None], 0.0), axis=1)
    rows = jnp.arange(route.shape[0])
    earlier = (rows[None, :] < rows[:, None]).astype(BF16)
    places = jnp.dot(earlier, member.astype(BF16), preferred_element_type=F32)
    picked = member[:, :, None] & (places[:, :, None] == jnp.arange(CAP, dtype=F32))
    picked_b = picked.astype(BF16).reshape(-1, 8 * CAP)
    picked_w = jnp.where(picked, weight[:, :, None], 0.0)
    pair = lambda a: jnp.broadcast_to(a.reshape(-1, 2, 1, 4, CAP), (a.shape[0], 2, 2, 4, CAP))
    twice_b = pair(picked.astype(BF16)).reshape(-1, 16 * CAP)
    twice_w = pair(picked_w).reshape(-1, 16 * CAP)
    picked_w = picked_w.reshape(-1, 8 * CAP)
    slot_gate = jnp.sum(picked_w, axis=0)
    x_slots = jnp.einsum("ts,td->sd", picked_b, tokens, preferred_element_type=F32).astype(BF16)
    gate_other = lax.ppermute(w_gate[0], "core", SWAP)
    up_other = lax.ppermute(w_up[0], "core", SWAP)
    down_other = lax.ppermute(w_down[0], "core", SWAP)

    d_rows = jnp.einsum("ts,td->sd", picked_b, cotangent, preferred_element_type=F32)
    d_slots = (d_rows * slot_gate[:, None]).astype(BF16)
    plane_x = move_plane(to_plane(x_slots))
    x_near = near_z(plane_x[: 3 * LINE])
    d_twice, plane_x = tie(to_plane(d_slots), plane_x)
    plane_d = move_plane(d_twice)
    x_far = far_z(*tie(*halves(*x_near)))
    x_side = near_x(*x_near)
    d_ring, *x_near = tie(plane_d[: 3 * LINE], *x_near)
    d_near = near_z(d_ring)
    x_last = across(x_far[0][:LINE])
    tied = tie(w_gate[0], gate_other, w_up[0], up_other, w_down[0], down_other, *x_far)
    parts, x_far = tied[:6], tied[6:]
    w_in = jnp.concatenate(parts[:4], axis=1)
    w_out = jnp.concatenate(parts[4:], axis=0)
    w_in, w_out = tie(w_in, w_out)
    rows_x = all_rows(plane_x, *x_near, *x_far, x_side, x_last)

    pre = jnp.dot(rows_x, w_in, preferred_element_type=F32)
    gate_pre, up_pre = pre[:, : 2 * half], pre[:, 2 * half :]
    logistic = jax.nn.sigmoid(gate_pre)
    hidden = (gate_pre * logistic * up_pre).astype(BF16)
    hidden, gate_pre, up_pre = tie(hidden, gate_pre, up_pre)
    d_low, d_high = tie(*halves(*d_near))
    d_far = far_z(d_low, d_high)
    d_side = near_x(*d_near)
    y_part = jnp.dot(hidden, w_out, preferred_element_type=F32).astype(BF16)
    d_last = across(d_far[0][:LINE])
    y_up, y_down, *d_far = tie(*scatter_in(y_part), *d_far)
    y_1 = far_z(y_up, y_down)
    rows_d = all_rows(plane_d, *d_near, *d_far, d_side, d_last)

    hidden_grad = jnp.einsum("rd,fd->rf", rows_d, w_out, preferred_element_type=F32)
    logistic = jax.nn.sigmoid(gate_pre)
    slope = logistic * (1.0 + gate_pre * (1.0 - logistic))
    gate_grad = (hidden_grad * up_pre * slope).astype(BF16)
    up_grad = (hidden_grad * gate_pre * logistic).astype(BF16)
    both = jnp.concatenate([gate_grad, up_grad], axis=1)
    q_part = jnp.einsum("rf,df->rd", both, w_in, preferred_element_type=F32).astype(BF16)
    y_up, y_down, *y_1 = tie(*scatter_far(y_part, *y_1), *y_1)
    y_2 = far_z(y_up, y_down)
    q_up, q_down, *y_1 = tie(*scatter_in(q_part), *y_1)
    q_1 = far_z(q_up, q_down)
    y_rows = scatter_out(y_part, *y_1, *y_2)
    back_out = to_slots(y_rows)
    q_up, q_down, back_out, *q_1 = tie(*scatter_far(q_part, *q_1), back_out, *q_1)
    q_2 = far_z(q_up, q_down)
    q_rows = scatter_out(q_part, *q_1, *q_2)

    gate_grad, up_grad, hidden, q_part = tie(gate_grad, up_grad, hidden, q_part)
    late = lambda a, b: jnp.einsum("rd,rf->df", a, b, preferred_element_type=F32)
    gate_got = lax.ppermute(late(rows_x, gate_grad[:, half:]).astype(BF16), "core", SWAP)
    up_got = lax.ppermute(late(rows_x, up_grad[:, half:]).astype(BF16), "core", SWAP)
    out_got = lax.ppermute(late(hidden[:, half:], rows_d).astype(BF16), "core", SWAP)
    grad_gate = add(late(rows_x, gate_grad[:, :half]), gate_got)
    grad_up = add(late(rows_x, up_grad[:, :half]), up_got)
    grad_down = add(late(hidden[:, :half], rows_d), out_got)

    back_in = to_slots(q_rows)
    mixed = jnp.dot(
        twice_w, back_out.astype(F32), precision=lax.Precision.HIGHEST
    ).astype(BF16)
    grad_tokens = jnp.dot(twice_b, back_in, preferred_element_type=F32).astype(BF16)
    return (mixed, grad_tokens, grad_gate[None], grad_up[None], grad_down[None])


def solution(mesh):
    fine = Mesh(mesh.devices.reshape(2, 4, 2, 4, 2), PAIR + REST)
    rows = P(PAIR + REST, None)
    wide = P(PAIR, None, REST)
    tall = P(PAIR, REST, None)
    return jax.shard_map(
        local,
        mesh=fine,
        in_specs=(rows, rows, rows, rows, wide, wide, tall),
        out_specs=(rows, rows, wide, wide, tall),
        check_vma=False,
    )
```

time: 216 us -> 196 us (0.907)
  waiting for transfers between devices: 118 us -> 58.5 us
  local copies, waits for them, and re-layouts: 15.8 us -> 27.7 us
  matrix products: 27.9 us -> 38.5 us
  starting transfers between devices: 43.8 us -> 52.3 us
  other arithmetic: 8.52 us -> 16.6 us
    ppermute x14 -> x19, waiting for transfers between devices: 70.4 us -> 33.4 us  [the longest x12 28 us: far_z(): return (lax.ppermute(low, 'z', z_by(1)), lax.ppermute(high, 'z', z_by(3)))]
    ppermute x14 -> x19, starting transfers between devices: 12.9 us -> 25 us  [the longest x12 17.4 us: far_z(): return (lax.ppermute(low, 'z', z_by(1)), lax.ppermute(high, 'z', z_by(3)))]
    all_to_all x2, waiting for transfers between devices: 12.5 us -> 3.4 us  [to_slots(): back = lax.all_to_all(sent, PLANE, split_axis=0, concat_axis=0, tiled=True)]
    unnamed x34 -> x37, local copies, waits for them, and re-layouts: 3.6 us -> 11.9 us
    all_to_all x2, waiting for transfers between devices: 21.1 us -> 13.4 us  [move_plane(): lax.all_to_all(twice, PLANE, split_axis=0, concat_axis=0, tiled=True)]
    dot_general x4 -> x7, matrix products: 14.5 us -> 21.9 us  [the longest x6 21.7 us: local(): jnp.einsum('rd,rf->df', a, b, preferred_element_type=F32)]
    ppermute x4, waiting for transfers between devices: 14.2 us -> 8.36 us  [near_z(): return (lax.ppermute(rows, 'z', z_by(1)), lax.ppermute(rows, 'z', z_by(3)))]
    convert_element_type x6 -> x4, other arithmetic: 2.11 us -> 7.24 us  [add(): return sum((t.astype(F32) for t in terms)).astype(BF16)]
  transfers between devices with their start and end apart: 25 -> 30, of which waited for: 12 -> 13; matrix products, arithmetic and copies ran while one was open for 19% -> 40% of each run, Pallas kernels for 0% -> 0%
where the time goes in v2:
time: 196 us; the launch traced here: 195 us
  waiting for transfers between devices  58.5 us (30%)
  starting transfers between devices  52.3 us (27%)
  matrix products  38.5 us (20%)
  local copies, waits for them, and re-layouts  27.7 us (14%)
  other arithmetic  16.6 us (8%)
    ppermute x12, waiting for transfers between devices, far_z(): return (lax.ppermute(low, 'z', z_by(1)), lax.ppermute(high, 'z', z_by(3)))  28 us
    dot_general x6, matrix products, local(): jnp.einsum('rd,rf->df', a, b, preferred_element_type=F32)  21.7 us
    ppermute x12, starting transfers between devices, far_z(): return (lax.ppermute(low, 'z', z_by(1)), lax.ppermute(high, 'z', z_by(3)))  17.4 us
    all_to_all x2, waiting for transfers between devices, move_plane(): lax.all_to_all(twice, PLANE, split_axis=0, concat_axis=0, tiled=True)  13.4 us
    unnamed x37, local copies, waits for them, and re-layouts  11.9 us
    all_to_all x2, starting transfers between devices, move_plane(): lax.all_to_all(twice, PLANE, split_axis=0, concat_axis=0, tiled=True)  11 us
    all_to_all x2, starting transfers between devices, to_slots(): back = lax.all_to_all(sent, PLANE, split_axis=0, concat_axis=0, tiled=True)  9.6 us
    ppermute x4, waiting for transfers between devices, near_z(): return (lax.ppermute(rows, 'z', z_by(1)), lax.ppermute(rows, 'z', z_by(3)))  8.36 us
  transfers between devices with their start and end apart: 30, of which 13 were waited for; matrix products, arithmetic and copies ran while one was open for 40% of the time, Pallas kernels for 0%

profile of v2, /device:TPU:0, one launch (start us, length us, event | category | flops | bytes accessed | tf_op | source)
XLA Modules:
  0.0 194.8 jit_solution(15451382005844765543)
XLA Ops:
  4.1 7.1 %all-to-all-start = ((bf16[16,4,7168]{2,1,0:T(4,128)(2,1)}), bf16[16,4,7168]{2,1,0:T(4,128)(2,1)S(1)}, u32[]{:S(2)}, u32[]{:S(2)}) async-start(bf16[16,4,7168]{2,1,0:T(4,128)(2,1)} %bitcast.7), calls=%async_computation | async-start | bytes 1835008 | tf_op jit(solution)/shard_map/all_to_all | solution.py:95
  13.6 13.4 %all-to-all-done = bf16[16,4,7168]{2,1,0:T(4,128)(2,1)S(1)} async-done(((bf16[16,4,7168]{2,1,0:T(4,128)(2,1)}), bf16[16,4,7168]{2,1,0:T(4,128)(2,1)S(1)}, u32[]{:S(2)}, u32[]{:S(2)}) %all-to-all-start) | async-done | bytes 917536 | tf_op jit(solution)/shard_map/all_to_all | solution.py:95
  31.1 2.1 %collective-permute-start.1 = (bf16[48,7168]{1,0:T(8,128)(2,1)}, bf16[48,7168]{1,0:T(8,128)(2,1)}, u32[]{:S(2)}, u32[]{:S(2)}) collective-permute-start(bf16[48,7168]{1,0:T(8,128)(2,1)} %constant_dynamic-update-slice_fusion), channel_id=1, source_target_pairs={{0,6},{2,0},{4,2},{6,4},{1,7},{3,1},{5,3},{7,5},{8,14},{10,8},{12,... | collective-permute-start | bytes 2064392 | tf_op jit(solution)/shard_map/ppermute | solution.py:27
  34.5 3.8 %all-to-all-start.1 = ((bf16[16,4,7168]{2,1,0:T(4,128)(2,1)}), bf16[16,4,7168]{2,1,0:T(4,128)(2,1)S(1)}, u32[]{:S(2)}, u32[]{:S(2)}) async-start(bf16[16,4,7168]{2,1,0:T(4,128)(2,1)} %bitcast.40), calls=%async_computation.1 | async-start | bytes 1835008 | tf_op jit(solution)/shard_map/all_to_all | solution.py:95
  39.3 8.4 %collective-permute-done = bf16[48,7168]{1,0:T(8,128)(2,1)S(1)} collective-permute-done((bf16[48,7168]{1,0:T(8,128)(2,1)}, bf16[48,7168]{1,0:T(8,128)(2,1)S(1)}, u32[]{:S(2)}, u32[]{:S(2)}) %collective-permute-start) | collective-permute-done | bytes 688160 | tf_op jit(solution)/shard_map/ppermute | solution.py:27
  50.8 2.6 %collective-permute-start.10 = (bf16[24,7168]{1,0:T(8,128)(2,1)}, bf16[24,7168]{1,0:T(8,128)(2,1)}, u32[]{:S(2)}, u32[]{:S(2)}) collective-permute-start(bf16[24,7168]{1,0:T(8,128)(2,1)} %slice.259), channel_id=1, source_target_pairs={{0,6},{2,0},{4,2},{6,4},{1,7},{3,1},{5,3},{7,5},{8,14},{10,8},{12,... | collective-permute-start | bytes 1032200 | tf_op jit(solution)/shard_map/ppermute | solution.py:36
  60.4 2.4 %collective-permute-start.5 = (bf16[32,7168]{1,0:T(8,128)(2,1)}, bf16[32,7168]{1,0:T(8,128)(2,1)S(1)}, u32[]{:S(2)}, u32[]{:S(2)}) collective-permute-start(bf16[32,7168]{1,0:T(8,128)(2,1)} %pad_maximum_fusion.9), channel_id=1, source_target_pairs={{0,8},{8,0},{1,9},{9,1},{2,10},{10,2},{3,11},{11,3},{4,12},{12,4},... | collective-permute-start | bytes 1376264 | tf_op jit(solution)/shard_map/ppermute | solution.py:40
  64.8 4.0 %pad_maximum_fusion = bf16[7168,512]{1,0:T(8,128)(2,1)S(1)} fusion(bf16[7168,128]{1,0:T(8,128)(2,1)} %collective-permute-done.7, bf16[7168,128]{1,0:T(8,128)(2,1)} %bitcast.42, bf16[7168,128]{1,0:T(8,128)(2,1)} %collective-permute-done.6, bf16[7168,128]{1,0:T(8,128)(2,1)} %bitcast.44), kind=kLoop, calls=%fused_computation.19 | loop fusion | flops 29360128 | bytes 14680064 | tf_op jit(solution)/shard_map/concatenate | solution.py:141
  73.9 4.5 %collective-permute-done.11 = bf16[16,7168]{1,0:T(8,128)(2,1)S(1)} collective-permute-done((bf16[16,7168]{1,0:T(8,128)(2,1)S(1)}, bf16[16,7168]{1,0:T(8,128)(2,1)S(1)}, u32[]{:S(2)}, u32[]{:S(2)}) %collective-permute-start.11) | collective-permute-done | bytes 229408 | tf_op jit(solution)/shard_map/ppermute | solution.py:40
  84.6 3.2 %collective-permute-start.13 = (bf16[24,7168]{1,0:T(8,128)(2,1)S(1)}, bf16[24,7168]{1,0:T(8,128)(2,1)S(1)}, u32[]{:S(2)}, u32[]{:S(2)}) collective-permute-start(bf16[24,7168]{1,0:T(8,128)(2,1)S(1)} %slice.267), channel_id=1, source_target_pairs={{0,6},{2,0},{4,2},{6,4},{1,7},{3,1},{5,3},{7,5},{8,14},{10,8},{12,... | collective-permute-start | bytes 1032200 | tf_op jit(solution)/shard_map/ppermute | solution.py:36
  88.8 4.5 %collective-permute-done.12 = bf16[24,7168]{1,0:T(8,128)(2,1)S(1)} collective-permute-done((bf16[24,7168]{1,0:T(8,128)(2,1)S(1)}, bf16[24,7168]{1,0:T(8,128)(2,1)S(1)}, u32[]{:S(2)}, u32[]{:S(2)}) %collective-permute-start.12) | collective-permute-done | bytes 344096 | tf_op jit(solution)/shard_map/ppermute | solution.py:36
  93.3 2.1 %collective-permute-start.14 = (bf16[16,7168]{1,0:T(8,128)(2,1)S(1)}, bf16[16,7168]{1,0:T(8,128)(2,1)S(1)}, u32[]{:S(2)}, u32[]{:S(2)}) collective-permute-start(bf16[16,7168]{1,0:T(8,128)(2,1)S(1)} %slice.268), channel_id=1, source_target_pairs={{0,8},{8,0},{1,9},{9,1},{2,10},{10,2},{3,11},{11,3},{4,12},{12,4},... | collective-permute-start | bytes 688136 | tf_op jit(solution)/shard_map/ppermute | solution.py:40
  95.4 3.2 %collective-permute-start.16 = (bf16[64,7168]{1,0:T(8,128)(2,1)}, bf16[64,7168]{1,0:T(8,128)(2,1)}, u32[]{:S(2)}, u32[]{:S(2)}) collective-permute-start(bf16[64,7168]{1,0:T(8,128)(2,1)} %get-tuple-element.72), channel_id=1, source_target_pairs={{0,6},{2,0},{4,2},{6,4},{1,7},{3,1},{5,3},{7,5},{8,14},{10,8},{12,... | collective-permute-start | bytes 2752520 | tf_op jit(solution)/shard_map/ppermute | solution.py:36
  103.2 3.2 %multiply_convert_fusion.1 = (bf16[256,256]{1,0:T(8,128)(2,1)S(1)}, bf16[256,256]{1,0:T(8,128)(2,1)S(1)}) fusion(f32[256,256]{1,0:T(8,128)S(1)} %get-tuple-element.70, f32[256,256]{1,0:T(8,128)S(1)} %get-tuple-element.69, bf16[256,7168]{1,0:T(8,128)(2,1)} %slice_dynamic-update-slice_fusion, bf16[256,7168]{1,0:T(8,128)(2,1)S(1)} %pad_maximum_fusion.1), kind=kOutput, calls=%fused_computation.51 | convolution fusion | flops 940376064 | bytes 8126464 | tf_op jit(solution)/shard_map/rd,fd->rf/dot_general | solution.py:160
  106.4 2.1 %convolution_convert_fusion = bf16[256,7168]{1,0:T(8,128)(2,1)S(1)} fusion(bf16[7168,512]{1,0:T(8,128)(2,1)S(1)} %pad_maximum_fusion, bf16[256,256]{1,0:T(8,128)(2,1)S(1)} %get-tuple-element.87, bf16[256,256]{1,0:T(8,128)(2,1)S(1)} %get-tuple-element.86), kind=kOutput, calls=%fused_computation | convolution fusion | flops 1881407488 | bytes 11272192 | tf_op jit(solution)/shard_map/rf,df->rd/dot_general | solution.py:166
  110.0 2.9 %collective-permute-done.16 = bf16[64,7168]{1,0:T(8,128)(2,1)} collective-permute-done((bf16[64,7168]{1,0:T(8,128)(2,1)}, bf16[64,7168]{1,0:T(8,128)(2,1)}, u32[]{:S(2)}, u32[]{:S(2)}) %collective-permute-start.16) | collective-permute-done | bytes 917536 | tf_op jit(solution)/shard_map/ppermute | solution.py:36
  112.9 4.7 %collective-permute-done.15 = bf16[64,7168]{1,0:T(8,128)(2,1)} collective-permute-done((bf16[64,7168]{1,0:T(8,128)(2,1)S(1)}, bf16[64,7168]{1,0:T(8,128)(2,1)}, u32[]{:S(2)}, u32[]{:S(2)}) %collective-permute-start.15) | collective-permute-done | bytes 917536 | tf_op jit(solution)/shard_map/ppermute | solution.py:36
  119.1 3.2 %collective-permute-start.20 = (bf16[32,7168]{1,0:T(8,128)(2,1)S(1)}, bf16[32,7168]{1,0:T(8,128)(2,1)S(1)}, u32[]{:S(2)}, u32[]{:S(2)}) collective-permute-start(bf16[32,7168]{1,0:T(8,128)(2,1)S(1)} %get-tuple-element.80), channel_id=1, source_target_pairs={{0,6},{2,0},{4,2},{6,4},{1,7},{3,1},{5,3},{7,5},{8,14},{10,8},{12,... | collective-permute-start | bytes 1376264 | tf_op jit(solution)/shard_map/ppermute | solution.py:36
  122.3 2.4 %convolution_convert_fusion.4 = bf16[7168,128]{1,0:T(8,128)(2,1)} fusion(bf16[256,7168]{1,0:T(8,128)(2,1)S(1)} %slice_dynamic-update-slice_fusion.1, bf16[256,256]{1,0:T(8,128)(2,1)S(1)} %get-tuple-element.86), kind=kOutput, calls=%fused_computation.10 | convolution fusion | flops 470679552 | bytes 5570560 | tf_op jit(solution)/shard_map/rd,rf->df/dot_general | solution.py:178
  124.8 2.4 %convolution_convert_fusion.3 = bf16[7168,128]{1,0:T(8,128)(2,1)} fusion(bf16[256,7168]{1,0:T(8,128)(2,1)S(1)} %slice_dynamic-update-slice_fusion.1, bf16[256,256]{1,0:T(8,128)(2,1)S(1)} %get-tuple-element.87), kind=kOutput, calls=%fused_computation.9 | convolution fusion | flops 470679552 | bytes 5570560 | tf_op jit(solution)/shard_map/rd,rf->df/dot_general | solution.py:178
  132.7 4.8 %all-to-all-start.2 = ((bf16[16,4,7168]{2,1,0:T(4,128)(2,1)}), bf16[16,4,7168]{2,1,0:T(4,128)(2,1)S(1)}, u32[]{:S(2)}, u32[]{:S(2)}) async-start(bf16[16,4,7168]{2,1,0:T(4,128)(2,1)} %reshape.134), calls=%async_computation.2 | async-start | bytes 1835008 | tf_op jit(solution)/shard_map/all_to_all | solution.py:102
  137.6 12.7 %collective-permute-done.18 = bf16[64,7168]{1,0:T(8,128)(2,1)} collective-permute-done((bf16[64,7168]{1,0:T(8,128)(2,1)}, bf16[64,7168]{1,0:T(8,128)(2,1)}, u32[]{:S(2)}, u32[]{:S(2)}) %collective-permute-start.18) | collective-permute-done | bytes 917536 | tf_op jit(solution)/shard_map/ppermute | solution.py:36
  151.5 2.6 %add_convert_fusion.4 = (bf16[32,7168]{1,0:T(8,128)(2,1)}, bf16[32,7168]{1,0:T(8,128)(2,1)}) fusion(bf16[64,7168]{1,0:T(8,128)(2,1)} %collective-permute-done.18, bf16[256,7168]{1,0:T(8,128)(2,1)} %copy-done.5, bf16[64,7168]{1,0:T(8,128)(2,1)} %collective-permute-done.17), kind=kLoop, calls=%fused_computation.28 | loop fusion | flops 1835008 | bytes 2752512 | tf_op jit(solution)/shard_map/convert_element_type | solution.py:23
  155.7 2.8 %collective-permute-start.22 = (bf16[32,7168]{1,0:T(8,128)(2,1)}, bf16[32,7168]{1,0:T(8,128)(2,1)S(1)}, u32[]{:S(2)}, u32[]{:S(2)}) collective-permute-start(bf16[32,7168]{1,0:T(8,128)(2,1)} %get-tuple-element.85), channel_id=1, source_target_pairs={{0,6},{2,0},{4,2},{6,4},{1,7},{3,1},{5,3},{7,5},{8,14},{10,8},{12,... | collective-permute-start | bytes 1376264 | tf_op jit(solution)/shard_map/ppermute | solution.py:36
  158.5 3.9 %convolution_convert_fusion.2 = bf16[128,7168]{1,0:T(8,128)(2,1)} fusion(bf16[256,7168]{1,0:T(8,128)(2,1)} %slice_dynamic-update-slice_fusion, bf16[256,256]{1,0:T(8,128)(2,1)S(1)} %get-tuple-element.88), kind=kOutput, calls=%fused_computation.8 | convolution fusion | flops 470679552 | bytes 5570560 | tf_op jit(solution)/shard_map/rd,rf->df/dot_general | solution.py:178
  162.5 3.9 %fusion.5 = bf16[1,7168,128]{2,1,0:T(8,128)(2,1)} fusion(bf16[256,7168]{1,0:T(8,128)(2,1)S(1)} %copy-done.4, bf16[7168,128]{1,0:T(8,128)(2,1)} %collective-permute-done.23, bf16[256,256]{1,0:T(8,128)(2,1)S(1)} %get-tuple-element.86), kind=kOutput, calls=%fused_computation.15 | convolution fusion | flops 472514560 | bytes 7405568 | tf_op jit(solution)/shard_map/rd,rf->df/dot_general | solution.py:178
  170.4 4.8 %all-to-all-start.3 = ((bf16[16,4,7168]{2,1,0:T(4,128)(2,1)}), bf16[16,4,7168]{2,1,0:T(4,128)(2,1)S(1)}, u32[]{:S(2)}, u32[]{:S(2)}) async-start(bf16[16,4,7168]{2,1,0:T(4,128)(2,1)} %reshape.137), calls=%async_computation.3 | async-start | bytes 1835008 | tf_op jit(solution)/shard_map/all_to_all | solution.py:102
  175.3 4.4 %fusion.4 = bf16[1,7168,128]{2,1,0:T(8,128)(2,1)} fusion(bf16[256,7168]{1,0:T(8,128)(2,1)} %copy-done.3, bf16[7168,128]{1,0:T(8,128)(2,1)S(1)} %collective-permute-done.24, bf16[256,256]{1,0:T(8,128)(2,1)S(1)} %get-tuple-element.87), kind=kOutput, calls=%fused_computation.14 | convolution fusion | flops 472514560 | bytes 7405568 | tf_op jit(solution)/shard_map/rd,rf->df/dot_general | solution.py:178
  179.7 4.6 %fusion.3 = bf16[1,128,7168]{2,1,0:T(8,128)(2,1)} fusion(bf16[256,7168]{1,0:T(8,128)(2,1)} %slice_dynamic-update-slice_fusion, bf16[128,7168]{1,0:T(8,128)(2,1)} %collective-permute-done.25, bf16[256,256]{1,0:T(8,128)(2,1)S(1)} %get-tuple-element.88), kind=kOutput, calls=%fused_computation.13 | convolution fusion | flops 472514560 | bytes 7405568 | tf_op jit(solution)/shard_map/rd,rf->df/dot_general | solution.py:178
  184.3 2.9 %convolution_convert_fusion.6 = bf16[128,7168]{1,0:T(8,128)(2,1)} fusion(f32[128,64]{0,1:T(8,128)S(1)} %bitcast.47, bf16[64,7168]{1,0:T(8,128)(2,1)S(1)} %copy-done.6), kind=kOutput, calls=%fused_computation.12 | convolution fusion | flops 705560576 | bytes 2785280 | tf_op jit(solution)/shard_map/dot_general | solution.py:187
  187.2 3.4 %all-to-all-done.3 = bf16[16,4,7168]{2,1,0:T(4,128)(2,1)S(1)} async-done(((bf16[16,4,7168]{2,1,0:T(4,128)(2,1)}), bf16[16,4,7168]{2,1,0:T(4,128)(2,1)S(1)}, u32[]{:S(2)}, u32[]{:S(2)}) %all-to-all-start.3) | async-done | bytes 917536 | tf_op jit(solution)/shard_map/all_to_all | solution.py:102
  191.8 3.1 %convolution_convert_fusion.5 = bf16[128,7168]{1,0:T(8,128)(2,1)} fusion(bf16[128,64]{0,1:T(8,128)(2,1)S(1)} %bitcast.48, bf16[64,7168]{1,0:T(8,128)(2,1)} %reshape.138), kind=kOutput, calls=%fused_computation.11 | convolution fusion | flops 118358016 | bytes 2768896 | tf_op jit(solution)/shard_map/dot_general | solution.py:190
  (143 shorter events, 57.5 us)
Async XLA Ops:
  0.7 59.7 %collective-permute-start.6 = (bf16[7168,128]{1,0:T(8,128)(2,1)}, bf16[7168,128]{1,0:T(8,128)(2,1)}, u32[]{:S(2)}, u32[]{:S(2)}) collective-permute-start(bf16[7168,128]{1,0:T(8,128)(2,1)} %bitcast.43), channel_id=1, source_target_pairs={{0,1},{1,0},{2,3},{3,2},{4,5},{5,4},{6,7},{7,6},{8,9},{9,8},{10,11... | collective-permute-start | bytes 5505032 | tf_op jit(solution)/shard_map/ppermute | solution.py:124
  0.8 62.0 %collective-permute-start.7 = (bf16[7168,128]{1,0:T(8,128)(2,1)}, bf16[7168,128]{1,0:T(8,128)(2,1)}, u32[]{:S(2)}, u32[]{:S(2)}) collective-permute-start(bf16[7168,128]{1,0:T(8,128)(2,1)} %bitcast.41), channel_id=1, source_target_pairs={{0,1},{1,0},{2,3},{3,2},{4,5},{5,4},{6,7},{7,6},{8,9},{9,8},{10,11... | collective-permute-start | bytes 5505032 | tf_op jit(solution)/shard_map/ppermute | solution.py:125
  1.3 62.6 %collective-permute-start.8 = (bf16[128,7168]{1,0:T(8,128)(2,1)}, bf16[128,7168]{1,0:T(8,128)(2,1)}, u32[]{:S(2)}, u32[]{:S(2)}) collective-permute-start(bf16[128,7168]{1,0:T(8,128)(2,1)} %bitcast.45), channel_id=1, source_target_pairs={{0,1},{1,0},{2,3},{3,2},{4,5},{5,4},{6,7},{7,6},{8,9},{9,8},{10,11... | collective-permute-start | bytes 5505032 | tf_op jit(solution)/shard_map/ppermute | solution.py:126
  4.1 22.8 %all-to-all-start = ((bf16[16,4,7168]{2,1,0:T(4,128)(2,1)}), bf16[16,4,7168]{2,1,0:T(4,128)(2,1)S(1)}, u32[]{:S(2)}, u32[]{:S(2)}) async-start(bf16[16,4,7168]{2,1,0:T(4,128)(2,1)} %bitcast.7), calls=%async_computation | async-start | bytes 1835008 | tf_op jit(solution)/shard_map/all_to_all | solution.py:95
  29.2 18.5 %collective-permute-start = (bf16[48,7168]{1,0:T(8,128)(2,1)}, bf16[48,7168]{1,0:T(8,128)(2,1)S(1)}, u32[]{:S(2)}, u32[]{:S(2)}) collective-permute-start(bf16[48,7168]{1,0:T(8,128)(2,1)} %constant_dynamic-update-slice_fusion), channel_id=1, source_target_pairs={{0,2},{2,4},{4,6},{6,0},{1,3},{3,5},{5,7},{7,1},{8,10},{10,12},{12... | collective-permute-start | bytes 2064392 | tf_op jit(solution)/shard_map/ppermute | solution.py:27
  31.1 17.4 %collective-permute-start.1 = (bf16[48,7168]{1,0:T(8,128)(2,1)}, bf16[48,7168]{1,0:T(8,128)(2,1)}, u32[]{:S(2)}, u32[]{:S(2)}) collective-permute-start(bf16[48,7168]{1,0:T(8,128)(2,1)} %constant_dynamic-update-slice_fusion), channel_id=1, source_target_pairs={{0,6},{2,0},{4,2},{6,4},{1,7},{3,1},{5,3},{7,5},{8,14},{10,8},{12,... | collective-permute-start | bytes 2064392 | tf_op jit(solution)/shard_map/ppermute | solution.py:27
  34.5 20.7 %all-to-all-start.1 = ((bf16[16,4,7168]{2,1,0:T(4,128)(2,1)}), bf16[16,4,7168]{2,1,0:T(4,128)(2,1)S(1)}, u32[]{:S(2)}, u32[]{:S(2)}) async-start(bf16[16,4,7168]{2,1,0:T(4,128)(2,1)} %bitcast.40), calls=%async_computation.1 | async-start | bytes 1835008 | tf_op jit(solution)/shard_map/all_to_all | solution.py:95
  50.2 14.6 %collective-permute-start.9 = (bf16[24,7168]{1,0:T(8,128)(2,1)}, bf16[24,7168]{1,0:T(8,128)(2,1)S(1)}, u32[]{:S(2)}, u32[]{:S(2)}) collective-permute-start(bf16[24,7168]{1,0:T(8,128)(2,1)} %slice.258), channel_id=1, source_target_pairs={{0,2},{2,4},{4,6},{6,0},{1,3},{3,5},{5,7},{7,1},{8,10},{10,12},{12... | collective-permute-start | bytes 1032200 | tf_op jit(solution)/shard_map/ppermute | solution.py:36
  50.8 14.0 %collective-permute-start.10 = (bf16[24,7168]{1,0:T(8,128)(2,1)}, bf16[24,7168]{1,0:T(8,128)(2,1)}, u32[]{:S(2)}, u32[]{:S(2)}) collective-permute-start(bf16[24,7168]{1,0:T(8,128)(2,1)} %slice.259), channel_id=1, source_target_pairs={{0,6},{2,0},{4,2},{6,4},{1,7},{3,1},{5,3},{7,5},{8,14},{10,8},{12,... | collective-permute-start | bytes 1032200 | tf_op jit(solution)/shard_map/ppermute | solution.py:36
  60.4 12.4 %collective-permute-start.5 = (bf16[32,7168]{1,0:T(8,128)(2,1)}, bf16[32,7168]{1,0:T(8,128)(2,1)S(1)}, u32[]{:S(2)}, u32[]{:S(2)}) collective-permute-start(bf16[32,7168]{1,0:T(8,128)(2,1)} %pad_maximum_fusion.9), channel_id=1, source_target_pairs={{0,8},{8,0},{1,9},{9,1},{2,10},{10,2},{3,11},{11,3},{4,12},{12,4},... | collective-permute-start | bytes 1376264 | tf_op jit(solution)/shard_map/ppermute | solution.py:40
  62.8 20.0 %collective-permute-start.2 = (bf16[48,7168]{1,0:T(8,128)(2,1)S(1)}, bf16[48,7168]{1,0:T(8,128)(2,1)S(1)}, u32[]{:S(2)}, u32[]{:S(2)}) collective-permute-start(bf16[48,7168]{1,0:T(8,128)(2,1)S(1)} %pad_maximum_fusion.5), channel_id=1, source_target_pairs={{0,6},{2,0},{4,2},{6,4},{1,7},{3,1},{5,3},{7,5},{8,14},{10,8},{12,... | collective-permute-start | bytes 2064392 | tf_op jit(solution)/shard_map/ppermute | solution.py:27
  63.9 18.9 %collective-permute-start.3 = (bf16[48,7168]{1,0:T(8,128)(2,1)S(1)}, bf16[48,7168]{1,0:T(8,128)(2,1)S(1)}, u32[]{:S(2)}, u32[]{:S(2)}) collective-permute-start(bf16[48,7168]{1,0:T(8,128)(2,1)S(1)} %pad_maximum_fusion.5), channel_id=1, source_target_pairs={{0,2},{2,4},{4,6},{6,0},{1,3},{3,5},{5,7},{7,1},{8,10},{10,12},{12... | collective-permute-start | bytes 2064392 | tf_op jit(solution)/shard_map/ppermute | solution.py:27
  70.7 7.6 %collective-permute-start.11 = (bf16[16,7168]{1,0:T(8,128)(2,1)S(1)}, bf16[16,7168]{1,0:T(8,128)(2,1)S(1)}, u32[]{:S(2)}, u32[]{:S(2)}) collective-permute-start(bf16[16,7168]{1,0:T(8,128)(2,1)S(1)} %slice.260), channel_id=1, source_target_pairs={{0,8},{8,0},{1,9},{9,1},{2,10},{10,2},{3,11},{11,3},{4,12},{12,4},... | collective-permute-start | bytes 688136 | tf_op jit(solution)/shard_map/ppermute | solution.py:40
  78.4 46.3 %copy-start.3 = (bf16[256,7168]{1,0:T(8,128)(2,1)}, bf16[256,7168]{1,0:T(8,128)(2,1)S(1)}, u32[]{:S(2)}) copy-start(bf16[256,7168]{1,0:T(8,128)(2,1)S(1)} %slice_dynamic-update-slice_fusion.1) | copy-start | bytes 11010052
  82.9 15.7 %collective-permute-start.4 = (bf16[32,7168]{1,0:T(8,128)(2,1)S(1)}, bf16[32,7168]{1,0:T(8,128)(2,1)S(1)}, u32[]{:S(2)}, u32[]{:S(2)}) collective-permute-start(bf16[32,7168]{1,0:T(8,128)(2,1)S(1)} %pad_maximum_fusion.8), channel_id=1, source_target_pairs={{0,8},{8,0},{1,9},{9,1},{2,10},{10,2},{3,11},{11,3},{4,12},{12,4},... | collective-permute-start | bytes 1376264 | tf_op jit(solution)/shard_map/ppermute | solution.py:40
  84.3 8.9 %collective-permute-start.12 = (bf16[24,7168]{1,0:T(8,128)(2,1)S(1)}, bf16[24,7168]{1,0:T(8,128)(2,1)S(1)}, u32[]{:S(2)}, u32[]{:S(2)}) collective-permute-start(bf16[24,7168]{1,0:T(8,128)(2,1)S(1)} %slice.266), channel_id=1, source_target_pairs={{0,2},{2,4},{4,6},{6,0},{1,3},{3,5},{5,7},{7,1},{8,10},{10,12},{12... | collective-permute-start | bytes 1032200 | tf_op jit(solution)/shard_map/ppermute | solution.py:36
  84.6 8.7 %collective-permute-start.13 = (bf16[24,7168]{1,0:T(8,128)(2,1)S(1)}, bf16[24,7168]{1,0:T(8,128)(2,1)S(1)}, u32[]{:S(2)}, u32[]{:S(2)}) collective-permute-start(bf16[24,7168]{1,0:T(8,128)(2,1)S(1)} %slice.267), channel_id=1, source_target_pairs={{0,6},{2,0},{4,2},{6,4},{1,7},{3,1},{5,3},{7,5},{8,14},{10,8},{12,... | collective-permute-start | bytes 1032200 | tf_op jit(solution)/shard_map/ppermute | solution.py:36
  93.3 7.6 %collective-permute-start.14 = (bf16[16,7168]{1,0:T(8,128)(2,1)S(1)}, bf16[16,7168]{1,0:T(8,128)(2,1)S(1)}, u32[]{:S(2)}, u32[]{:S(2)}) collective-permute-start(bf16[16,7168]{1,0:T(8,128)(2,1)S(1)} %slice.268), channel_id=1, source_target_pairs={{0,8},{8,0},{1,9},{9,1},{2,10},{10,2},{3,11},{11,3},{4,12},{12,4},... | collective-permute-start | bytes 688136 | tf_op jit(solution)/shard_map/ppermute | solution.py:40
  95.4 17.5 %collective-permute-start.16 = (bf16[64,7168]{1,0:T(8,128)(2,1)}, bf16[64,7168]{1,0:T(8,128)(2,1)}, u32[]{:S(2)}, u32[]{:S(2)}) collective-permute-start(bf16[64,7168]{1,0:T(8,128)(2,1)} %get-tuple-element.72), channel_id=1, source_target_pairs={{0,6},{2,0},{4,2},{6,4},{1,7},{3,1},{5,3},{7,5},{8,14},{10,8},{12,... | collective-permute-start | bytes 2752520 | tf_op jit(solution)/shard_map/ppermute | solution.py:36
  98.6 19.1 %collective-permute-start.15 = (bf16[64,7168]{1,0:T(8,128)(2,1)S(1)}, bf16[64,7168]{1,0:T(8,128)(2,1)}, u32[]{:S(2)}, u32[]{:S(2)}) collective-permute-start(bf16[64,7168]{1,0:T(8,128)(2,1)S(1)} %get-tuple-element.71), channel_id=1, source_target_pairs={{0,2},{2,4},{4,6},{6,0},{1,3},{3,5},{5,7},{7,1},{8,10},{10,12},{12... | collective-permute-start | bytes 2752520 | tf_op jit(solution)/shard_map/ppermute | solution.py:36
  108.5 16.2 %copy-start.5 = (bf16[256,7168]{1,0:T(8,128)(2,1)}, bf16[256,7168]{1,0:T(8,128)(2,1)S(1)}, u32[]{:S(2)}) copy-start(bf16[256,7168]{1,0:T(8,128)(2,1)S(1)} %convolution_convert_fusion) | copy-start | bytes 11010052
  119.0 9.8 %collective-permute-start.19 = (bf16[32,7168]{1,0:T(8,128)(2,1)S(1)}, bf16[32,7168]{1,0:T(8,128)(2,1)S(1)}, u32[]{:S(2)}, u32[]{:S(2)}) collective-permute-start(bf16[32,7168]{1,0:T(8,128)(2,1)S(1)} %get-tuple-element.78), channel_id=1, source_target_pairs={{0,2},{2,4},{4,6},{6,0},{1,3},{3,5},{5,7},{7,1},{8,10},{10,12},{12... | collective-permute-start | bytes 1376264 | tf_op jit(solution)/shard_map/ppermute | solution.py:36
  119.1 10.6 %collective-permute-start.20 = (bf16[32,7168]{1,0:T(8,128)(2,1)S(1)}, bf16[32,7168]{1,0:T(8,128)(2,1)S(1)}, u32[]{:S(2)}, u32[]{:S(2)}) collective-permute-start(bf16[32,7168]{1,0:T(8,128)(2,1)S(1)} %get-tuple-element.80), channel_id=1, source_target_pairs={{0,6},{2,0},{4,2},{6,4},{1,7},{3,1},{5,3},{7,5},{8,14},{10,8},{12,... | collective-permute-start | bytes 1376264 | tf_op jit(solution)/shard_map/ppermute | solution.py:36
  124.8 37.7 %collective-permute-start.23 = (bf16[7168,128]{1,0:T(8,128)(2,1)}, bf16[7168,128]{1,0:T(8,128)(2,1)}, u32[]{:S(2)}, u32[]{:S(2)}) collective-permute-start(bf16[7168,128]{1,0:T(8,128)(2,1)} %convolution_convert_fusion.4), channel_id=1, source_target_pairs={{0,1},{1,0},{2,3},{3,2},{4,5},{5,4},{6,7},{7,6},{8,9},{9,8},{10,11... | collective-permute-start | bytes 5505032 | tf_op jit(solution)/shard_map/ppermute | solution.py:179
  127.2 48.1 %collective-permute-start.24 = (bf16[7168,128]{1,0:T(8,128)(2,1)}, bf16[7168,128]{1,0:T(8,128)(2,1)S(1)}, u32[]{:S(2)}, u32[]{:S(2)}) collective-permute-start(bf16[7168,128]{1,0:T(8,128)(2,1)} %convolution_convert_fusion.3), channel_id=1, source_target_pairs={{0,1},{1,0},{2,3},{3,2},{4,5},{5,4},{6,7},{7,6},{8,9},{9,8},{10,11... | collective-permute-start | bytes 5505032 | tf_op jit(solution)/shard_map/ppermute | solution.py:180
  127.7 22.6 %collective-permute-start.18 = (bf16[64,7168]{1,0:T(8,128)(2,1)}, bf16[64,7168]{1,0:T(8,128)(2,1)}, u32[]{:S(2)}, u32[]{:S(2)}) collective-permute-start(bf16[64,7168]{1,0:T(8,128)(2,1)} %get-tuple-element.76), channel_id=1, source_target_pairs={{0,6},{2,0},{4,2},{6,4},{1,7},{3,1},{5,3},{7,5},{8,14},{10,8},{12,... | collective-permute-start | bytes 2752520 | tf_op jit(solution)/shard_map/ppermute | solution.py:36
  128.8 22.7 %collective-permute-start.17 = (bf16[64,7168]{1,0:T(8,128)(2,1)}, bf16[64,7168]{1,0:T(8,128)(2,1)}, u32[]{:S(2)}, u32[]{:S(2)}) collective-permute-start(bf16[64,7168]{1,0:T(8,128)(2,1)} %get-tuple-element.75), channel_id=1, source_target_pairs={{0,2},{2,4},{4,6},{6,0},{1,3},{3,5},{5,7},{7,1},{8,10},{10,12},{12... | collective-permute-start | bytes 2752520 | tf_op jit(solution)/shard_map/ppermute | solution.py:36
  132.7 21.4 %all-to-all-start.2 = ((bf16[16,4,7168]{2,1,0:T(4,128)(2,1)}), bf16[16,4,7168]{2,1,0:T(4,128)(2,1)S(1)}, u32[]{:S(2)}, u32[]{:S(2)}) async-start(bf16[16,4,7168]{2,1,0:T(4,128)(2,1)} %reshape.134), calls=%async_computation.2 | async-start | bytes 1835008 | tf_op jit(solution)/shard_map/all_to_all | solution.py:102
  155.3 11.9 %collective-permute-start.21 = (bf16[32,7168]{1,0:T(8,128)(2,1)}, bf16[32,7168]{1,0:T(8,128)(2,1)S(1)}, u32[]{:S(2)}, u32[]{:S(2)}) collective-permute-start(bf16[32,7168]{1,0:T(8,128)(2,1)} %get-tuple-element.83), channel_id=1, source_target_pairs={{0,2},{2,4},{4,6},{6,0},{1,3},{3,5},{5,7},{7,1},{8,10},{10,12},{12... | collective-permute-start | bytes 1376264 | tf_op jit(solution)/shard_map/ppermute | solution.py:36
  155.7 11.4 %collective-permute-start.22 = (bf16[32,7168]{1,0:T(8,128)(2,1)}, bf16[32,7168]{1,0:T(8,128)(2,1)S(1)}, u32[]{:S(2)}, u32[]{:S(2)}) collective-permute-start(bf16[32,7168]{1,0:T(8,128)(2,1)} %get-tuple-element.85), channel_id=1, source_target_pairs={{0,6},{2,0},{4,2},{6,4},{1,7},{3,1},{5,3},{7,5},{8,14},{10,8},{12,... | collective-permute-start | bytes 1376264 | tf_op jit(solution)/shard_map/ppermute | solution.py:36
  162.4 17.3 %collective-permute-start.25 = (bf16[128,7168]{1,0:T(8,128)(2,1)}, bf16[128,7168]{1,0:T(8,128)(2,1)}, u32[]{:S(2)}, u32[]{:S(2)}) collective-permute-start(bf16[128,7168]{1,0:T(8,128)(2,1)} %convolution_convert_fusion.2), channel_id=1, source_target_pairs={{0,1},{1,0},{2,3},{3,2},{4,5},{5,4},{6,7},{7,6},{8,9},{9,8},{10,11... | collective-permute-start | bytes 5505032 | tf_op jit(solution)/shard_map/ppermute | solution.py:181
  170.4 20.1 %all-to-all-start.3 = ((bf16[16,4,7168]{2,1,0:T(4,128)(2,1)}), bf16[16,4,7168]{2,1,0:T(4,128)(2,1)S(1)}, u32[]{:S(2)}, u32[]{:S(2)}) async-start(bf16[16,4,7168]{2,1,0:T(4,128)(2,1)} %reshape.137), calls=%async_computation.3 | async-start | bytes 1835008 | tf_op jit(solution)/shard_map/all_to_all | solution.py:102
  (8 other events, 57.7 us)

commit v3 on v2

--- a/solution.py
+++ b/solution.py
@@ -162,6 +162,13 @@
     slope = logistic * (1.0 + gate_pre * (1.0 - logistic))
     gate_grad = (hidden_grad * up_pre * slope).astype(BF16)
     up_grad = (hidden_grad * gate_pre * logistic).astype(BF16)
+    late = lambda a, b: jnp.einsum("rd,rf->df", a, b, preferred_element_type=F32)
+    gate_part = late(rows_x, gate_grad[:, half:]).astype(BF16)
+    up_part = late(rows_x, up_grad[:, half:]).astype(BF16)
+    out_part = late(hidden[:, half:], rows_d).astype(BF16)
+    gate_grad, up_grad, gate_part, up_part, out_part = tie(
+        gate_grad, up_grad, gate_part, up_part, out_part
+    )
     both = jnp.concatenate([gate_grad, up_grad], axis=1)
     q_part = jnp.einsum("rf,df->rd", both, w_in, preferred_element_type=F32).astype(BF16)
     y_up, y_down, *y_1 = tie(*scatter_far(y_part, *y_1), *y_1)
@@ -174,11 +181,9 @@
     q_2 = far_z(q_up, q_down)
     q_rows = scatter_out(q_part, *q_1, *q_2)
 
-    gate_grad, up_grad, hidden, q_part = tie(gate_grad, up_grad, hidden, q_part)
-    late = lambda a, b: jnp.einsum("rd,rf->df", a, b, preferred_element_type=F32)
-    gate_got = lax.ppermute(late(rows_x, gate_grad[:, half:]).astype(BF16), "core", SWAP)
-    up_got = lax.ppermute(late(rows_x, up_grad[:, half:]).astype(BF16), "core", SWAP)
-    out_got = lax.ppermute(late(hidden[:, half:], rows_d).astype(BF16), "core", SWAP)
+    gate_got = lax.ppermute(gate_part, "core", SWAP)
+    up_got = lax.ppermute(up_part, "core", SWAP)
+    out_got = lax.ppermute(out_part, "core", SWAP)
     grad_gate = add(late(rows_x, gate_grad[:, :half]), gate_got)
     grad_up = add(late(rows_x, up_grad[:, :half]), up_got)
     grad_down = add(late(hidden[:, :half], rows_d), out_got)

time: 196 us -> 191 us (0.974)
  waiting for transfers between devices: 58.5 us -> 51.7 us
  starting transfers between devices: 52.3 us -> 55.9 us
  other arithmetic: 16.6 us -> 14.4 us
    ppermute x12, waiting for transfers between devices: 28 us -> 25.4 us  [far_z(): return (lax.ppermute(low, 'z', z_by(1)), lax.ppermute(high, 'z', z_by(3)))]
    convert_element_type x4, other arithmetic: 7.24 us -> 4.9 us  [add(): return sum((t.astype(F32) for t in terms)).astype(BF16)]
    unnamed x37 -> x35, local copies, waits for them, and re-layouts: 11.9 us -> 12.3 us
  transfers between devices with their start and end apart: 30 -> 30, of which waited for: 13 -> 11; matrix products, arithmetic and copies ran while one was open for 40% -> 39% of each run, Pallas kernels for 0% -> 0%
where the time goes in v3:
time: 191 us; the launch traced here: 190 us
  starting transfers between devices  55.9 us (29%)
  waiting for transfers between devices  51.7 us (27%)
  matrix products  39.6 us (21%)
  local copies, waits for them, and re-layouts  27 us (14%)
  other arithmetic  14.4 us (8%)
    ppermute x12, waiting for transfers between devices, far_z(): return (lax.ppermute(low, 'z', z_by(1)), lax.ppermute(high, 'z', z_by(3)))  25.4 us
    dot_general x6, matrix products, local(): jnp.einsum('rd,rf->df', a, b, preferred_element_type=F32)  22.8 us
    ppermute x12, starting transfers between devices, far_z(): return (lax.ppermute(low, 'z', z_by(1)), lax.ppermute(high, 'z', z_by(3)))  18.9 us
    all_to_all x2, waiting for transfers between devices, move_plane(): lax.all_to_all(twice, PLANE, split_axis=0, concat_axis=0, tiled=True)  12.4 us
    unnamed x35, local copies, waits for them, and re-layouts  12.3 us
    all_to_all x2, starting transfers between devices, to_slots(): back = lax.all_to_all(sent, PLANE, split_axis=0, concat_axis=0, tiled=True)  11.3 us
    all_to_all x2, starting transfers between devices, move_plane(): lax.all_to_all(twice, PLANE, split_axis=0, concat_axis=0, tiled=True)  11 us
    ppermute x4, starting transfers between devices, across(): return lax.ppermute(rows, 'xh', SWAP)  7.25 us
  transfers between devices with their start and end apart: 30, of which 11 were waited for; matrix products, arithmetic and copies ran while one was open for 39% of the time, Pallas kernels for 0%

profile of v3, /device:TPU:0, one launch (start us, length us, event | category | flops | bytes accessed | tf_op | source)
XLA Modules:
  0.0 189.8 jit_solution(7245132366802913529)
XLA Ops:
  3.9 7.1 %all-to-all-start = ((bf16[16,4,7168]{2,1,0:T(4,128)(2,1)}), bf16[16,4,7168]{2,1,0:T(4,128)(2,1)S(1)}, u32[]{:S(2)}, u32[]{:S(2)}) async-start(bf16[16,4,7168]{2,1,0:T(4,128)(2,1)} %bitcast.7), calls=%async_computation | async-start | bytes 1835008 | tf_op jit(solution)/shard_map/all_to_all | solution.py:95
  14.0 12.4 %all-to-all-done = bf16[16,4,7168]{2,1,0:T(4,128)(2,1)S(1)} async-done(((bf16[16,4,7168]{2,1,0:T(4,128)(2,1)}), bf16[16,4,7168]{2,1,0:T(4,128)(2,1)S(1)}, u32[]{:S(2)}, u32[]{:S(2)}) %all-to-all-start) | async-done | bytes 917536 | tf_op jit(solution)/shard_map/all_to_all | solution.py:95
  30.5 2.1 %collective-permute-start.1 = (bf16[48,7168]{1,0:T(8,128)(2,1)}, bf16[48,7168]{1,0:T(8,128)(2,1)}, u32[]{:S(2)}, u32[]{:S(2)}) collective-permute-start(bf16[48,7168]{1,0:T(8,128)(2,1)} %constant_dynamic-update-slice_fusion), channel_id=1, source_target_pairs={{0,6},{2,0},{4,2},{6,4},{1,7},{3,1},{5,3},{7,5},{8,14},{10,8},{12,... | collective-permute-start | bytes 2064392 | tf_op jit(solution)/shard_map/ppermute | solution.py:27
  33.9 3.9 %all-to-all-start.1 = ((bf16[16,4,7168]{2,1,0:T(4,128)(2,1)}), bf16[16,4,7168]{2,1,0:T(4,128)(2,1)S(1)}, u32[]{:S(2)}, u32[]{:S(2)}) async-start(bf16[16,4,7168]{2,1,0:T(4,128)(2,1)} %bitcast.40), calls=%async_computation.1 | async-start | bytes 1835008 | tf_op jit(solution)/shard_map/all_to_all | solution.py:95
  38.9 7.1 %collective-permute-done = bf16[48,7168]{1,0:T(8,128)(2,1)S(1)} collective-permute-done((bf16[48,7168]{1,0:T(8,128)(2,1)}, bf16[48,7168]{1,0:T(8,128)(2,1)S(1)}, u32[]{:S(2)}, u32[]{:S(2)}) %collective-permute-start) | collective-permute-done | bytes 688160 | tf_op jit(solution)/shard_map/ppermute | solution.py:27
  49.1 2.6 %collective-permute-start.10 = (bf16[24,7168]{1,0:T(8,128)(2,1)}, bf16[24,7168]{1,0:T(8,128)(2,1)}, u32[]{:S(2)}, u32[]{:S(2)}) collective-permute-start(bf16[24,7168]{1,0:T(8,128)(2,1)} %slice.259), channel_id=1, source_target_pairs={{0,6},{2,0},{4,2},{6,4},{1,7},{3,1},{5,3},{7,5},{8,14},{10,8},{12,... | collective-permute-start | bytes 1032200 | tf_op jit(solution)/shard_map/ppermute | solution.py:36
  58.7 2.2 %collective-permute-start.5 = (bf16[32,7168]{1,0:T(8,128)(2,1)}, bf16[32,7168]{1,0:T(8,128)(2,1)S(1)}, u32[]{:S(2)}, u32[]{:S(2)}) collective-permute-start(bf16[32,7168]{1,0:T(8,128)(2,1)} %pad_maximum_fusion.9), channel_id=1, source_target_pairs={{0,8},{8,0},{1,9},{9,1},{2,10},{10,2},{3,11},{11,3},{4,12},{12,4},... | collective-permute-start | bytes 1376264 | tf_op jit(solution)/shard_map/ppermute | solution.py:40
  63.0 4.0 %pad_maximum_fusion = bf16[7168,512]{1,0:T(8,128)(2,1)S(1)} fusion(bf16[7168,128]{1,0:T(8,128)(2,1)} %collective-permute-done.7, bf16[7168,128]{1,0:T(8,128)(2,1)} %bitcast.42, bf16[7168,128]{1,0:T(8,128)(2,1)} %collective-permute-done.6, bf16[7168,128]{1,0:T(8,128)(2,1)} %bitcast.44), kind=kLoop, calls=%fused_computation.19 | loop fusion | flops 29360128 | bytes 14680064 | tf_op jit(solution)/shard_map/concatenate | solution.py:141
  71.4 5.1 %collective-permute-done.11 = bf16[16,7168]{1,0:T(8,128)(2,1)S(1)} collective-permute-done((bf16[16,7168]{1,0:T(8,128)(2,1)S(1)}, bf16[16,7168]{1,0:T(8,128)(2,1)S(1)}, u32[]{:S(2)}, u32[]{:S(2)}) %collective-permute-start.11) | collective-permute-done | bytes 229408 | tf_op jit(solution)/shard_map/ppermute | solution.py:40
  81.8 3.2 %collective-permute-start.13 = (bf16[24,7168]{1,0:T(8,128)(2,1)S(1)}, bf16[24,7168]{1,0:T(8,128)(2,1)S(1)}, u32[]{:S(2)}, u32[]{:S(2)}) collective-permute-start(bf16[24,7168]{1,0:T(8,128)(2,1)S(1)} %slice.267), channel_id=1, source_target_pairs={{0,6},{2,0},{4,2},{6,4},{1,7},{3,1},{5,3},{7,5},{8,14},{10,8},{12,... | collective-permute-start | bytes 1032200 | tf_op jit(solution)/shard_map/ppermute | solution.py:36
  86.0 4.3 %collective-permute-done.12 = bf16[24,7168]{1,0:T(8,128)(2,1)S(1)} collective-permute-done((bf16[24,7168]{1,0:T(8,128)(2,1)S(1)}, bf16[24,7168]{1,0:T(8,128)(2,1)S(1)}, u32[]{:S(2)}, u32[]{:S(2)}) %collective-permute-start.12) | collective-permute-done | bytes 344096 | tf_op jit(solution)/shard_map/ppermute | solution.py:36
  90.4 2.3 %collective-permute-start.14 = (bf16[16,7168]{1,0:T(8,128)(2,1)S(1)}, bf16[16,7168]{1,0:T(8,128)(2,1)S(1)}, u32[]{:S(2)}, u32[]{:S(2)}) collective-permute-start(bf16[16,7168]{1,0:T(8,128)(2,1)S(1)} %slice.268), channel_id=1, source_target_pairs={{0,8},{8,0},{1,9},{9,1},{2,10},{10,2},{3,11},{11,3},{4,12},{12,4},... | collective-permute-start | bytes 688136 | tf_op jit(solution)/shard_map/ppermute | solution.py:40
  92.6 3.2 %collective-permute-start.16 = (bf16[64,7168]{1,0:T(8,128)(2,1)S(1)}, bf16[64,7168]{1,0:T(8,128)(2,1)S(1)}, u32[]{:S(2)}, u32[]{:S(2)}) collective-permute-start(bf16[64,7168]{1,0:T(8,128)(2,1)S(1)} %get-tuple-element.76), channel_id=1, source_target_pairs={{0,6},{2,0},{4,2},{6,4},{1,7},{3,1},{5,3},{7,5},{8,14},{10,8},{12,... | collective-permute-start | bytes 2752520 | tf_op jit(solution)/shard_map/ppermute | solution.py:36
  100.4 3.9 %convolution_convert_fusion.4 = bf16[128,7168]{1,0:T(8,128)(2,1)} fusion(bf16[256,7168]{1,0:T(8,128)(2,1)} %slice_dynamic-update-slice_fusion, bf16[256,256]{1,0:T(8,128)(2,1)S(1)} %get-tuple-element.65), kind=kOutput, calls=%fused_computation.10 | convolution fusion | flops 470679552 | bytes 5570560 | tf_op jit(solution)/shard_map/rd,rf->df/dot_general | solution.py:165
  104.4 3.2 %multiply_convert_fusion = (bf16[256,256]{1,0:T(8,128)(2,1)S(1)}, bf16[256,256]{1,0:T(8,128)(2,1)S(1)}) fusion(f32[256,256]{1,0:T(8,128)S(1)} %get-tuple-element.72, f32[256,256]{1,0:T(8,128)S(1)} %get-tuple-element.71, bf16[256,7168]{1,0:T(8,128)(2,1)} %slice_dynamic-update-slice_fusion, bf16[256,7168]{1,0:T(8,128)(2,1)S(1)} %pad_maximum_fusion.1), kind=kOutput, calls=%fused_computation.50 | convolution fusion | flops 940376064 | bytes 8126464 | tf_op jit(solution)/shard_map/rd,fd->rf/dot_general | solution.py:160
  107.6 2.4 %convolution_convert_fusion.6 = bf16[7168,128]{1,0:T(8,128)(2,1)} fusion(bf16[256,7168]{1,0:T(8,128)(2,1)S(1)} %slice_dynamic-update-slice_fusion.1, bf16[256,256]{1,0:T(8,128)(2,1)S(1)} %get-tuple-element.73), kind=kOutput, calls=%fused_computation.12 | convolution fusion | flops 470679552 | bytes 5570560 | tf_op jit(solution)/shard_map/rd,rf->df/dot_general | solution.py:165
  110.0 2.4 %convolution_convert_fusion.5 = bf16[7168,128]{1,0:T(8,128)(2,1)} fusion(bf16[256,7168]{1,0:T(8,128)(2,1)S(1)} %slice_dynamic-update-slice_fusion.1, bf16[256,256]{1,0:T(8,128)(2,1)S(1)} %get-tuple-element.74), kind=kOutput, calls=%fused_computation.11 | convolution fusion | flops 470679552 | bytes 5570560 | tf_op jit(solution)/shard_map/rd,rf->df/dot_general | solution.py:165
  112.4 2.1 %convolution_convert_fusion = bf16[256,7168]{1,0:T(8,128)(2,1)S(1)} fusion(bf16[7168,512]{1,0:T(8,128)(2,1)S(1)} %pad_maximum_fusion, bf16[256,256]{1,0:T(8,128)(2,1)S(1)} %get-tuple-element.74, bf16[256,256]{1,0:T(8,128)(2,1)S(1)} %get-tuple-element.73), kind=kOutput, calls=%fused_computation | convolution fusion | flops 1881407488 | bytes 11272192 | tf_op jit(solution)/shard_map/rf,df->rd/dot_general | solution.py:173
  114.8 2.2 %collective-permute-start.19 = (bf16[32,7168]{1,0:T(8,128)(2,1)S(1)}, bf16[32,7168]{1,0:T(8,128)(2,1)S(1)}, u32[]{:S(2)}, u32[]{:S(2)}) collective-permute-start(bf16[32,7168]{1,0:T(8,128)(2,1)S(1)} %get-tuple-element.82), channel_id=1, source_target_pairs={{0,2},{2,4},{4,6},{6,0},{1,3},{3,5},{5,7},{7,1},{8,10},{10,12},{12... | collective-permute-start | bytes 1376264 | tf_op jit(solution)/shard_map/ppermute | solution.py:36
  121.9 3.0 %collective-permute-done.19 = bf16[32,7168]{1,0:T(8,128)(2,1)S(1)} collective-permute-done((bf16[32,7168]{1,0:T(8,128)(2,1)S(1)}, bf16[32,7168]{1,0:T(8,128)(2,1)S(1)}, u32[]{:S(2)}, u32[]{:S(2)}) %collective-permute-start.19) | collective-permute-done | bytes 458784 | tf_op jit(solution)/shard_map/ppermute | solution.py:36
  124.8 2.9 %collective-permute-done.20 = bf16[32,7168]{1,0:T(8,128)(2,1)S(1)} collective-permute-done((bf16[32,7168]{1,0:T(8,128)(2,1)S(1)}, bf16[32,7168]{1,0:T(8,128)(2,1)S(1)}, u32[]{:S(2)}, u32[]{:S(2)}) %collective-permute-start.20) | collective-permute-done | bytes 458784 | tf_op jit(solution)/shard_map/ppermute | solution.py:36
  129.6 5.9 %all-to-all-start.2 = ((bf16[16,4,7168]{2,1,0:T(4,128)(2,1)}), bf16[16,4,7168]{2,1,0:T(4,128)(2,1)S(1)}, u32[]{:S(2)}, u32[]{:S(2)}) async-start(bf16[16,4,7168]{2,1,0:T(4,128)(2,1)} %reshape.134), calls=%async_computation.2 | async-start | bytes 1835008 | tf_op jit(solution)/shard_map/all_to_all | solution.py:102
  135.5 9.7 %collective-permute-done.18 = bf16[64,7168]{1,0:T(8,128)(2,1)} collective-permute-done((bf16[64,7168]{1,0:T(8,128)(2,1)}, bf16[64,7168]{1,0:T(8,128)(2,1)}, u32[]{:S(2)}, u32[]{:S(2)}) %collective-permute-start.18) | collective-permute-done | bytes 917536 | tf_op jit(solution)/shard_map/ppermute | solution.py:36
  145.8 2.6 %add_convert_fusion.4 = (bf16[32,7168]{1,0:T(8,128)(2,1)}, bf16[32,7168]{1,0:T(8,128)(2,1)}) fusion(bf16[64,7168]{1,0:T(8,128)(2,1)} %collective-permute-done.18, bf16[256,7168]{1,0:T(8,128)(2,1)} %copy-done.4, bf16[64,7168]{1,0:T(8,128)(2,1)} %collective-permute-done.17), kind=kLoop, calls=%fused_computation.28 | loop fusion | flops 1835008 | bytes 2752512 | tf_op jit(solution)/shard_map/convert_element_type | solution.py:23
  150.6 2.1 %collective-permute-start.22 = (bf16[32,7168]{1,0:T(8,128)(2,1)}, bf16[32,7168]{1,0:T(8,128)(2,1)S(1)}, u32[]{:S(2)}, u32[]{:S(2)}) collective-permute-start(bf16[32,7168]{1,0:T(8,128)(2,1)} %get-tuple-element.89), channel_id=1, source_target_pairs={{0,6},{2,0},{4,2},{6,4},{1,7},{3,1},{5,3},{7,5},{8,14},{10,8},{12,... | collective-permute-start | bytes 1376264 | tf_op jit(solution)/shard_map/ppermute | solution.py:36
  153.4 4.4 %fusion.5 = bf16[1,7168,128]{2,1,0:T(8,128)(2,1)} fusion(bf16[256,7168]{1,0:T(8,128)(2,1)} %copy-done.3, bf16[7168,128]{1,0:T(8,128)(2,1)S(1)} %collective-permute-done.23, bf16[256,256]{1,0:T(8,128)(2,1)S(1)} %get-tuple-element.73), kind=kOutput, calls=%fused_computation.15 | convolution fusion | flops 472514560 | bytes 7405568 | tf_op jit(solution)/shard_map/rd,rf->df/dot_general | solution.py:165
  157.8 5.0 %collective-permute-done.21 = bf16[32,7168]{1,0:T(8,128)(2,1)S(1)} collective-permute-done((bf16[32,7168]{1,0:T(8,128)(2,1)}, bf16[32,7168]{1,0:T(8,128)(2,1)S(1)}, u32[]{:S(2)}, u32[]{:S(2)}) %collective-permute-start.21) | collective-permute-done | bytes 458784 | tf_op jit(solution)/shard_map/ppermute | solution.py:36
  166.1 5.4 %all-to-all-start.3 = ((bf16[16,4,7168]{2,1,0:T(4,128)(2,1)}), bf16[16,4,7168]{2,1,0:T(4,128)(2,1)S(1)}, u32[]{:S(2)}, u32[]{:S(2)}) async-start(bf16[16,4,7168]{2,1,0:T(4,128)(2,1)} %reshape.137), calls=%async_computation.3 | async-start | bytes 1835008 | tf_op jit(solution)/shard_map/all_to_all | solution.py:102
  171.5 5.0 %fusion.4 = bf16[1,7168,128]{2,1,0:T(8,128)(2,1)} fusion(bf16[256,7168]{1,0:T(8,128)(2,1)} %copy-done.3, bf16[7168,128]{1,0:T(8,128)(2,1)} %collective-permute-done.24, bf16[256,256]{1,0:T(8,128)(2,1)S(1)} %get-tuple-element.74), kind=kOutput, calls=%fused_computation.14 | convolution fusion | flops 472514560 | bytes 7405568 | tf_op jit(solution)/shard_map/rd,rf->df/dot_general | solution.py:165
  176.5 4.6 %fusion.3 = bf16[1,128,7168]{2,1,0:T(8,128)(2,1)} fusion(bf16[256,7168]{1,0:T(8,128)(2,1)} %slice_dynamic-update-slice_fusion, bf16[128,7168]{1,0:T(8,128)(2,1)} %collective-permute-done.25, bf16[256,256]{1,0:T(8,128)(2,1)S(1)} %get-tuple-element.65), kind=kOutput, calls=%fused_computation.13 | convolution fusion | flops 472514560 | bytes 7405568 | tf_op jit(solution)/shard_map/rd,rf->df/dot_general | solution.py:165
  181.2 2.9 %convolution_convert_fusion.3 = bf16[128,7168]{1,0:T(8,128)(2,1)} fusion(f32[128,64]{0,1:T(8,128)S(1)} %bitcast.47, bf16[64,7168]{1,0:T(8,128)(2,1)S(1)} %copy-done.5), kind=kOutput, calls=%fused_computation.9 | convolution fusion | flops 705560576 | bytes 2785280 | tf_op jit(solution)/shard_map/dot_general | solution.py:192
  186.7 3.1 %convolution_convert_fusion.2 = bf16[128,7168]{1,0:T(8,128)(2,1)} fusion(bf16[128,64]{0,1:T(8,128)(2,1)S(1)} %bitcast.48, bf16[64,7168]{1,0:T(8,128)(2,1)} %reshape.138), kind=kOutput, calls=%fused_computation.8 | convolution fusion | flops 118358016 | bytes 2768896 | tf_op jit(solution)/shard_map/dot_general | solution.py:195
  (141 shorter events, 56.0 us)
Async XLA Ops:
  3.9 22.5 %all-to-all-start = ((bf16[16,4,7168]{2,1,0:T(4,128)(2,1)}), bf16[16,4,7168]{2,1,0:T(4,128)(2,1)S(1)}, u32[]{:S(2)}, u32[]{:S(2)}) async-start(bf16[16,4,7168]{2,1,0:T(4,128)(2,1)} %bitcast.7), calls=%async_computation | async-start | bytes 1835008 | tf_op jit(solution)/shard_map/all_to_all | solution.py:95
  11.0 47.7 %collective-permute-start.6 = (bf16[7168,128]{1,0:T(8,128)(2,1)}, bf16[7168,128]{1,0:T(8,128)(2,1)}, u32[]{:S(2)}, u32[]{:S(2)}) collective-permute-start(bf16[7168,128]{1,0:T(8,128)(2,1)} %bitcast.43), channel_id=1, source_target_pairs={{0,1},{1,0},{2,3},{3,2},{4,5},{5,4},{6,7},{7,6},{8,9},{9,8},{10,11... | collective-permute-start | bytes 5505032 | tf_op jit(solution)/shard_map/ppermute | solution.py:124
  11.1 49.9 %collective-permute-start.7 = (bf16[7168,128]{1,0:T(8,128)(2,1)}, bf16[7168,128]{1,0:T(8,128)(2,1)}, u32[]{:S(2)}, u32[]{:S(2)}) collective-permute-start(bf16[7168,128]{1,0:T(8,128)(2,1)} %bitcast.41), channel_id=1, source_target_pairs={{0,1},{1,0},{2,3},{3,2},{4,5},{5,4},{6,7},{7,6},{8,9},{9,8},{10,11... | collective-permute-start | bytes 5505032 | tf_op jit(solution)/shard_map/ppermute | solution.py:125
  11.6 50.5 %collective-permute-start.8 = (bf16[128,7168]{1,0:T(8,128)(2,1)}, bf16[128,7168]{1,0:T(8,128)(2,1)}, u32[]{:S(2)}, u32[]{:S(2)}) collective-permute-start(bf16[128,7168]{1,0:T(8,128)(2,1)} %bitcast.45), channel_id=1, source_target_pairs={{0,1},{1,0},{2,3},{3,2},{4,5},{5,4},{6,7},{7,6},{8,9},{9,8},{10,11... | collective-permute-start | bytes 5505032 | tf_op jit(solution)/shard_map/ppermute | solution.py:126
  28.6 17.4 %collective-permute-start = (bf16[48,7168]{1,0:T(8,128)(2,1)}, bf16[48,7168]{1,0:T(8,128)(2,1)S(1)}, u32[]{:S(2)}, u32[]{:S(2)}) collective-permute-start(bf16[48,7168]{1,0:T(8,128)(2,1)} %constant_dynamic-update-slice_fusion), channel_id=1, source_target_pairs={{0,2},{2,4},{4,6},{6,0},{1,3},{3,5},{5,7},{7,1},{8,10},{10,12},{12... | collective-permute-start | bytes 2064392 | tf_op jit(solution)/shard_map/ppermute | solution.py:27
  30.5 16.2 %collective-permute-start.1 = (bf16[48,7168]{1,0:T(8,128)(2,1)}, bf16[48,7168]{1,0:T(8,128)(2,1)}, u32[]{:S(2)}, u32[]{:S(2)}) collective-permute-start(bf16[48,7168]{1,0:T(8,128)(2,1)} %constant_dynamic-update-slice_fusion), channel_id=1, source_target_pairs={{0,6},{2,0},{4,2},{6,4},{1,7},{3,1},{5,3},{7,5},{8,14},{10,8},{12,... | collective-permute-start | bytes 2064392 | tf_op jit(solution)/shard_map/ppermute | solution.py:27
  33.9 19.6 %all-to-all-start.1 = ((bf16[16,4,7168]{2,1,0:T(4,128)(2,1)}), bf16[16,4,7168]{2,1,0:T(4,128)(2,1)S(1)}, u32[]{:S(2)}, u32[]{:S(2)}) async-start(bf16[16,4,7168]{2,1,0:T(4,128)(2,1)} %bitcast.40), calls=%async_computation.1 | async-start | bytes 1835008 | tf_op jit(solution)/shard_map/all_to_all | solution.py:95
  48.5 14.5 %collective-permute-start.9 = (bf16[24,7168]{1,0:T(8,128)(2,1)}, bf16[24,7168]{1,0:T(8,128)(2,1)S(1)}, u32[]{:S(2)}, u32[]{:S(2)}) collective-permute-start(bf16[24,7168]{1,0:T(8,128)(2,1)} %slice.258), channel_id=1, source_target_pairs={{0,2},{2,4},{4,6},{6,0},{1,3},{3,5},{5,7},{7,1},{8,10},{10,12},{12... | collective-permute-start | bytes 1032200 | tf_op jit(solution)/shard_map/ppermute | solution.py:36
  49.1 13.9 %collective-permute-start.10 = (bf16[24,7168]{1,0:T(8,128)(2,1)}, bf16[24,7168]{1,0:T(8,128)(2,1)}, u32[]{:S(2)}, u32[]{:S(2)}) collective-permute-start(bf16[24,7168]{1,0:T(8,128)(2,1)} %slice.259), channel_id=1, source_target_pairs={{0,6},{2,0},{4,2},{6,4},{1,7},{3,1},{5,3},{7,5},{8,14},{10,8},{12,... | collective-permute-start | bytes 1032200 | tf_op jit(solution)/shard_map/ppermute | solution.py:36
  58.7 11.6 %collective-permute-start.5 = (bf16[32,7168]{1,0:T(8,128)(2,1)}, bf16[32,7168]{1,0:T(8,128)(2,1)S(1)}, u32[]{:S(2)}, u32[]{:S(2)}) collective-permute-start(bf16[32,7168]{1,0:T(8,128)(2,1)} %pad_maximum_fusion.9), channel_id=1, source_target_pairs={{0,8},{8,0},{1,9},{9,1},{2,10},{10,2},{3,11},{11,3},{4,12},{12,4},... | collective-permute-start | bytes 1376264 | tf_op jit(solution)/shard_map/ppermute | solution.py:40
  60.9 19.1 %collective-permute-start.2 = (bf16[48,7168]{1,0:T(8,128)(2,1)S(1)}, bf16[48,7168]{1,0:T(8,128)(2,1)S(1)}, u32[]{:S(2)}, u32[]{:S(2)}) collective-permute-start(bf16[48,7168]{1,0:T(8,128)(2,1)S(1)} %pad_maximum_fusion.5), channel_id=1, source_target_pairs={{0,6},{2,0},{4,2},{6,4},{1,7},{3,1},{5,3},{7,5},{8,14},{10,8},{12,... | collective-permute-start | bytes 2064392 | tf_op jit(solution)/shard_map/ppermute | solution.py:27
  62.0 18.0 %collective-permute-start.3 = (bf16[48,7168]{1,0:T(8,128)(2,1)S(1)}, bf16[48,7168]{1,0:T(8,128)(2,1)S(1)}, u32[]{:S(2)}, u32[]{:S(2)}) collective-permute-start(bf16[48,7168]{1,0:T(8,128)(2,1)S(1)} %pad_maximum_fusion.5), channel_id=1, source_target_pairs={{0,2},{2,4},{4,6},{6,0},{1,3},{3,5},{5,7},{7,1},{8,10},{10,12},{12... | collective-permute-start | bytes 2064392 | tf_op jit(solution)/shard_map/ppermute | solution.py:27
  68.9 7.6 %collective-permute-start.11 = (bf16[16,7168]{1,0:T(8,128)(2,1)S(1)}, bf16[16,7168]{1,0:T(8,128)(2,1)S(1)}, u32[]{:S(2)}, u32[]{:S(2)}) collective-permute-start(bf16[16,7168]{1,0:T(8,128)(2,1)S(1)} %slice.260), channel_id=1, source_target_pairs={{0,8},{8,0},{1,9},{9,1},{2,10},{10,2},{3,11},{11,3},{4,12},{12,4},... | collective-permute-start | bytes 688136 | tf_op jit(solution)/shard_map/ppermute | solution.py:40
  76.6 33.4 %copy-start.3 = (bf16[256,7168]{1,0:T(8,128)(2,1)}, bf16[256,7168]{1,0:T(8,128)(2,1)S(1)}, u32[]{:S(2)}) copy-start(bf16[256,7168]{1,0:T(8,128)(2,1)S(1)} %slice_dynamic-update-slice_fusion.1) | copy-start | bytes 11010052
  80.1 15.7 %collective-permute-start.4 = (bf16[32,7168]{1,0:T(8,128)(2,1)S(1)}, bf16[32,7168]{1,0:T(8,128)(2,1)S(1)}, u32[]{:S(2)}, u32[]{:S(2)}) collective-permute-start(bf16[32,7168]{1,0:T(8,128)(2,1)S(1)} %pad_maximum_fusion.8), channel_id=1, source_target_pairs={{0,8},{8,0},{1,9},{9,1},{2,10},{10,2},{3,11},{11,3},{4,12},{12,4},... | collective-permute-start | bytes 1376264 | tf_op jit(solution)/shard_map/ppermute | solution.py:40
  81.6 8.7 %collective-permute-start.12 = (bf16[24,7168]{1,0:T(8,128)(2,1)S(1)}, bf16[24,7168]{1,0:T(8,128)(2,1)S(1)}, u32[]{:S(2)}, u32[]{:S(2)}) collective-permute-start(bf16[24,7168]{1,0:T(8,128)(2,1)S(1)} %slice.266), channel_id=1, source_target_pairs={{0,2},{2,4},{4,6},{6,0},{1,3},{3,5},{5,7},{7,1},{8,10},{10,12},{12... | collective-permute-start | bytes 1032200 | tf_op jit(solution)/shard_map/ppermute | solution.py:36
  81.8 8.5 %collective-permute-start.13 = (bf16[24,7168]{1,0:T(8,128)(2,1)S(1)}, bf16[24,7168]{1,0:T(8,128)(2,1)S(1)}, u32[]{:S(2)}, u32[]{:S(2)}) collective-permute-start(bf16[24,7168]{1,0:T(8,128)(2,1)S(1)} %slice.267), channel_id=1, source_target_pairs={{0,6},{2,0},{4,2},{6,4},{1,7},{3,1},{5,3},{7,5},{8,14},{10,8},{12,... | collective-permute-start | bytes 1032200 | tf_op jit(solution)/shard_map/ppermute | solution.py:36
  90.4 7.8 %collective-permute-start.14 = (bf16[16,7168]{1,0:T(8,128)(2,1)S(1)}, bf16[16,7168]{1,0:T(8,128)(2,1)S(1)}, u32[]{:S(2)}, u32[]{:S(2)}) collective-permute-start(bf16[16,7168]{1,0:T(8,128)(2,1)S(1)} %slice.268), channel_id=1, source_target_pairs={{0,8},{8,0},{1,9},{9,1},{2,10},{10,2},{3,11},{11,3},{4,12},{12,4},... | collective-permute-start | bytes 688136 | tf_op jit(solution)/shard_map/ppermute | solution.py:40
  92.6 21.9 %collective-permute-start.16 = (bf16[64,7168]{1,0:T(8,128)(2,1)S(1)}, bf16[64,7168]{1,0:T(8,128)(2,1)S(1)}, u32[]{:S(2)}, u32[]{:S(2)}) collective-permute-start(bf16[64,7168]{1,0:T(8,128)(2,1)S(1)} %get-tuple-element.76), channel_id=1, source_target_pairs={{0,6},{2,0},{4,2},{6,4},{1,7},{3,1},{5,3},{7,5},{8,14},{10,8},{12,... | collective-permute-start | bytes 2752520 | tf_op jit(solution)/shard_map/ppermute | solution.py:36
  95.9 18.7 %collective-permute-start.15 = (bf16[64,7168]{1,0:T(8,128)(2,1)S(1)}, bf16[64,7168]{1,0:T(8,128)(2,1)S(1)}, u32[]{:S(2)}, u32[]{:S(2)}) collective-permute-start(bf16[64,7168]{1,0:T(8,128)(2,1)S(1)} %get-tuple-element.75), channel_id=1, source_target_pairs={{0,2},{2,4},{4,6},{6,0},{1,3},{3,5},{5,7},{7,1},{8,10},{10,12},{12... | collective-permute-start | bytes 2752520 | tf_op jit(solution)/shard_map/ppermute | solution.py:36
  114.5 13.6 %copy-start.4 = (bf16[256,7168]{1,0:T(8,128)(2,1)}, bf16[256,7168]{1,0:T(8,128)(2,1)S(1)}, u32[]{:S(2)}) copy-start(bf16[256,7168]{1,0:T(8,128)(2,1)S(1)} %convolution_convert_fusion) | copy-start | bytes 11010052
  114.8 10.1 %collective-permute-start.19 = (bf16[32,7168]{1,0:T(8,128)(2,1)S(1)}, bf16[32,7168]{1,0:T(8,128)(2,1)S(1)}, u32[]{:S(2)}, u32[]{:S(2)}) collective-permute-start(bf16[32,7168]{1,0:T(8,128)(2,1)S(1)} %get-tuple-element.82), channel_id=1, source_target_pairs={{0,2},{2,4},{4,6},{6,0},{1,3},{3,5},{5,7},{7,1},{8,10},{10,12},{12... | collective-permute-start | bytes 1376264 | tf_op jit(solution)/shard_map/ppermute | solution.py:36
  117.0 10.7 %collective-permute-start.20 = (bf16[32,7168]{1,0:T(8,128)(2,1)S(1)}, bf16[32,7168]{1,0:T(8,128)(2,1)S(1)}, u32[]{:S(2)}, u32[]{:S(2)}) collective-permute-start(bf16[32,7168]{1,0:T(8,128)(2,1)S(1)} %get-tuple-element.84), channel_id=1, source_target_pairs={{0,6},{2,0},{4,2},{6,4},{1,7},{3,1},{5,3},{7,5},{8,14},{10,8},{12,... | collective-permute-start | bytes 1376264 | tf_op jit(solution)/shard_map/ppermute | solution.py:36
  119.8 33.5 %collective-permute-start.23 = (bf16[7168,128]{1,0:T(8,128)(2,1)}, bf16[7168,128]{1,0:T(8,128)(2,1)S(1)}, u32[]{:S(2)}, u32[]{:S(2)}) collective-permute-start(bf16[7168,128]{1,0:T(8,128)(2,1)} %convolution_convert_fusion.6), channel_id=1, source_target_pairs={{0,1},{1,0},{2,3},{3,2},{4,5},{5,4},{6,7},{7,6},{8,9},{9,8},{10,11... | collective-permute-start | bytes 5505032 | tf_op jit(solution)/shard_map/ppermute | solution.py:184
  119.8 25.4 %collective-permute-start.18 = (bf16[64,7168]{1,0:T(8,128)(2,1)}, bf16[64,7168]{1,0:T(8,128)(2,1)}, u32[]{:S(2)}, u32[]{:S(2)}) collective-permute-start(bf16[64,7168]{1,0:T(8,128)(2,1)} %get-tuple-element.80), channel_id=1, source_target_pairs={{0,6},{2,0},{4,2},{6,4},{1,7},{3,1},{5,3},{7,5},{8,14},{10,8},{12,... | collective-permute-start | bytes 2752520 | tf_op jit(solution)/shard_map/ppermute | solution.py:36
  121.8 24.0 %collective-permute-start.17 = (bf16[64,7168]{1,0:T(8,128)(2,1)}, bf16[64,7168]{1,0:T(8,128)(2,1)}, u32[]{:S(2)}, u32[]{:S(2)}) collective-permute-start(bf16[64,7168]{1,0:T(8,128)(2,1)} %get-tuple-element.79), channel_id=1, source_target_pairs={{0,2},{2,4},{4,6},{6,0},{1,3},{3,5},{5,7},{7,1},{8,10},{10,12},{12... | collective-permute-start | bytes 2752520 | tf_op jit(solution)/shard_map/ppermute | solution.py:36
  129.6 18.8 %all-to-all-start.2 = ((bf16[16,4,7168]{2,1,0:T(4,128)(2,1)}), bf16[16,4,7168]{2,1,0:T(4,128)(2,1)S(1)}, u32[]{:S(2)}, u32[]{:S(2)}) async-start(bf16[16,4,7168]{2,1,0:T(4,128)(2,1)} %reshape.134), calls=%async_computation.2 | async-start | bytes 1835008 | tf_op jit(solution)/shard_map/all_to_all | solution.py:102
  149.5 13.3 %collective-permute-start.21 = (bf16[32,7168]{1,0:T(8,128)(2,1)}, bf16[32,7168]{1,0:T(8,128)(2,1)S(1)}, u32[]{:S(2)}, u32[]{:S(2)}) collective-permute-start(bf16[32,7168]{1,0:T(8,128)(2,1)} %get-tuple-element.87), channel_id=1, source_target_pairs={{0,2},{2,4},{4,6},{6,0},{1,3},{3,5},{5,7},{7,1},{8,10},{10,12},{12... | collective-permute-start | bytes 1376264 | tf_op jit(solution)/shard_map/ppermute | solution.py:36
  150.6 12.2 %collective-permute-start.22 = (bf16[32,7168]{1,0:T(8,128)(2,1)}, bf16[32,7168]{1,0:T(8,128)(2,1)S(1)}, u32[]{:S(2)}, u32[]{:S(2)}) collective-permute-start(bf16[32,7168]{1,0:T(8,128)(2,1)} %get-tuple-element.89), channel_id=1, source_target_pairs={{0,6},{2,0},{4,2},{6,4},{1,7},{3,1},{5,3},{7,5},{8,14},{10,8},{12,... | collective-permute-start | bytes 1376264 | tf_op jit(solution)/shard_map/ppermute | solution.py:36
  152.8 18.7 %collective-permute-start.24 = (bf16[7168,128]{1,0:T(8,128)(2,1)}, bf16[7168,128]{1,0:T(8,128)(2,1)}, u32[]{:S(2)}, u32[]{:S(2)}) collective-permute-start(bf16[7168,128]{1,0:T(8,128)(2,1)} %convolution_convert_fusion.5), channel_id=1, source_target_pairs={{0,1},{1,0},{2,3},{3,2},{4,5},{5,4},{6,7},{7,6},{8,9},{9,8},{10,11... | collective-permute-start | bytes 5505032 | tf_op jit(solution)/shard_map/ppermute | solution.py:185
  152.9 23.7 %collective-permute-start.25 = (bf16[128,7168]{1,0:T(8,128)(2,1)}, bf16[128,7168]{1,0:T(8,128)(2,1)}, u32[]{:S(2)}, u32[]{:S(2)}) collective-permute-start(bf16[128,7168]{1,0:T(8,128)(2,1)} %convolution_convert_fusion.4), channel_id=1, source_target_pairs={{0,1},{1,0},{2,3},{3,2},{4,5},{5,4},{6,7},{7,6},{8,9},{9,8},{10,11... | collective-permute-start | bytes 5505032 | tf_op jit(solution)/shard_map/ppermute | solution.py:186
  166.1 19.5 %all-to-all-start.3 = ((bf16[16,4,7168]{2,1,0:T(4,128)(2,1)}), bf16[16,4,7168]{2,1,0:T(4,128)(2,1)S(1)}, u32[]{:S(2)}, u32[]{:S(2)}) async-start(bf16[16,4,7168]{2,1,0:T(4,128)(2,1)} %reshape.137), calls=%async_computation.3 | async-start | bytes 1835008 | tf_op jit(solution)/shard_map/all_to_all | solution.py:102
  (7 other events, 48.4 us)

commit v4 on v3

--- a/solution.py
+++ b/solution.py
@@ -100,7 +100,7 @@
     width = rows.shape[1]
     sent = absolute(rows).reshape(16, CAP, width)
     back = lax.all_to_all(sent, PLANE, split_axis=0, concat_axis=0, tiled=True)
-    return back.reshape(16 * CAP, width)
+    return back
 
 
 def local(tokens, route, gates, cotangent, w_gate, w_up, w_down):
@@ -116,8 +116,8 @@
     picked_b = picked.astype(BF16).reshape(-1, 8 * CAP)
     picked_w = jnp.where(picked, weight[:, :, None], 0.0)
     pair = lambda a: jnp.broadcast_to(a.reshape(-1, 2, 1, 4, CAP), (a.shape[0], 2, 2, 4, CAP))
-    twice_b = pair(picked.astype(BF16)).reshape(-1, 16 * CAP)
-    twice_w = pair(picked_w).reshape(-1, 16 * CAP)
+    twice_b = pair(picked.astype(BF16)).reshape(-1, 16, CAP)
+    twice_w = pair(picked_w).reshape(-1, 16, CAP)
     picked_w = picked_w.reshape(-1, 8 * CAP)
     slot_gate = jnp.sum(picked_w, axis=0)
     x_slots = jnp.einsum("ts,td->sd", picked_b, tokens, preferred_element_type=F32).astype(BF16)
@@ -189,10 +189,12 @@
     grad_down = add(late(hidden[:, :half], rows_d), out_got)
 
     back_in = to_slots(q_rows)
-    mixed = jnp.dot(
-        twice_w, back_out.astype(F32), precision=lax.Precision.HIGHEST
+    mixed = jnp.einsum(
+        "tgc,gcd->td", twice_w, back_out.astype(F32), precision=lax.Precision.HIGHEST
     ).astype(BF16)
-    grad_tokens = jnp.dot(twice_b, back_in, preferred_element_type=F32).astype(BF16)
+    grad_tokens = jnp.einsum(
+        "tgc,gcd->td", twice_b, back_in, preferred_element_type=F32
+    ).astype(BF16)
     return (mixed, grad_tokens, grad_gate[None], grad_up[None], grad_down[None])
 
 

time: 191 us -> 188 us (0.984)
  local copies, waits for them, and re-layouts: 27 us -> 23.6 us
  starting transfers between devices: 55.9 us -> 53 us
    all_to_all x2, starting transfers between devices: 11.3 us -> 8.08 us  [to_slots(): back = lax.all_to_all(sent, PLANE, split_axis=0, concat_axis=0, tiled=True)]
    reshape x2 -> x0, local copies, waits for them, and re-layouts: 2.29 us -> none  [to_slots(): return back.reshape(16 * CAP, width)]
    ppermute x12, waiting for transfers between devices: 25.4 us -> 27.5 us  [far_z(): return (lax.ppermute(low, 'z', z_by(1)), lax.ppermute(high, 'z', z_by(3)))]
    unnamed x35 -> x43, local copies, waits for them, and re-layouts: 12.3 us -> 11.2 us
where the time goes in v4:
time: 188 us; the launch traced here: 187 us
  waiting for transfers between devices  53.6 us (29%)
  starting transfers between devices  53 us (28%)
  matrix products  39.6 us (21%)
  local copies, waits for them, and re-layouts  23.6 us (13%)
  other arithmetic  15.8 us (8%)
    ppermute x12, waiting for transfers between devices, far_z(): return (lax.ppermute(low, 'z', z_by(1)), lax.ppermute(high, 'z', z_by(3)))  27.5 us
    dot_general x6, matrix products, local(): jnp.einsum('rd,rf->df', a, b, preferred_element_type=F32)  22.9 us
    ppermute x12, starting transfers between devices, far_z(): return (lax.ppermute(low, 'z', z_by(1)), lax.ppermute(high, 'z', z_by(3)))  19 us
    all_to_all x2, waiting for transfers between devices, move_plane(): lax.all_to_all(twice, PLANE, split_axis=0, concat_axis=0, tiled=True)  13.5 us
    unnamed x43, local copies, waits for them, and re-layouts  11.2 us
    all_to_all x2, starting transfers between devices, move_plane(): lax.all_to_all(twice, PLANE, split_axis=0, concat_axis=0, tiled=True)  11 us
    all_to_all x2, starting transfers between devices, to_slots(): back = lax.all_to_all(sent, PLANE, split_axis=0, concat_axis=0, tiled=True)  8.08 us
    ppermute x4, starting transfers between devices, across(): return lax.ppermute(rows, 'xh', SWAP)  7.3 us
  transfers between devices with their start and end apart: 30, of which 11 were waited for; matrix products, arithmetic and copies ran while one was open for 39% of the time, Pallas kernels for 0%

profile of v4, /device:TPU:0, one launch (start us, length us, event | category | flops | bytes accessed | tf_op | source)
XLA Modules:
  0.0 186.8 jit_solution(14902448877406429192)
XLA Ops:
  3.9 7.1 %all-to-all-start = ((bf16[16,4,7168]{2,1,0:T(4,128)(2,1)}), bf16[16,4,7168]{2,1,0:T(4,128)(2,1)S(1)}, u32[]{:S(2)}, u32[]{:S(2)}) async-start(bf16[16,4,7168]{2,1,0:T(4,128)(2,1)} %bitcast.7), calls=%async_computation | async-start | bytes 1835008 | tf_op jit(solution)/shard_map/all_to_all | solution.py:95
  15.3 11.0 %all-to-all-done = bf16[16,4,7168]{2,1,0:T(4,128)(2,1)S(1)} async-done(((bf16[16,4,7168]{2,1,0:T(4,128)(2,1)}), bf16[16,4,7168]{2,1,0:T(4,128)(2,1)S(1)}, u32[]{:S(2)}, u32[]{:S(2)}) %all-to-all-start) | async-done | bytes 917536 | tf_op jit(solution)/shard_map/all_to_all | solution.py:95
  30.5 2.1 %collective-permute-start.1 = (bf16[48,7168]{1,0:T(8,128)(2,1)}, bf16[48,7168]{1,0:T(8,128)(2,1)S(1)}, u32[]{:S(2)}, u32[]{:S(2)}) collective-permute-start(bf16[48,7168]{1,0:T(8,128)(2,1)} %constant_dynamic-update-slice_fusion), channel_id=1, source_target_pairs={{0,6},{2,0},{4,2},{6,4},{1,7},{3,1},{5,3},{7,5},{8,14},{10,8},{12,... | collective-permute-start | bytes 2064392 | tf_op jit(solution)/shard_map/ppermute | solution.py:27
  32.8 2.2 %broadcast_in_dim.82 = bf16[2,2,4,4,7168]{4,3,2,1,0:T(4,128)(2,1)} broadcast(bf16[2,4,4,7168]{3,2,1,0:T(4,128)(2,1)} %broadcast_in_dim.81), dimensions={0,2,3,4} | broadcast | bytes 1376256 | tf_op jit(solution)/shard_map/broadcast_in_dim | solution.py:90
  35.0 3.9 %all-to-all-start.1 = ((bf16[16,4,7168]{2,1,0:T(4,128)(2,1)}), bf16[16,4,7168]{2,1,0:T(4,128)(2,1)S(1)}, u32[]{:S(2)}, u32[]{:S(2)}) async-start(bf16[16,4,7168]{2,1,0:T(4,128)(2,1)} %bitcast.6), calls=%async_computation.1 | async-start | bytes 1835008 | tf_op jit(solution)/shard_map/all_to_all | solution.py:95
  40.0 6.0 %collective-permute-done = bf16[48,7168]{1,0:T(8,128)(2,1)S(1)} collective-permute-done((bf16[48,7168]{1,0:T(8,128)(2,1)}, bf16[48,7168]{1,0:T(8,128)(2,1)S(1)}, u32[]{:S(2)}, u32[]{:S(2)}) %collective-permute-start) | collective-permute-done | bytes 688160 | tf_op jit(solution)/shard_map/ppermute | solution.py:27
  48.0 2.7 %collective-permute-start.10 = (bf16[24,7168]{1,0:T(8,128)(2,1)}, bf16[24,7168]{1,0:T(8,128)(2,1)}, u32[]{:S(2)}, u32[]{:S(2)}) collective-permute-start(bf16[24,7168]{1,0:T(8,128)(2,1)} %slice.259), channel_id=1, source_target_pairs={{0,6},{2,0},{4,2},{6,4},{1,7},{3,1},{5,3},{7,5},{8,14},{10,8},{12,... | collective-permute-start | bytes 1032200 | tf_op jit(solution)/shard_map/ppermute | solution.py:36
  51.6 2.4 %all-to-all-done.1 = bf16[16,4,7168]{2,1,0:T(4,128)(2,1)S(1)} async-done(((bf16[16,4,7168]{2,1,0:T(4,128)(2,1)}), bf16[16,4,7168]{2,1,0:T(4,128)(2,1)S(1)}, u32[]{:S(2)}, u32[]{:S(2)}) %all-to-all-start.1) | async-done | bytes 917536 | tf_op jit(solution)/shard_map/all_to_all | solution.py:95
  62.5 4.0 %pad_maximum_fusion = bf16[7168,512]{1,0:T(8,128)(2,1)S(1)} fusion(bf16[7168,128]{1,0:T(8,128)(2,1)} %collective-permute-done.7, bf16[7168,128]{1,0:T(8,128)(2,1)} %bitcast.47, bf16[7168,128]{1,0:T(8,128)(2,1)} %collective-permute-done.6, bf16[7168,128]{1,0:T(8,128)(2,1)} %bitcast.49), kind=kLoop, calls=%fused_computation.21 | loop fusion | flops 29360128 | bytes 14680064 | tf_op jit(solution)/shard_map/concatenate | solution.py:141
  68.4 2.1 %collective-permute-start.11 = (bf16[16,7168]{1,0:T(8,128)(2,1)S(1)}, bf16[16,7168]{1,0:T(8,128)(2,1)S(1)}, u32[]{:S(2)}, u32[]{:S(2)}) collective-permute-start(bf16[16,7168]{1,0:T(8,128)(2,1)S(1)} %slice.260), channel_id=1, source_target_pairs={{0,8},{8,0},{1,9},{9,1},{2,10},{10,2},{3,11},{11,3},{4,12},{12,4},... | collective-permute-start | bytes 688136 | tf_op jit(solution)/shard_map/ppermute | solution.py:40
  71.5 4.5 %collective-permute-done.11 = bf16[16,7168]{1,0:T(8,128)(2,1)S(1)} collective-permute-done((bf16[16,7168]{1,0:T(8,128)(2,1)S(1)}, bf16[16,7168]{1,0:T(8,128)(2,1)S(1)}, u32[]{:S(2)}, u32[]{:S(2)}) %collective-permute-start.11) | collective-permute-done | bytes 229408 | tf_op jit(solution)/shard_map/ppermute | solution.py:40
  82.1 3.2 %collective-permute-start.13 = (bf16[24,7168]{1,0:T(8,128)(2,1)S(1)}, bf16[24,7168]{1,0:T(8,128)(2,1)S(1)}, u32[]{:S(2)}, u32[]{:S(2)}) collective-permute-start(bf16[24,7168]{1,0:T(8,128)(2,1)S(1)} %slice.267), channel_id=1, source_target_pairs={{0,6},{2,0},{4,2},{6,4},{1,7},{3,1},{5,3},{7,5},{8,14},{10,8},{12,... | collective-permute-start | bytes 1032200 | tf_op jit(solution)/shard_map/ppermute | solution.py:36
  86.2 4.3 %collective-permute-done.12 = bf16[24,7168]{1,0:T(8,128)(2,1)S(1)} collective-permute-done((bf16[24,7168]{1,0:T(8,128)(2,1)S(1)}, bf16[24,7168]{1,0:T(8,128)(2,1)S(1)}, u32[]{:S(2)}, u32[]{:S(2)}) %collective-permute-start.12) | collective-permute-done | bytes 344096 | tf_op jit(solution)/shard_map/ppermute | solution.py:36
  92.1 3.2 %collective-permute-start.16 = (bf16[64,7168]{1,0:T(8,128)(2,1)S(1)}, bf16[64,7168]{1,0:T(8,128)(2,1)S(1)}, u32[]{:S(2)}, u32[]{:S(2)}) collective-permute-start(bf16[64,7168]{1,0:T(8,128)(2,1)S(1)} %get-tuple-element.76), channel_id=1, source_target_pairs={{0,6},{2,0},{4,2},{6,4},{1,7},{3,1},{5,3},{7,5},{8,14},{10,8},{12,... | collective-permute-start | bytes 2752520 | tf_op jit(solution)/shard_map/ppermute | solution.py:36
  100.5 3.9 %convolution_convert_fusion.2 = bf16[128,7168]{1,0:T(8,128)(2,1)} fusion(bf16[256,7168]{1,0:T(8,128)(2,1)} %slice_dynamic-update-slice_fusion, bf16[256,256]{1,0:T(8,128)(2,1)S(1)} %get-tuple-element.65), kind=kOutput, calls=%fused_computation.12 | convolution fusion | flops 470679552 | bytes 5570560 | tf_op jit(solution)/shard_map/rd,rf->df/dot_general | solution.py:165
  104.4 3.2 %multiply_convert_fusion = (bf16[256,256]{1,0:T(8,128)(2,1)S(1)}, bf16[256,256]{1,0:T(8,128)(2,1)S(1)}) fusion(f32[256,256]{1,0:T(8,128)S(1)} %get-tuple-element.72, f32[256,256]{1,0:T(8,128)S(1)} %get-tuple-element.71, bf16[256,7168]{1,0:T(8,128)(2,1)} %slice_dynamic-update-slice_fusion, bf16[256,7168]{1,0:T(8,128)(2,1)S(1)} %pad_maximum_fusion.1), kind=kOutput, calls=%fused_computation.54 | convolution fusion | flops 940376064 | bytes 8126464 | tf_op jit(solution)/shard_map/rd,fd->rf/dot_general | solution.py:160
  107.6 2.4 %convolution_convert_fusion.4 = bf16[7168,128]{1,0:T(8,128)(2,1)} fusion(bf16[256,7168]{1,0:T(8,128)(2,1)S(1)} %slice_dynamic-update-slice_fusion.1, bf16[256,256]{1,0:T(8,128)(2,1)S(1)} %get-tuple-element.73), kind=kOutput, calls=%fused_computation.14 | convolution fusion | flops 470679552 | bytes 5570560 | tf_op jit(solution)/shard_map/rd,rf->df/dot_general | solution.py:165
  110.0 2.4 %convolution_convert_fusion.3 = bf16[7168,128]{1,0:T(8,128)(2,1)} fusion(bf16[256,7168]{1,0:T(8,128)(2,1)S(1)} %slice_dynamic-update-slice_fusion.1, bf16[256,256]{1,0:T(8,128)(2,1)S(1)} %get-tuple-element.74), kind=kOutput, calls=%fused_computation.13 | convolution fusion | flops 470679552 | bytes 5570560 | tf_op jit(solution)/shard_map/rd,rf->df/dot_general | solution.py:165
  112.5 2.1 %convolution_convert_fusion = bf16[256,7168]{1,0:T(8,128)(2,1)S(1)} fusion(bf16[7168,512]{1,0:T(8,128)(2,1)S(1)} %pad_maximum_fusion, bf16[256,256]{1,0:T(8,128)(2,1)S(1)} %get-tuple-element.74, bf16[256,256]{1,0:T(8,128)(2,1)S(1)} %get-tuple-element.73), kind=kOutput, calls=%fused_computation | convolution fusion | flops 1881407488 | bytes 11272192 | tf_op jit(solution)/shard_map/rf,df->rd/dot_general | solution.py:173
  114.8 3.3 %collective-permute-start.19 = (bf16[32,7168]{1,0:T(8,128)(2,1)S(1)}, bf16[32,7168]{1,0:T(8,128)(2,1)S(1)}, u32[]{:S(2)}, u32[]{:S(2)}) collective-permute-start(bf16[32,7168]{1,0:T(8,128)(2,1)S(1)} %get-tuple-element.82), channel_id=1, source_target_pairs={{0,2},{2,4},{4,6},{6,0},{1,3},{3,5},{5,7},{7,1},{8,10},{10,12},{12... | collective-permute-start | bytes 1376264 | tf_op jit(solution)/shard_map/ppermute | solution.py:36
  122.0 3.3 %collective-permute-done.19 = bf16[32,7168]{1,0:T(8,128)(2,1)S(1)} collective-permute-done((bf16[32,7168]{1,0:T(8,128)(2,1)S(1)}, bf16[32,7168]{1,0:T(8,128)(2,1)S(1)}, u32[]{:S(2)}, u32[]{:S(2)}) %collective-permute-start.19) | collective-permute-done | bytes 458784 | tf_op jit(solution)/shard_map/ppermute | solution.py:36
  125.3 4.5 %collective-permute-done.20 = bf16[32,7168]{1,0:T(8,128)(2,1)S(1)} collective-permute-done((bf16[32,7168]{1,0:T(8,128)(2,1)S(1)}, bf16[32,7168]{1,0:T(8,128)(2,1)S(1)}, u32[]{:S(2)}, u32[]{:S(2)}) %collective-permute-start.20) | collective-permute-done | bytes 458784 | tf_op jit(solution)/shard_map/ppermute | solution.py:36
  131.7 3.6 %all-to-all-start.2 = ((bf16[16,4,7168]{2,1,0:T(4,128)(2,1)}), bf16[16,4,7168]{2,1,0:T(4,128)(2,1)S(1)}, u32[]{:S(2)}, u32[]{:S(2)}) async-start(bf16[16,4,7168]{2,1,0:T(4,128)(2,1)} %reshape.128), calls=%async_computation.2 | async-start | bytes 1835008 | tf_op jit(solution)/shard_map/all_to_all | solution.py:102
  135.3 11.0 %collective-permute-done.18 = bf16[64,7168]{1,0:T(8,128)(2,1)} collective-permute-done((bf16[64,7168]{1,0:T(8,128)(2,1)}, bf16[64,7168]{1,0:T(8,128)(2,1)}, u32[]{:S(2)}, u32[]{:S(2)}) %collective-permute-start.18) | collective-permute-done | bytes 917536 | tf_op jit(solution)/shard_map/ppermute | solution.py:36
  146.3 2.6 %add_convert_fusion.4 = (bf16[32,7168]{1,0:T(8,128)(2,1)}, bf16[32,7168]{1,0:T(8,128)(2,1)}) fusion(bf16[64,7168]{1,0:T(8,128)(2,1)} %collective-permute-done.18, bf16[256,7168]{1,0:T(8,128)(2,1)} %copy-done.4, bf16[64,7168]{1,0:T(8,128)(2,1)} %collective-permute-done.17), kind=kLoop, calls=%fused_computation.32 | loop fusion | flops 1835008 | bytes 2752512 | tf_op jit(solution)/shard_map/convert_element_type | solution.py:23
  153.0 4.4 %fusion.7 = bf16[1,7168,128]{2,1,0:T(8,128)(2,1)} fusion(bf16[256,7168]{1,0:T(8,128)(2,1)} %copy-done.3, bf16[7168,128]{1,0:T(8,128)(2,1)S(1)} %collective-permute-done.23, bf16[256,256]{1,0:T(8,128)(2,1)S(1)} %get-tuple-element.73), kind=kOutput, calls=%fused_computation.17 | convolution fusion | flops 472514560 | bytes 7405568 | tf_op jit(solution)/shard_map/rd,rf->df/dot_general | solution.py:165
  157.4 4.4 %collective-permute-done.21 = bf16[32,7168]{1,0:T(8,128)(2,1)S(1)} collective-permute-done((bf16[32,7168]{1,0:T(8,128)(2,1)}, bf16[32,7168]{1,0:T(8,128)(2,1)S(1)}, u32[]{:S(2)}, u32[]{:S(2)}) %collective-permute-start.21) | collective-permute-done | bytes 458784 | tf_op jit(solution)/shard_map/ppermute | solution.py:36
  165.2 4.4 %all-to-all-start.3 = ((bf16[16,4,7168]{2,1,0:T(4,128)(2,1)}), bf16[16,4,7168]{2,1,0:T(4,128)(2,1)}, u32[]{:S(2)}, u32[]{:S(2)}) async-start(bf16[16,4,7168]{2,1,0:T(4,128)(2,1)} %reshape.130), calls=%async_computation.3 | async-start | bytes 1835008 | tf_op jit(solution)/shard_map/all_to_all | solution.py:102
  169.6 5.0 %fusion.6 = bf16[1,7168,128]{2,1,0:T(8,128)(2,1)} fusion(bf16[256,7168]{1,0:T(8,128)(2,1)} %copy-done.3, bf16[7168,128]{1,0:T(8,128)(2,1)} %collective-permute-done.24, bf16[256,256]{1,0:T(8,128)(2,1)S(1)} %get-tuple-element.74), kind=kOutput, calls=%fused_computation.16 | convolution fusion | flops 472514560 | bytes 7405568 | tf_op jit(solution)/shard_map/rd,rf->df/dot_general | solution.py:165
  174.7 4.7 %fusion.5 = bf16[1,128,7168]{2,1,0:T(8,128)(2,1)} fusion(bf16[256,7168]{1,0:T(8,128)(2,1)} %slice_dynamic-update-slice_fusion, bf16[128,7168]{1,0:T(8,128)(2,1)} %collective-permute-done.25, bf16[256,256]{1,0:T(8,128)(2,1)S(1)} %get-tuple-element.65), kind=kOutput, calls=%fused_computation.15 | convolution fusion | flops 472514560 | bytes 7405568 | tf_op jit(solution)/shard_map/rd,rf->df/dot_general | solution.py:165
  179.3 2.9 %fusion = bf16[128,7168]{1,0:T(8,128)(2,1)} fusion(f32[128,16,4]{0,1,2:T(8,128)S(1)} %bitcast.52, bf16[16,4,7168]{2,1,0:T(4,128)(2,1)S(1)} %all-to-all-done.2), kind=kOutput, calls=%fused_computation.7 | convolution fusion | flops 705560576 | bytes 2785280 | tf_op jit(solution)/shard_map/tgc,gcd->td/dot_general | solution.py:192
  183.7 3.1 %fusion.1 = bf16[128,7168]{1,0:T(8,128)(2,1)} fusion(bf16[128,16,4]{0,1,2:T(8,128)(2,1)S(1)} %bitcast.53, bf16[16,4,7168]{2,1,0:T(4,128)(2,1)} %all-to-all-done.3), kind=kOutput, calls=%fused_computation.8 | convolution fusion | flops 118358016 | bytes 2768896 | tf_op jit(solution)/shard_map/tgc,gcd->td/dot_general | solution.py:195
  (147 shorter events, 55.5 us)
Async XLA Ops:
  3.9 22.5 %all-to-all-start = ((bf16[16,4,7168]{2,1,0:T(4,128)(2,1)}), bf16[16,4,7168]{2,1,0:T(4,128)(2,1)S(1)}, u32[]{:S(2)}, u32[]{:S(2)}) async-start(bf16[16,4,7168]{2,1,0:T(4,128)(2,1)} %bitcast.7), calls=%async_computation | async-start | bytes 1835008 | tf_op jit(solution)/shard_map/all_to_all | solution.py:95
  11.0 47.9 %collective-permute-start.6 = (bf16[7168,128]{1,0:T(8,128)(2,1)}, bf16[7168,128]{1,0:T(8,128)(2,1)}, u32[]{:S(2)}, u32[]{:S(2)}) collective-permute-start(bf16[7168,128]{1,0:T(8,128)(2,1)} %bitcast.48), channel_id=1, source_target_pairs={{0,1},{1,0},{2,3},{3,2},{4,5},{5,4},{6,7},{7,6},{8,9},{9,8},{10,11... | collective-permute-start | bytes 5505032 | tf_op jit(solution)/shard_map/ppermute | solution.py:124
  11.1 49.4 %collective-permute-start.7 = (bf16[7168,128]{1,0:T(8,128)(2,1)}, bf16[7168,128]{1,0:T(8,128)(2,1)}, u32[]{:S(2)}, u32[]{:S(2)}) collective-permute-start(bf16[7168,128]{1,0:T(8,128)(2,1)} %bitcast.46), channel_id=1, source_target_pairs={{0,1},{1,0},{2,3},{3,2},{4,5},{5,4},{6,7},{7,6},{8,9},{9,8},{10,11... | collective-permute-start | bytes 5505032 | tf_op jit(solution)/shard_map/ppermute | solution.py:125
  11.6 50.6 %collective-permute-start.8 = (bf16[128,7168]{1,0:T(8,128)(2,1)}, bf16[128,7168]{1,0:T(8,128)(2,1)}, u32[]{:S(2)}, u32[]{:S(2)}) collective-permute-start(bf16[128,7168]{1,0:T(8,128)(2,1)} %bitcast.50), channel_id=1, source_target_pairs={{0,1},{1,0},{2,3},{3,2},{4,5},{5,4},{6,7},{7,6},{8,9},{9,8},{10,11... | collective-permute-start | bytes 5505032 | tf_op jit(solution)/shard_map/ppermute | solution.py:126
  28.6 17.4 %collective-permute-start = (bf16[48,7168]{1,0:T(8,128)(2,1)}, bf16[48,7168]{1,0:T(8,128)(2,1)S(1)}, u32[]{:S(2)}, u32[]{:S(2)}) collective-permute-start(bf16[48,7168]{1,0:T(8,128)(2,1)} %constant_dynamic-update-slice_fusion), channel_id=1, source_target_pairs={{0,2},{2,4},{4,6},{6,0},{1,3},{3,5},{5,7},{7,1},{8,10},{10,12},{12... | collective-permute-start | bytes 2064392 | tf_op jit(solution)/shard_map/ppermute | solution.py:27
  30.5 16.2 %collective-permute-start.1 = (bf16[48,7168]{1,0:T(8,128)(2,1)}, bf16[48,7168]{1,0:T(8,128)(2,1)S(1)}, u32[]{:S(2)}, u32[]{:S(2)}) collective-permute-start(bf16[48,7168]{1,0:T(8,128)(2,1)} %constant_dynamic-update-slice_fusion), channel_id=1, source_target_pairs={{0,6},{2,0},{4,2},{6,4},{1,7},{3,1},{5,3},{7,5},{8,14},{10,8},{12,... | collective-permute-start | bytes 2064392 | tf_op jit(solution)/shard_map/ppermute | solution.py:27
  35.0 19.0 %all-to-all-start.1 = ((bf16[16,4,7168]{2,1,0:T(4,128)(2,1)}), bf16[16,4,7168]{2,1,0:T(4,128)(2,1)S(1)}, u32[]{:S(2)}, u32[]{:S(2)}) async-start(bf16[16,4,7168]{2,1,0:T(4,128)(2,1)} %bitcast.6), calls=%async_computation.1 | async-start | bytes 1835008 | tf_op jit(solution)/shard_map/all_to_all | solution.py:95
  47.5 15.0 %collective-permute-start.9 = (bf16[24,7168]{1,0:T(8,128)(2,1)}, bf16[24,7168]{1,0:T(8,128)(2,1)S(1)}, u32[]{:S(2)}, u32[]{:S(2)}) collective-permute-start(bf16[24,7168]{1,0:T(8,128)(2,1)} %slice.258), channel_id=1, source_target_pairs={{0,2},{2,4},{4,6},{6,0},{1,3},{3,5},{5,7},{7,1},{8,10},{10,12},{12... | collective-permute-start | bytes 1032200 | tf_op jit(solution)/shard_map/ppermute | solution.py:36
  48.0 14.5 %collective-permute-start.10 = (bf16[24,7168]{1,0:T(8,128)(2,1)}, bf16[24,7168]{1,0:T(8,128)(2,1)}, u32[]{:S(2)}, u32[]{:S(2)}) collective-permute-start(bf16[24,7168]{1,0:T(8,128)(2,1)} %slice.259), channel_id=1, source_target_pairs={{0,6},{2,0},{4,2},{6,4},{1,7},{3,1},{5,3},{7,5},{8,14},{10,8},{12,... | collective-permute-start | bytes 1032200 | tf_op jit(solution)/shard_map/ppermute | solution.py:36
  58.9 11.6 %collective-permute-start.5 = (bf16[32,7168]{1,0:T(8,128)(2,1)}, bf16[32,7168]{1,0:T(8,128)(2,1)S(1)}, u32[]{:S(2)}, u32[]{:S(2)}) collective-permute-start(bf16[32,7168]{1,0:T(8,128)(2,1)} %pad_maximum_fusion.9), channel_id=1, source_target_pairs={{0,8},{8,0},{1,9},{9,1},{2,10},{10,2},{3,11},{11,3},{4,12},{12,4},... | collective-permute-start | bytes 1376264 | tf_op jit(solution)/shard_map/ppermute | solution.py:40
  60.5 19.1 %collective-permute-start.2 = (bf16[48,7168]{1,0:T(8,128)(2,1)}, bf16[48,7168]{1,0:T(8,128)(2,1)S(1)}, u32[]{:S(2)}, u32[]{:S(2)}) collective-permute-start(bf16[48,7168]{1,0:T(8,128)(2,1)} %pad_maximum_fusion.5), channel_id=1, source_target_pairs={{0,6},{2,0},{4,2},{6,4},{1,7},{3,1},{5,3},{7,5},{8,14},{10,8},{12,... | collective-permute-start | bytes 2064392 | tf_op jit(solution)/shard_map/ppermute | solution.py:27
  62.2 17.4 %collective-permute-start.3 = (bf16[48,7168]{1,0:T(8,128)(2,1)}, bf16[48,7168]{1,0:T(8,128)(2,1)S(1)}, u32[]{:S(2)}, u32[]{:S(2)}) collective-permute-start(bf16[48,7168]{1,0:T(8,128)(2,1)} %pad_maximum_fusion.5), channel_id=1, source_target_pairs={{0,2},{2,4},{4,6},{6,0},{1,3},{3,5},{5,7},{7,1},{8,10},{10,12},{12... | collective-permute-start | bytes 2064392 | tf_op jit(solution)/shard_map/ppermute | solution.py:27
  68.4 7.6 %collective-permute-start.11 = (bf16[16,7168]{1,0:T(8,128)(2,1)S(1)}, bf16[16,7168]{1,0:T(8,128)(2,1)S(1)}, u32[]{:S(2)}, u32[]{:S(2)}) collective-permute-start(bf16[16,7168]{1,0:T(8,128)(2,1)S(1)} %slice.260), channel_id=1, source_target_pairs={{0,8},{8,0},{1,9},{9,1},{2,10},{10,2},{3,11},{11,3},{4,12},{12,4},... | collective-permute-start | bytes 688136 | tf_op jit(solution)/shard_map/ppermute | solution.py:40
  76.1 33.9 %copy-start.3 = (bf16[256,7168]{1,0:T(8,128)(2,1)}, bf16[256,7168]{1,0:T(8,128)(2,1)S(1)}, u32[]{:S(2)}) copy-start(bf16[256,7168]{1,0:T(8,128)(2,1)S(1)} %slice_dynamic-update-slice_fusion.1) | copy-start | bytes 11010052
  79.7 15.7 %collective-permute-start.4 = (bf16[32,7168]{1,0:T(8,128)(2,1)S(1)}, bf16[32,7168]{1,0:T(8,128)(2,1)S(1)}, u32[]{:S(2)}, u32[]{:S(2)}) collective-permute-start(bf16[32,7168]{1,0:T(8,128)(2,1)S(1)} %pad_maximum_fusion.8), channel_id=1, source_target_pairs={{0,8},{8,0},{1,9},{9,1},{2,10},{10,2},{3,11},{11,3},{4,12},{12,4},... | collective-permute-start | bytes 1376264 | tf_op jit(solution)/shard_map/ppermute | solution.py:40
  81.8 8.7 %collective-permute-start.12 = (bf16[24,7168]{1,0:T(8,128)(2,1)S(1)}, bf16[24,7168]{1,0:T(8,128)(2,1)S(1)}, u32[]{:S(2)}, u32[]{:S(2)}) collective-permute-start(bf16[24,7168]{1,0:T(8,128)(2,1)S(1)} %slice.266), channel_id=1, source_target_pairs={{0,2},{2,4},{4,6},{6,0},{1,3},{3,5},{5,7},{7,1},{8,10},{10,12},{12... | collective-permute-start | bytes 1032200 | tf_op jit(solution)/shard_map/ppermute | solution.py:36
  82.1 8.4 %collective-permute-start.13 = (bf16[24,7168]{1,0:T(8,128)(2,1)S(1)}, bf16[24,7168]{1,0:T(8,128)(2,1)S(1)}, u32[]{:S(2)}, u32[]{:S(2)}) collective-permute-start(bf16[24,7168]{1,0:T(8,128)(2,1)S(1)} %slice.267), channel_id=1, source_target_pairs={{0,6},{2,0},{4,2},{6,4},{1,7},{3,1},{5,3},{7,5},{8,14},{10,8},{12,... | collective-permute-start | bytes 1032200 | tf_op jit(solution)/shard_map/ppermute | solution.py:36
  90.5 7.6 %collective-permute-start.14 = (bf16[16,7168]{1,0:T(8,128)(2,1)S(1)}, bf16[16,7168]{1,0:T(8,128)(2,1)S(1)}, u32[]{:S(2)}, u32[]{:S(2)}) collective-permute-start(bf16[16,7168]{1,0:T(8,128)(2,1)S(1)} %slice.268), channel_id=1, source_target_pairs={{0,8},{8,0},{1,9},{9,1},{2,10},{10,2},{3,11},{11,3},{4,12},{12,4},... | collective-permute-start | bytes 688136 | tf_op jit(solution)/shard_map/ppermute | solution.py:40
  92.1 22.4 %collective-permute-start.16 = (bf16[64,7168]{1,0:T(8,128)(2,1)S(1)}, bf16[64,7168]{1,0:T(8,128)(2,1)S(1)}, u32[]{:S(2)}, u32[]{:S(2)}) collective-permute-start(bf16[64,7168]{1,0:T(8,128)(2,1)S(1)} %get-tuple-element.76), channel_id=1, source_target_pairs={{0,6},{2,0},{4,2},{6,4},{1,7},{3,1},{5,3},{7,5},{8,14},{10,8},{12,... | collective-permute-start | bytes 2752520 | tf_op jit(solution)/shard_map/ppermute | solution.py:36
  95.4 19.2 %collective-permute-start.15 = (bf16[64,7168]{1,0:T(8,128)(2,1)S(1)}, bf16[64,7168]{1,0:T(8,128)(2,1)S(1)}, u32[]{:S(2)}, u32[]{:S(2)}) collective-permute-start(bf16[64,7168]{1,0:T(8,128)(2,1)S(1)} %get-tuple-element.75), channel_id=1, source_target_pairs={{0,2},{2,4},{4,6},{6,0},{1,3},{3,5},{5,7},{7,1},{8,10},{10,12},{12... | collective-permute-start | bytes 2752520 | tf_op jit(solution)/shard_map/ppermute | solution.py:36
  114.8 10.5 %collective-permute-start.19 = (bf16[32,7168]{1,0:T(8,128)(2,1)S(1)}, bf16[32,7168]{1,0:T(8,128)(2,1)S(1)}, u32[]{:S(2)}, u32[]{:S(2)}) collective-permute-start(bf16[32,7168]{1,0:T(8,128)(2,1)S(1)} %get-tuple-element.82), channel_id=1, source_target_pairs={{0,2},{2,4},{4,6},{6,0},{1,3},{3,5},{5,7},{7,1},{8,10},{10,12},{12... | collective-permute-start | bytes 1376264 | tf_op jit(solution)/shard_map/ppermute | solution.py:36
  118.1 11.7 %collective-permute-start.20 = (bf16[32,7168]{1,0:T(8,128)(2,1)S(1)}, bf16[32,7168]{1,0:T(8,128)(2,1)S(1)}, u32[]{:S(2)}, u32[]{:S(2)}) collective-permute-start(bf16[32,7168]{1,0:T(8,128)(2,1)S(1)} %get-tuple-element.84), channel_id=1, source_target_pairs={{0,6},{2,0},{4,2},{6,4},{1,7},{3,1},{5,3},{7,5},{8,14},{10,8},{12,... | collective-permute-start | bytes 1376264 | tf_op jit(solution)/shard_map/ppermute | solution.py:36
  120.0 33.0 %collective-permute-start.23 = (bf16[7168,128]{1,0:T(8,128)(2,1)}, bf16[7168,128]{1,0:T(8,128)(2,1)S(1)}, u32[]{:S(2)}, u32[]{:S(2)}) collective-permute-start(bf16[7168,128]{1,0:T(8,128)(2,1)} %convolution_convert_fusion.4), channel_id=1, source_target_pairs={{0,1},{1,0},{2,3},{3,2},{4,5},{5,4},{6,7},{7,6},{8,9},{9,8},{10,11... | collective-permute-start | bytes 5505032 | tf_op jit(solution)/shard_map/ppermute | solution.py:184
  120.0 26.4 %collective-permute-start.18 = (bf16[64,7168]{1,0:T(8,128)(2,1)}, bf16[64,7168]{1,0:T(8,128)(2,1)}, u32[]{:S(2)}, u32[]{:S(2)}) collective-permute-start(bf16[64,7168]{1,0:T(8,128)(2,1)} %get-tuple-element.80), channel_id=1, source_target_pairs={{0,6},{2,0},{4,2},{6,4},{1,7},{3,1},{5,3},{7,5},{8,14},{10,8},{12,... | collective-permute-start | bytes 2752520 | tf_op jit(solution)/shard_map/ppermute | solution.py:36
  122.0 24.4 %collective-permute-start.17 = (bf16[64,7168]{1,0:T(8,128)(2,1)}, bf16[64,7168]{1,0:T(8,128)(2,1)}, u32[]{:S(2)}, u32[]{:S(2)}) collective-permute-start(bf16[64,7168]{1,0:T(8,128)(2,1)} %get-tuple-element.79), channel_id=1, source_target_pairs={{0,2},{2,4},{4,6},{6,0},{1,3},{3,5},{5,7},{7,1},{8,10},{10,12},{12... | collective-permute-start | bytes 2752520 | tf_op jit(solution)/shard_map/ppermute | solution.py:36
  130.4 21.7 %copy-start.8 = (f32[128,8]{0,1:T(8,128)S(1)}, f32[128,8]{0,1:T(8,128)}, u32[]{:S(2)}) copy-start(f32[128,8]{0,1:T(8,128)} %copy-done.7) | copy-start | bytes 12292
  131.7 17.2 %all-to-all-start.2 = ((bf16[16,4,7168]{2,1,0:T(4,128)(2,1)}), bf16[16,4,7168]{2,1,0:T(4,128)(2,1)S(1)}, u32[]{:S(2)}, u32[]{:S(2)}) async-start(bf16[16,4,7168]{2,1,0:T(4,128)(2,1)} %reshape.128), calls=%async_computation.2 | async-start | bytes 1835008 | tf_op jit(solution)/shard_map/all_to_all | solution.py:102
  148.9 12.9 %collective-permute-start.21 = (bf16[32,7168]{1,0:T(8,128)(2,1)}, bf16[32,7168]{1,0:T(8,128)(2,1)S(1)}, u32[]{:S(2)}, u32[]{:S(2)}) collective-permute-start(bf16[32,7168]{1,0:T(8,128)(2,1)} %get-tuple-element.87), channel_id=1, source_target_pairs={{0,2},{2,4},{4,6},{6,0},{1,3},{3,5},{5,7},{7,1},{8,10},{10,12},{12... | collective-permute-start | bytes 1376264 | tf_op jit(solution)/shard_map/ppermute | solution.py:36
  150.7 11.1 %collective-permute-start.22 = (bf16[32,7168]{1,0:T(8,128)(2,1)}, bf16[32,7168]{1,0:T(8,128)(2,1)S(1)}, u32[]{:S(2)}, u32[]{:S(2)}) collective-permute-start(bf16[32,7168]{1,0:T(8,128)(2,1)} %get-tuple-element.89), channel_id=1, source_target_pairs={{0,6},{2,0},{4,2},{6,4},{1,7},{3,1},{5,3},{7,5},{8,14},{10,8},{12,... | collective-permute-start | bytes 1376264 | tf_op jit(solution)/shard_map/ppermute | solution.py:36
  152.2 17.4 %collective-permute-start.24 = (bf16[7168,128]{1,0:T(8,128)(2,1)}, bf16[7168,128]{1,0:T(8,128)(2,1)}, u32[]{:S(2)}, u32[]{:S(2)}) collective-permute-start(bf16[7168,128]{1,0:T(8,128)(2,1)} %convolution_convert_fusion.3), channel_id=1, source_target_pairs={{0,1},{1,0},{2,3},{3,2},{4,5},{5,4},{6,7},{7,6},{8,9},{9,8},{10,11... | collective-permute-start | bytes 5505032 | tf_op jit(solution)/shard_map/ppermute | solution.py:185
  152.5 22.2 %collective-permute-start.25 = (bf16[128,7168]{1,0:T(8,128)(2,1)}, bf16[128,7168]{1,0:T(8,128)(2,1)}, u32[]{:S(2)}, u32[]{:S(2)}) collective-permute-start(bf16[128,7168]{1,0:T(8,128)(2,1)} %convolution_convert_fusion.2), channel_id=1, source_target_pairs={{0,1},{1,0},{2,3},{3,2},{4,5},{5,4},{6,7},{7,6},{8,9},{9,8},{10,11... | collective-permute-start | bytes 5505032 | tf_op jit(solution)/shard_map/ppermute | solution.py:186
  165.2 18.5 %all-to-all-start.3 = ((bf16[16,4,7168]{2,1,0:T(4,128)(2,1)}), bf16[16,4,7168]{2,1,0:T(4,128)(2,1)}, u32[]{:S(2)}, u32[]{:S(2)}) async-start(bf16[16,4,7168]{2,1,0:T(4,128)(2,1)} %reshape.130), calls=%async_computation.3 | async-start | bytes 1835008 | tf_op jit(solution)/shard_map/all_to_all | solution.py:102
  (11 other events, 115.5 us)

commit v5 on v4

--- a/solution.py
+++ b/solution.py
@@ -120,14 +120,14 @@
     twice_w = pair(picked_w).reshape(-1, 16, CAP)
     picked_w = picked_w.reshape(-1, 8 * CAP)
     slot_gate = jnp.sum(picked_w, axis=0)
-    x_slots = jnp.einsum("ts,td->sd", picked_b, tokens, preferred_element_type=F32).astype(BF16)
     gate_other = lax.ppermute(w_gate[0], "core", SWAP)
     up_other = lax.ppermute(w_up[0], "core", SWAP)
     down_other = lax.ppermute(w_down[0], "core", SWAP)
 
     d_rows = jnp.einsum("ts,td->sd", picked_b, cotangent, preferred_element_type=F32)
     d_slots = (d_rows * slot_gate[:, None]).astype(BF16)
-    plane_x = move_plane(to_plane(x_slots))
+    x_twice = jnp.einsum("tgc,td->gcd", twice_b, tokens, preferred_element_type=F32)
+    plane_x = move_plane(x_twice.astype(BF16))
     x_near = near_z(plane_x[: 3 * LINE])
     d_twice, plane_x = tie(to_plane(d_slots), plane_x)
     plane_d = move_plane(d_twice)

time: 188 us -> 188 us (level)
    broadcast_in_dim x4 -> x2, local copies, waits for them, and re-layouts: 4.51 us -> 3.18 us  [to_plane(): jnp.broadcast_to(slots.reshape(2, 1, 4, CAP, width), (2, 2, 4, CAP, width))]
    unnamed x43 -> x49, local copies, waits for them, and re-layouts: 11.2 us -> 11.7 us
  transfers between devices with their start and end apart: 30 -> 30, of which waited for: 11 -> 11; matrix products, arithmetic and copies ran while one was open for 39% -> 38% of each run, Pallas kernels for 0% -> 0%
where the time goes in v5:
time: 188 us; the launch traced here: 187 us
  waiting for transfers between devices  53.9 us (29%)
  starting transfers between devices  52.7 us (28%)
  matrix products  39.7 us (21%)
  local copies, waits for them, and re-layouts  24.3 us (13%)
  other arithmetic  15.2 us (8%)
    ppermute x12, waiting for transfers between devices, far_z(): return (lax.ppermute(low, 'z', z_by(1)), lax.ppermute(high, 'z', z_by(3)))  27.7 us
    dot_general x6, matrix products, local(): jnp.einsum('rd,rf->df', a, b, preferred_element_type=F32)  22.9 us
    ppermute x12, starting transfers between devices, far_z(): return (lax.ppermute(low, 'z', z_by(1)), lax.ppermute(high, 'z', z_by(3)))  18.8 us
    all_to_all x2, waiting for transfers between devices, move_plane(): lax.all_to_all(twice, PLANE, split_axis=0, concat_axis=0, tiled=True)  13.6 us
    unnamed x49, local copies, waits for them, and re-layouts  11.7 us
    all_to_all x2, starting transfers between devices, move_plane(): lax.all_to_all(twice, PLANE, split_axis=0, concat_axis=0, tiled=True)  11 us
    all_to_all x2, starting transfers between devices, to_slots(): back = lax.all_to_all(sent, PLANE, split_axis=0, concat_axis=0, tiled=True)  8.07 us
    ppermute x4, starting transfers between devices, across(): return lax.ppermute(rows, 'xh', SWAP)  7.48 us
  transfers between devices with their start and end apart: 30, of which 11 were waited for; matrix products, arithmetic and copies ran while one was open for 38% of the time, Pallas kernels for 0%

profile of v5, /device:TPU:0, one launch (start us, length us, event | category | flops | bytes accessed | tf_op | source)
XLA Modules:
  0.0 187.1 jit_solution(2087995282288091462)
XLA Ops:
  4.3 7.1 %all-to-all-start = ((bf16[16,4,7168]{2,1,0:T(4,128)(2,1)}), bf16[16,4,7168]{2,1,0:T(4,128)(2,1)S(1)}, u32[]{:S(2)}, u32[]{:S(2)}) async-start(bf16[16,4,7168]{2,1,0:T(4,128)(2,1)} %copy.36), calls=%async_computation | async-start | bytes 1835008 | tf_op jit(solution)/shard_map/all_to_all | solution.py:95
  15.6 11.2 %all-to-all-done = bf16[16,4,7168]{2,1,0:T(4,128)(2,1)S(1)} async-done(((bf16[16,4,7168]{2,1,0:T(4,128)(2,1)}), bf16[16,4,7168]{2,1,0:T(4,128)(2,1)S(1)}, u32[]{:S(2)}, u32[]{:S(2)}) %all-to-all-start) | async-done | bytes 917536 | tf_op jit(solution)/shard_map/all_to_all | solution.py:95
  31.0 2.1 %collective-permute-start.1 = (bf16[48,7168]{1,0:T(8,128)(2,1)}, bf16[48,7168]{1,0:T(8,128)(2,1)S(1)}, u32[]{:S(2)}, u32[]{:S(2)}) collective-permute-start(bf16[48,7168]{1,0:T(8,128)(2,1)} %constant_dynamic-update-slice_fusion), channel_id=1, source_target_pairs={{0,6},{2,0},{4,2},{6,4},{1,7},{3,1},{5,3},{7,5},{8,14},{10,8},{12,... | collective-permute-start | bytes 2064392 | tf_op jit(solution)/shard_map/ppermute | solution.py:27
  33.2 2.2 %broadcast_in_dim.75 = bf16[2,2,4,4,7168]{4,3,2,1,0:T(4,128)(2,1)} broadcast(bf16[2,4,4,7168]{3,2,1,0:T(4,128)(2,1)} %broadcast_in_dim.74), dimensions={0,2,3,4} | broadcast | bytes 1376256 | tf_op jit(solution)/shard_map/broadcast_in_dim | solution.py:90
  35.5 3.9 %all-to-all-start.1 = ((bf16[16,4,7168]{2,1,0:T(4,128)(2,1)}), bf16[16,4,7168]{2,1,0:T(4,128)(2,1)S(1)}, u32[]{:S(2)}, u32[]{:S(2)}) async-start(bf16[16,4,7168]{2,1,0:T(4,128)(2,1)} %bitcast.6), calls=%async_computation.1 | async-start | bytes 1835008 | tf_op jit(solution)/shard_map/all_to_all | solution.py:95
  40.4 6.1 %collective-permute-done = bf16[48,7168]{1,0:T(8,128)(2,1)S(1)} collective-permute-done((bf16[48,7168]{1,0:T(8,128)(2,1)}, bf16[48,7168]{1,0:T(8,128)(2,1)S(1)}, u32[]{:S(2)}, u32[]{:S(2)}) %collective-permute-start) | collective-permute-done | bytes 688160 | tf_op jit(solution)/shard_map/ppermute | solution.py:27
  48.5 2.7 %collective-permute-start.10 = (bf16[24,7168]{1,0:T(8,128)(2,1)}, bf16[24,7168]{1,0:T(8,128)(2,1)}, u32[]{:S(2)}, u32[]{:S(2)}) collective-permute-start(bf16[24,7168]{1,0:T(8,128)(2,1)} %slice.259), channel_id=1, source_target_pairs={{0,6},{2,0},{4,2},{6,4},{1,7},{3,1},{5,3},{7,5},{8,14},{10,8},{12,... | collective-permute-start | bytes 1032200 | tf_op jit(solution)/shard_map/ppermute | solution.py:36
  52.0 2.4 %all-to-all-done.1 = bf16[16,4,7168]{2,1,0:T(4,128)(2,1)S(1)} async-done(((bf16[16,4,7168]{2,1,0:T(4,128)(2,1)}), bf16[16,4,7168]{2,1,0:T(4,128)(2,1)S(1)}, u32[]{:S(2)}, u32[]{:S(2)}) %all-to-all-start.1) | async-done | bytes 917536 | tf_op jit(solution)/shard_map/all_to_all | solution.py:95
  62.9 4.0 %pad_maximum_fusion = bf16[7168,512]{1,0:T(8,128)(2,1)S(1)} fusion(bf16[7168,128]{1,0:T(8,128)(2,1)} %collective-permute-done.7, bf16[7168,128]{1,0:T(8,128)(2,1)} %bitcast.47, bf16[7168,128]{1,0:T(8,128)(2,1)} %collective-permute-done.6, bf16[7168,128]{1,0:T(8,128)(2,1)} %bitcast.49), kind=kLoop, calls=%fused_computation.21 | loop fusion | flops 29360128 | bytes 14680064 | tf_op jit(solution)/shard_map/concatenate | solution.py:141
  72.0 4.5 %collective-permute-done.11 = bf16[16,7168]{1,0:T(8,128)(2,1)S(1)} collective-permute-done((bf16[16,7168]{1,0:T(8,128)(2,1)S(1)}, bf16[16,7168]{1,0:T(8,128)(2,1)S(1)}, u32[]{:S(2)}, u32[]{:S(2)}) %collective-permute-start.11) | collective-permute-done | bytes 229408 | tf_op jit(solution)/shard_map/ppermute | solution.py:40
  80.1 2.2 %collective-permute-start.4 = (bf16[32,7168]{1,0:T(8,128)(2,1)S(1)}, bf16[32,7168]{1,0:T(8,128)(2,1)S(1)}, u32[]{:S(2)}, u32[]{:S(2)}) collective-permute-start(bf16[32,7168]{1,0:T(8,128)(2,1)S(1)} %pad_maximum_fusion.8), channel_id=1, source_target_pairs={{0,8},{8,0},{1,9},{9,1},{2,10},{10,2},{3,11},{11,3},{4,12},{12,4},... | collective-permute-start | bytes 1376264 | tf_op jit(solution)/shard_map/ppermute | solution.py:40
  82.5 3.2 %collective-permute-start.13 = (bf16[24,7168]{1,0:T(8,128)(2,1)S(1)}, bf16[24,7168]{1,0:T(8,128)(2,1)S(1)}, u32[]{:S(2)}, u32[]{:S(2)}) collective-permute-start(bf16[24,7168]{1,0:T(8,128)(2,1)S(1)} %slice.267), channel_id=1, source_target_pairs={{0,6},{2,0},{4,2},{6,4},{1,7},{3,1},{5,3},{7,5},{8,14},{10,8},{12,... | collective-permute-start | bytes 1032200 | tf_op jit(solution)/shard_map/ppermute | solution.py:36
  86.6 4.3 %collective-permute-done.12 = bf16[24,7168]{1,0:T(8,128)(2,1)S(1)} collective-permute-done((bf16[24,7168]{1,0:T(8,128)(2,1)S(1)}, bf16[24,7168]{1,0:T(8,128)(2,1)S(1)}, u32[]{:S(2)}, u32[]{:S(2)}) %collective-permute-start.12) | collective-permute-done | bytes 344096 | tf_op jit(solution)/shard_map/ppermute | solution.py:36
  92.6 3.2 %collective-permute-start.16 = (bf16[64,7168]{1,0:T(8,128)(2,1)S(1)}, bf16[64,7168]{1,0:T(8,128)(2,1)S(1)}, u32[]{:S(2)}, u32[]{:S(2)}) collective-permute-start(bf16[64,7168]{1,0:T(8,128)(2,1)S(1)} %get-tuple-element.76), channel_id=1, source_target_pairs={{0,6},{2,0},{4,2},{6,4},{1,7},{3,1},{5,3},{7,5},{8,14},{10,8},{12,... | collective-permute-start | bytes 2752520 | tf_op jit(solution)/shard_map/ppermute | solution.py:36
  100.9 3.9 %convolution_convert_fusion.2 = bf16[128,7168]{1,0:T(8,128)(2,1)} fusion(bf16[256,7168]{1,0:T(8,128)(2,1)} %slice_dynamic-update-slice_fusion, bf16[256,256]{1,0:T(8,128)(2,1)S(1)} %get-tuple-element.65), kind=kOutput, calls=%fused_computation.12 | convolution fusion | flops 470679552 | bytes 5570560 | tf_op jit(solution)/shard_map/rd,rf->df/dot_general | solution.py:165
  104.8 3.2 %multiply_convert_fusion = (bf16[256,256]{1,0:T(8,128)(2,1)S(1)}, bf16[256,256]{1,0:T(8,128)(2,1)S(1)}) fusion(f32[256,256]{1,0:T(8,128)S(1)} %get-tuple-element.72, f32[256,256]{1,0:T(8,128)S(1)} %get-tuple-element.71, bf16[256,7168]{1,0:T(8,128)(2,1)} %slice_dynamic-update-slice_fusion, bf16[256,7168]{1,0:T(8,128)(2,1)S(1)} %pad_maximum_fusion.1), kind=kOutput, calls=%fused_computation.55 | convolution fusion | flops 940376064 | bytes 8126464 | tf_op jit(solution)/shard_map/rd,fd->rf/dot_general | solution.py:160
  108.0 2.4 %convolution_convert_fusion.4 = bf16[7168,128]{1,0:T(8,128)(2,1)} fusion(bf16[256,7168]{1,0:T(8,128)(2,1)S(1)} %slice_dynamic-update-slice_fusion.1, bf16[256,256]{1,0:T(8,128)(2,1)S(1)} %get-tuple-element.73), kind=kOutput, calls=%fused_computation.14 | convolution fusion | flops 470679552 | bytes 5570560 | tf_op jit(solution)/shard_map/rd,rf->df/dot_general | solution.py:165
  110.4 2.4 %convolution_convert_fusion.3 = bf16[7168,128]{1,0:T(8,128)(2,1)} fusion(bf16[256,7168]{1,0:T(8,128)(2,1)S(1)} %slice_dynamic-update-slice_fusion.1, bf16[256,256]{1,0:T(8,128)(2,1)S(1)} %get-tuple-element.74), kind=kOutput, calls=%fused_computation.13 | convolution fusion | flops 470679552 | bytes 5570560 | tf_op jit(solution)/shard_map/rd,rf->df/dot_general | solution.py:165
  112.8 2.1 %convolution_convert_fusion = bf16[256,7168]{1,0:T(8,128)(2,1)S(1)} fusion(bf16[7168,512]{1,0:T(8,128)(2,1)S(1)} %pad_maximum_fusion, bf16[256,256]{1,0:T(8,128)(2,1)S(1)} %get-tuple-element.74, bf16[256,256]{1,0:T(8,128)(2,1)S(1)} %get-tuple-element.73), kind=kOutput, calls=%fused_computation | convolution fusion | flops 1881407488 | bytes 11272192 | tf_op jit(solution)/shard_map/rf,df->rd/dot_general | solution.py:173
  115.2 3.3 %collective-permute-start.19 = (bf16[32,7168]{1,0:T(8,128)(2,1)S(1)}, bf16[32,7168]{1,0:T(8,128)(2,1)S(1)}, u32[]{:S(2)}, u32[]{:S(2)}) collective-permute-start(bf16[32,7168]{1,0:T(8,128)(2,1)S(1)} %get-tuple-element.82), channel_id=1, source_target_pairs={{0,2},{2,4},{4,6},{6,0},{1,3},{3,5},{5,7},{7,1},{8,10},{10,12},{12... | collective-permute-start | bytes 1376264 | tf_op jit(solution)/shard_map/ppermute | solution.py:36
  122.4 3.3 %collective-permute-done.19 = bf16[32,7168]{1,0:T(8,128)(2,1)S(1)} collective-permute-done((bf16[32,7168]{1,0:T(8,128)(2,1)S(1)}, bf16[32,7168]{1,0:T(8,128)(2,1)S(1)}, u32[]{:S(2)}, u32[]{:S(2)}) %collective-permute-start.19) | collective-permute-done | bytes 458784 | tf_op jit(solution)/shard_map/ppermute | solution.py:36
  125.7 4.5 %collective-permute-done.20 = bf16[32,7168]{1,0:T(8,128)(2,1)S(1)} collective-permute-done((bf16[32,7168]{1,0:T(8,128)(2,1)S(1)}, bf16[32,7168]{1,0:T(8,128)(2,1)S(1)}, u32[]{:S(2)}, u32[]{:S(2)}) %collective-permute-start.20) | collective-permute-done | bytes 458784 | tf_op jit(solution)/shard_map/ppermute | solution.py:36
  132.1 3.6 %all-to-all-start.2 = ((bf16[16,4,7168]{2,1,0:T(4,128)(2,1)}), bf16[16,4,7168]{2,1,0:T(4,128)(2,1)S(1)}, u32[]{:S(2)}, u32[]{:S(2)}) async-start(bf16[16,4,7168]{2,1,0:T(4,128)(2,1)} %reshape.123), calls=%async_computation.2 | async-start | bytes 1835008 | tf_op jit(solution)/shard_map/all_to_all | solution.py:102
  135.8 11.0 %collective-permute-done.18 = bf16[64,7168]{1,0:T(8,128)(2,1)} collective-permute-done((bf16[64,7168]{1,0:T(8,128)(2,1)}, bf16[64,7168]{1,0:T(8,128)(2,1)}, u32[]{:S(2)}, u32[]{:S(2)}) %collective-permute-start.18) | collective-permute-done | bytes 917536 | tf_op jit(solution)/shard_map/ppermute | solution.py:36
  146.7 2.6 %add_convert_fusion.4 = (bf16[32,7168]{1,0:T(8,128)(2,1)}, bf16[32,7168]{1,0:T(8,128)(2,1)}) fusion(bf16[64,7168]{1,0:T(8,128)(2,1)} %collective-permute-done.18, bf16[256,7168]{1,0:T(8,128)(2,1)} %copy-done.4, bf16[64,7168]{1,0:T(8,128)(2,1)} %collective-permute-done.17), kind=kLoop, calls=%fused_computation.33 | loop fusion | flops 1835008 | bytes 2752512 | tf_op jit(solution)/shard_map/convert_element_type | solution.py:23
  153.2 4.4 %fusion.7 = bf16[1,7168,128]{2,1,0:T(8,128)(2,1)} fusion(bf16[256,7168]{1,0:T(8,128)(2,1)} %copy-done.3, bf16[7168,128]{1,0:T(8,128)(2,1)S(1)} %collective-permute-done.23, bf16[256,256]{1,0:T(8,128)(2,1)S(1)} %get-tuple-element.73), kind=kOutput, calls=%fused_computation.17 | convolution fusion | flops 472514560 | bytes 7405568 | tf_op jit(solution)/shard_map/rd,rf->df/dot_general | solution.py:165
  157.6 4.6 %collective-permute-done.21 = bf16[32,7168]{1,0:T(8,128)(2,1)S(1)} collective-permute-done((bf16[32,7168]{1,0:T(8,128)(2,1)}, bf16[32,7168]{1,0:T(8,128)(2,1)S(1)}, u32[]{:S(2)}, u32[]{:S(2)}) %collective-permute-start.21) | collective-permute-done | bytes 458784 | tf_op jit(solution)/shard_map/ppermute | solution.py:36
  165.5 4.4 %all-to-all-start.3 = ((bf16[16,4,7168]{2,1,0:T(4,128)(2,1)}), bf16[16,4,7168]{2,1,0:T(4,128)(2,1)}, u32[]{:S(2)}, u32[]{:S(2)}) async-start(bf16[16,4,7168]{2,1,0:T(4,128)(2,1)} %reshape.124), calls=%async_computation.3 | async-start | bytes 1835008 | tf_op jit(solution)/shard_map/all_to_all | solution.py:102
  170.0 5.0 %fusion.6 = bf16[1,7168,128]{2,1,0:T(8,128)(2,1)} fusion(bf16[256,7168]{1,0:T(8,128)(2,1)} %copy-done.3, bf16[7168,128]{1,0:T(8,128)(2,1)} %collective-permute-done.24, bf16[256,256]{1,0:T(8,128)(2,1)S(1)} %get-tuple-element.74), kind=kOutput, calls=%fused_computation.16 | convolution fusion | flops 472514560 | bytes 7405568 | tf_op jit(solution)/shard_map/rd,rf->df/dot_general | solution.py:165
  175.0 4.7 %fusion.5 = bf16[1,128,7168]{2,1,0:T(8,128)(2,1)} fusion(bf16[256,7168]{1,0:T(8,128)(2,1)} %slice_dynamic-update-slice_fusion, bf16[128,7168]{1,0:T(8,128)(2,1)} %collective-permute-done.25, bf16[256,256]{1,0:T(8,128)(2,1)S(1)} %get-tuple-element.65), kind=kOutput, calls=%fused_computation.15 | convolution fusion | flops 472514560 | bytes 7405568 | tf_op jit(solution)/shard_map/rd,rf->df/dot_general | solution.py:165
  179.7 2.9 %fusion = bf16[128,7168]{1,0:T(8,128)(2,1)} fusion(f32[128,16,4]{0,1,2:T(8,128)S(1)} %bitcast.54, bf16[16,4,7168]{2,1,0:T(4,128)(2,1)S(1)} %all-to-all-done.2), kind=kOutput, calls=%fused_computation.7 | convolution fusion | flops 705560576 | bytes 2785280 | tf_op jit(solution)/shard_map/tgc,gcd->td/dot_general | solution.py:192
  184.1 3.1 %fusion.1 = bf16[128,7168]{1,0:T(8,128)(2,1)} fusion(bf16[128,16,4]{0,1,2:T(8,128)(2,1)S(1)} %bitcast.53, bf16[16,4,7168]{2,1,0:T(4,128)(2,1)} %all-to-all-done.3), kind=kOutput, calls=%fused_computation.8 | convolution fusion | flops 118358016 | bytes 2768896 | tf_op jit(solution)/shard_map/tgc,gcd->td/dot_general | solution.py:195
  (151 shorter events, 55.2 us)
Async XLA Ops:
  4.3 22.5 %all-to-all-start = ((bf16[16,4,7168]{2,1,0:T(4,128)(2,1)}), bf16[16,4,7168]{2,1,0:T(4,128)(2,1)S(1)}, u32[]{:S(2)}, u32[]{:S(2)}) async-start(bf16[16,4,7168]{2,1,0:T(4,128)(2,1)} %copy.36), calls=%async_computation | async-start | bytes 1835008 | tf_op jit(solution)/shard_map/all_to_all | solution.py:95
  11.5 47.9 %collective-permute-start.6 = (bf16[7168,128]{1,0:T(8,128)(2,1)}, bf16[7168,128]{1,0:T(8,128)(2,1)}, u32[]{:S(2)}, u32[]{:S(2)}) collective-permute-start(bf16[7168,128]{1,0:T(8,128)(2,1)} %bitcast.48), channel_id=1, source_target_pairs={{0,1},{1,0},{2,3},{3,2},{4,5},{5,4},{6,7},{7,6},{8,9},{9,8},{10,11... | collective-permute-start | bytes 5505032 | tf_op jit(solution)/shard_map/ppermute | solution.py:123
  11.6 49.3 %collective-permute-start.7 = (bf16[7168,128]{1,0:T(8,128)(2,1)}, bf16[7168,128]{1,0:T(8,128)(2,1)}, u32[]{:S(2)}, u32[]{:S(2)}) collective-permute-start(bf16[7168,128]{1,0:T(8,128)(2,1)} %bitcast.46), channel_id=1, source_target_pairs={{0,1},{1,0},{2,3},{3,2},{4,5},{5,4},{6,7},{7,6},{8,9},{9,8},{10,11... | collective-permute-start | bytes 5505032 | tf_op jit(solution)/shard_map/ppermute | solution.py:124
  12.0 50.6 %collective-permute-start.8 = (bf16[128,7168]{1,0:T(8,128)(2,1)}, bf16[128,7168]{1,0:T(8,128)(2,1)}, u32[]{:S(2)}, u32[]{:S(2)}) collective-permute-start(bf16[128,7168]{1,0:T(8,128)(2,1)} %bitcast.50), channel_id=1, source_target_pairs={{0,1},{1,0},{2,3},{3,2},{4,5},{5,4},{6,7},{7,6},{8,9},{9,8},{10,11... | collective-permute-start | bytes 5505032 | tf_op jit(solution)/shard_map/ppermute | solution.py:125
  29.0 17.4 %collective-permute-start = (bf16[48,7168]{1,0:T(8,128)(2,1)}, bf16[48,7168]{1,0:T(8,128)(2,1)S(1)}, u32[]{:S(2)}, u32[]{:S(2)}) collective-permute-start(bf16[48,7168]{1,0:T(8,128)(2,1)} %constant_dynamic-update-slice_fusion), channel_id=1, source_target_pairs={{0,2},{2,4},{4,6},{6,0},{1,3},{3,5},{5,7},{7,1},{8,10},{10,12},{12... | collective-permute-start | bytes 2064392 | tf_op jit(solution)/shard_map/ppermute | solution.py:27
  31.0 16.2 %collective-permute-start.1 = (bf16[48,7168]{1,0:T(8,128)(2,1)}, bf16[48,7168]{1,0:T(8,128)(2,1)S(1)}, u32[]{:S(2)}, u32[]{:S(2)}) collective-permute-start(bf16[48,7168]{1,0:T(8,128)(2,1)} %constant_dynamic-update-slice_fusion), channel_id=1, source_target_pairs={{0,6},{2,0},{4,2},{6,4},{1,7},{3,1},{5,3},{7,5},{8,14},{10,8},{12,... | collective-permute-start | bytes 2064392 | tf_op jit(solution)/shard_map/ppermute | solution.py:27
  35.5 19.0 %all-to-all-start.1 = ((bf16[16,4,7168]{2,1,0:T(4,128)(2,1)}), bf16[16,4,7168]{2,1,0:T(4,128)(2,1)S(1)}, u32[]{:S(2)}, u32[]{:S(2)}) async-start(bf16[16,4,7168]{2,1,0:T(4,128)(2,1)} %bitcast.6), calls=%async_computation.1 | async-start | bytes 1835008 | tf_op jit(solution)/shard_map/all_to_all | solution.py:95
  48.0 14.9 %collective-permute-start.9 = (bf16[24,7168]{1,0:T(8,128)(2,1)}, bf16[24,7168]{1,0:T(8,128)(2,1)S(1)}, u32[]{:S(2)}, u32[]{:S(2)}) collective-permute-start(bf16[24,7168]{1,0:T(8,128)(2,1)} %slice.258), channel_id=1, source_target_pairs={{0,2},{2,4},{4,6},{6,0},{1,3},{3,5},{5,7},{7,1},{8,10},{10,12},{12... | collective-permute-start | bytes 1032200 | tf_op jit(solution)/shard_map/ppermute | solution.py:36
  48.5 14.4 %collective-permute-start.10 = (bf16[24,7168]{1,0:T(8,128)(2,1)}, bf16[24,7168]{1,0:T(8,128)(2,1)}, u32[]{:S(2)}, u32[]{:S(2)}) collective-permute-start(bf16[24,7168]{1,0:T(8,128)(2,1)} %slice.259), channel_id=1, source_target_pairs={{0,6},{2,0},{4,2},{6,4},{1,7},{3,1},{5,3},{7,5},{8,14},{10,8},{12,... | collective-permute-start | bytes 1032200 | tf_op jit(solution)/shard_map/ppermute | solution.py:36
  59.3 11.6 %collective-permute-start.5 = (bf16[32,7168]{1,0:T(8,128)(2,1)}, bf16[32,7168]{1,0:T(8,128)(2,1)S(1)}, u32[]{:S(2)}, u32[]{:S(2)}) collective-permute-start(bf16[32,7168]{1,0:T(8,128)(2,1)} %pad_maximum_fusion.9), channel_id=1, source_target_pairs={{0,8},{8,0},{1,9},{9,1},{2,10},{10,2},{3,11},{11,3},{4,12},{12,4},... | collective-permute-start | bytes 1376264 | tf_op jit(solution)/shard_map/ppermute | solution.py:40
  60.9 19.1 %collective-permute-start.2 = (bf16[48,7168]{1,0:T(8,128)(2,1)}, bf16[48,7168]{1,0:T(8,128)(2,1)S(1)}, u32[]{:S(2)}, u32[]{:S(2)}) collective-permute-start(bf16[48,7168]{1,0:T(8,128)(2,1)} %pad_maximum_fusion.5), channel_id=1, source_target_pairs={{0,6},{2,0},{4,2},{6,4},{1,7},{3,1},{5,3},{7,5},{8,14},{10,8},{12,... | collective-permute-start | bytes 2064392 | tf_op jit(solution)/shard_map/ppermute | solution.py:27
  62.6 17.4 %collective-permute-start.3 = (bf16[48,7168]{1,0:T(8,128)(2,1)}, bf16[48,7168]{1,0:T(8,128)(2,1)S(1)}, u32[]{:S(2)}, u32[]{:S(2)}) collective-permute-start(bf16[48,7168]{1,0:T(8,128)(2,1)} %pad_maximum_fusion.5), channel_id=1, source_target_pairs={{0,2},{2,4},{4,6},{6,0},{1,3},{3,5},{5,7},{7,1},{8,10},{10,12},{12... | collective-permute-start | bytes 2064392 | tf_op jit(solution)/shard_map/ppermute | solution.py:27
  68.8 7.6 %collective-permute-start.11 = (bf16[16,7168]{1,0:T(8,128)(2,1)S(1)}, bf16[16,7168]{1,0:T(8,128)(2,1)S(1)}, u32[]{:S(2)}, u32[]{:S(2)}) collective-permute-start(bf16[16,7168]{1,0:T(8,128)(2,1)S(1)} %slice.260), channel_id=1, source_target_pairs={{0,8},{8,0},{1,9},{9,1},{2,10},{10,2},{3,11},{11,3},{4,12},{12,4},... | collective-permute-start | bytes 688136 | tf_op jit(solution)/shard_map/ppermute | solution.py:40
  76.5 33.9 %copy-start.3 = (bf16[256,7168]{1,0:T(8,128)(2,1)}, bf16[256,7168]{1,0:T(8,128)(2,1)S(1)}, u32[]{:S(2)}) copy-start(bf16[256,7168]{1,0:T(8,128)(2,1)S(1)} %slice_dynamic-update-slice_fusion.1) | copy-start | bytes 11010052
  80.1 15.7 %collective-permute-start.4 = (bf16[32,7168]{1,0:T(8,128)(2,1)S(1)}, bf16[32,7168]{1,0:T(8,128)(2,1)S(1)}, u32[]{:S(2)}, u32[]{:S(2)}) collective-permute-start(bf16[32,7168]{1,0:T(8,128)(2,1)S(1)} %pad_maximum_fusion.8), channel_id=1, source_target_pairs={{0,8},{8,0},{1,9},{9,1},{2,10},{10,2},{3,11},{11,3},{4,12},{12,4},... | collective-permute-start | bytes 1376264 | tf_op jit(solution)/shard_map/ppermute | solution.py:40
  82.4 8.5 %collective-permute-start.12 = (bf16[24,7168]{1,0:T(8,128)(2,1)S(1)}, bf16[24,7168]{1,0:T(8,128)(2,1)S(1)}, u32[]{:S(2)}, u32[]{:S(2)}) collective-permute-start(bf16[24,7168]{1,0:T(8,128)(2,1)S(1)} %slice.266), channel_id=1, source_target_pairs={{0,2},{2,4},{4,6},{6,0},{1,3},{3,5},{5,7},{7,1},{8,10},{10,12},{12... | collective-permute-start | bytes 1032200 | tf_op jit(solution)/shard_map/ppermute | solution.py:36
  82.5 8.4 %collective-permute-start.13 = (bf16[24,7168]{1,0:T(8,128)(2,1)S(1)}, bf16[24,7168]{1,0:T(8,128)(2,1)S(1)}, u32[]{:S(2)}, u32[]{:S(2)}) collective-permute-start(bf16[24,7168]{1,0:T(8,128)(2,1)S(1)} %slice.267), channel_id=1, source_target_pairs={{0,6},{2,0},{4,2},{6,4},{1,7},{3,1},{5,3},{7,5},{8,14},{10,8},{12,... | collective-permute-start | bytes 1032200 | tf_op jit(solution)/shard_map/ppermute | solution.py:36
  90.9 7.6 %collective-permute-start.14 = (bf16[16,7168]{1,0:T(8,128)(2,1)S(1)}, bf16[16,7168]{1,0:T(8,128)(2,1)S(1)}, u32[]{:S(2)}, u32[]{:S(2)}) collective-permute-start(bf16[16,7168]{1,0:T(8,128)(2,1)S(1)} %slice.268), channel_id=1, source_target_pairs={{0,8},{8,0},{1,9},{9,1},{2,10},{10,2},{3,11},{11,3},{4,12},{12,4},... | collective-permute-start | bytes 688136 | tf_op jit(solution)/shard_map/ppermute | solution.py:40
  92.6 22.4 %collective-permute-start.16 = (bf16[64,7168]{1,0:T(8,128)(2,1)S(1)}, bf16[64,7168]{1,0:T(8,128)(2,1)S(1)}, u32[]{:S(2)}, u32[]{:S(2)}) collective-permute-start(bf16[64,7168]{1,0:T(8,128)(2,1)S(1)} %get-tuple-element.76), channel_id=1, source_target_pairs={{0,6},{2,0},{4,2},{6,4},{1,7},{3,1},{5,3},{7,5},{8,14},{10,8},{12,... | collective-permute-start | bytes 2752520 | tf_op jit(solution)/shard_map/ppermute | solution.py:36
  95.8 19.2 %collective-permute-start.15 = (bf16[64,7168]{1,0:T(8,128)(2,1)S(1)}, bf16[64,7168]{1,0:T(8,128)(2,1)S(1)}, u32[]{:S(2)}, u32[]{:S(2)}) collective-permute-start(bf16[64,7168]{1,0:T(8,128)(2,1)S(1)} %get-tuple-element.75), channel_id=1, source_target_pairs={{0,2},{2,4},{4,6},{6,0},{1,3},{3,5},{5,7},{7,1},{8,10},{10,12},{12... | collective-permute-start | bytes 2752520 | tf_op jit(solution)/shard_map/ppermute | solution.py:36
  115.2 10.5 %collective-permute-start.19 = (bf16[32,7168]{1,0:T(8,128)(2,1)S(1)}, bf16[32,7168]{1,0:T(8,128)(2,1)S(1)}, u32[]{:S(2)}, u32[]{:S(2)}) collective-permute-start(bf16[32,7168]{1,0:T(8,128)(2,1)S(1)} %get-tuple-element.82), channel_id=1, source_target_pairs={{0,2},{2,4},{4,6},{6,0},{1,3},{3,5},{5,7},{7,1},{8,10},{10,12},{12... | collective-permute-start | bytes 1376264 | tf_op jit(solution)/shard_map/ppermute | solution.py:36
  118.5 11.7 %collective-permute-start.20 = (bf16[32,7168]{1,0:T(8,128)(2,1)S(1)}, bf16[32,7168]{1,0:T(8,128)(2,1)S(1)}, u32[]{:S(2)}, u32[]{:S(2)}) collective-permute-start(bf16[32,7168]{1,0:T(8,128)(2,1)S(1)} %get-tuple-element.84), channel_id=1, source_target_pairs={{0,6},{2,0},{4,2},{6,4},{1,7},{3,1},{5,3},{7,5},{8,14},{10,8},{12,... | collective-permute-start | bytes 1376264 | tf_op jit(solution)/shard_map/ppermute | solution.py:36
  120.3 32.8 %collective-permute-start.23 = (bf16[7168,128]{1,0:T(8,128)(2,1)}, bf16[7168,128]{1,0:T(8,128)(2,1)S(1)}, u32[]{:S(2)}, u32[]{:S(2)}) collective-permute-start(bf16[7168,128]{1,0:T(8,128)(2,1)} %convolution_convert_fusion.4), channel_id=1, source_target_pairs={{0,1},{1,0},{2,3},{3,2},{4,5},{5,4},{6,7},{7,6},{8,9},{9,8},{10,11... | collective-permute-start | bytes 5505032 | tf_op jit(solution)/shard_map/ppermute | solution.py:184
  120.3 26.4 %collective-permute-start.18 = (bf16[64,7168]{1,0:T(8,128)(2,1)}, bf16[64,7168]{1,0:T(8,128)(2,1)}, u32[]{:S(2)}, u32[]{:S(2)}) collective-permute-start(bf16[64,7168]{1,0:T(8,128)(2,1)} %get-tuple-element.80), channel_id=1, source_target_pairs={{0,6},{2,0},{4,2},{6,4},{1,7},{3,1},{5,3},{7,5},{8,14},{10,8},{12,... | collective-permute-start | bytes 2752520 | tf_op jit(solution)/shard_map/ppermute | solution.py:36
  122.4 24.4 %collective-permute-start.17 = (bf16[64,7168]{1,0:T(8,128)(2,1)}, bf16[64,7168]{1,0:T(8,128)(2,1)}, u32[]{:S(2)}, u32[]{:S(2)}) collective-permute-start(bf16[64,7168]{1,0:T(8,128)(2,1)} %get-tuple-element.79), channel_id=1, source_target_pairs={{0,2},{2,4},{4,6},{6,0},{1,3},{3,5},{5,7},{7,1},{8,10},{10,12},{12... | collective-permute-start | bytes 2752520 | tf_op jit(solution)/shard_map/ppermute | solution.py:36
  130.8 21.7 %copy-start.9 = (f32[128,8]{0,1:T(8,128)S(1)}, f32[128,8]{0,1:T(8,128)}, u32[]{:S(2)}) copy-start(f32[128,8]{0,1:T(8,128)} %copy-done.8) | copy-start | bytes 12292
  132.1 17.2 %all-to-all-start.2 = ((bf16[16,4,7168]{2,1,0:T(4,128)(2,1)}), bf16[16,4,7168]{2,1,0:T(4,128)(2,1)S(1)}, u32[]{:S(2)}, u32[]{:S(2)}) async-start(bf16[16,4,7168]{2,1,0:T(4,128)(2,1)} %reshape.123), calls=%async_computation.2 | async-start | bytes 1835008 | tf_op jit(solution)/shard_map/all_to_all | solution.py:102
  149.3 12.9 %collective-permute-start.21 = (bf16[32,7168]{1,0:T(8,128)(2,1)}, bf16[32,7168]{1,0:T(8,128)(2,1)S(1)}, u32[]{:S(2)}, u32[]{:S(2)}) collective-permute-start(bf16[32,7168]{1,0:T(8,128)(2,1)} %get-tuple-element.87), channel_id=1, source_target_pairs={{0,2},{2,4},{4,6},{6,0},{1,3},{3,5},{5,7},{7,1},{8,10},{10,12},{12... | collective-permute-start | bytes 1376264 | tf_op jit(solution)/shard_map/ppermute | solution.py:36
  151.1 11.1 %collective-permute-start.22 = (bf16[32,7168]{1,0:T(8,128)(2,1)}, bf16[32,7168]{1,0:T(8,128)(2,1)S(1)}, u32[]{:S(2)}, u32[]{:S(2)}) collective-permute-start(bf16[32,7168]{1,0:T(8,128)(2,1)} %get-tuple-element.89), channel_id=1, source_target_pairs={{0,6},{2,0},{4,2},{6,4},{1,7},{3,1},{5,3},{7,5},{8,14},{10,8},{12,... | collective-permute-start | bytes 1376264 | tf_op jit(solution)/shard_map/ppermute | solution.py:36
  152.6 17.4 %collective-permute-start.24 = (bf16[7168,128]{1,0:T(8,128)(2,1)}, bf16[7168,128]{1,0:T(8,128)(2,1)}, u32[]{:S(2)}, u32[]{:S(2)}) collective-permute-start(bf16[7168,128]{1,0:T(8,128)(2,1)} %convolution_convert_fusion.3), channel_id=1, source_target_pairs={{0,1},{1,0},{2,3},{3,2},{4,5},{5,4},{6,7},{7,6},{8,9},{9,8},{10,11... | collective-permute-start | bytes 5505032 | tf_op jit(solution)/shard_map/ppermute | solution.py:185
  152.7 22.3 %collective-permute-start.25 = (bf16[128,7168]{1,0:T(8,128)(2,1)}, bf16[128,7168]{1,0:T(8,128)(2,1)}, u32[]{:S(2)}, u32[]{:S(2)}) collective-permute-start(bf16[128,7168]{1,0:T(8,128)(2,1)} %convolution_convert_fusion.2), channel_id=1, source_target_pairs={{0,1},{1,0},{2,3},{3,2},{4,5},{5,4},{6,7},{7,6},{8,9},{9,8},{10,11... | collective-permute-start | bytes 5505032 | tf_op jit(solution)/shard_map/ppermute | solution.py:186
  165.5 18.5 %all-to-all-start.3 = ((bf16[16,4,7168]{2,1,0:T(4,128)(2,1)}), bf16[16,4,7168]{2,1,0:T(4,128)(2,1)}, u32[]{:S(2)}, u32[]{:S(2)}) async-start(bf16[16,4,7168]{2,1,0:T(4,128)(2,1)} %reshape.124), calls=%async_computation.3 | async-start | bytes 1835008 | tf_op jit(solution)/shard_map/all_to_all | solution.py:102
  (14 other events, 143.8 us)
